TPU v7x, 768 devices: a whole 4x8x12 slice. The times are simulated.
768 devices in a mesh: dp: 48 (over z, x), fsdp: 16 (over y, core).
Axes of the slice: x: 4, y: 8, z: 12, core: 2. Of those that a mesh axis runs over, the one named last changes fastest.
Arguments:
- frames: bfloat16 [48, 16, 576, 1024], P('dp', 'fsdp'), may hold values from -6 to 6
- route: int32 [48, 16, 576], P('dp', 'fsdp'), may hold values from 0 to 575, each once within a row
- valid: int32 [48, 16, 576], P('dp', 'fsdp'), may hold values 0 or 1
- w_pw: bfloat16 [1024, 2048], P('fsdp'), may hold values from -0.1875 to 0.1875
- cotangent: bfloat16 [48, 16, 576, 1024], P('dp', 'fsdp'), may hold values from -6 to 6
Outputs:
- gated: bfloat16 [48, 16, 576, 1024], P('dp', 'fsdp')
- grad_pw: bfloat16 [48, 1024, 2048], P('dp', 'fsdp')
Inputs may be any that keep to these rules, and one draw needn't show every extreme that they name: Each row of route is a permutation of the frames of one device.
All inputs are finite; a program needn't handle non-finite values. No bound on the sum of `valid` on one device may be relied on, other than what follows from the above.
Results may differ from a plain program's by a relative error of at most 0.017.
Values may be sent and summed in bfloat16 or wider, within the bound.
No kernel may reach another device: no remote copies, remote signals or barrier semaphores. Data moves between devices by JAX's collectives and lax.ppermute only.
A program may use at most 32 MiB of HBM per device.

v0:
```python
import jax
import jax.numpy as jnp
from jax import lax
from jax.sharding import PartitionSpec as P


def per_device(frames, route, valid, w_pw, cotangent):
    width = frames.shape[3]
    local = frames[0, 0]
    order = route[0, 0]
    picked = jnp.take(local, order, axis=0)
    keep = jnp.take(valid[0, 0], order, axis=0)
    sent = jnp.where(keep[:, None] > 0, picked, jnp.zeros_like(picked))
    received = lax.all_to_all(sent, "dp", split_axis=0, concat_axis=0, tiled=True)
    values = received.astype(jnp.float32)
    mean = jnp.mean(values, axis=-1, keepdims=True)
    centred = values - mean
    variance = jnp.mean(centred * centred, axis=-1, keepdims=True)
    normed = (centred * lax.rsqrt(variance + 1e-05)).astype(jnp.bfloat16)
    columns = normed
    pre = jnp.dot(
        columns,
        lax.all_gather(w_pw, "fsdp", axis=0, tiled=True),
        preferred_element_type=jnp.float32,
    )
    first = pre[:, :width]
    second = jax.nn.sigmoid(pre[:, width:])
    gated = (first * second).astype(jnp.bfloat16)
    upstream = cotangent[0, 0].astype(jnp.float32)
    dpre = jnp.concatenate(
        [upstream * second, upstream * first * second * (1.0 - second)], axis=1
    ).astype(jnp.bfloat16)
    columns = normed
    grad_share = lax.psum_scatter(
        lax.dot_general(
            columns, dpre, (((0,), (0,)), ((), ())), preferred_element_type=jnp.float32
        ).astype(jnp.bfloat16),
        "fsdp",
        scatter_dimension=0,
        tiled=True,
    )
    return (gated[None, None], grad_share[None])


def solution(mesh):
    in_specs = (
        P("dp", "fsdp", None, None),
        P("dp", "fsdp", None),
        P("dp", "fsdp", None),
        P("fsdp", None),
        P("dp", "fsdp", None, None),
    )
    out_specs = (P("dp", "fsdp", None, None), P("dp", "fsdp", None))
    return jax.shard_map(
        per_device, mesh=mesh, in_specs=in_specs, out_specs=out_specs, check_vma=False
    )
```

profile of v0, /device:TPU:25, one launch (start us, length us, event | category | flops | bytes accessed | tf_op | source)
XLA Modules:
  0.0 182.0 jit_solution(5968335324256304832)
XLA Ops:
  7.2 0.0 copy-start
  7.2 0.0 all-gather.2.cloned.1.call-start
  7.2 0.7 all-gather.2.cloned.1.call-update
  7.9 0.0 reduce-scatter.2.cloned.1.call-start
  8.0 0.7 reduce.3
  8.7 0.7 reduce.2
  9.4 0.1 squeeze.12
  9.5 0.7 fusion.11
  10.2 2.6 %gather_fusion = s32[576]{0:T(1024)S(1)} fusion(s32[576]{0:T(1024)S(1)} %reduce.3, s32[1024]{0:T(1024)S(1)} %pad_clamp_fusion), kind=kCustom, calls=%fused_computation | custom fusion | bytes 6912 | tf_op jit(solution)/shard_map/jit(_take)/gather | solution.py:12
  12.8 0.1 gather.13
  12.9 0.0 copy-done
  12.9 3.4 %gather_fusion.1 = bf16[576,1024]{1,0:T(8,128)(2,1)} fusion(bf16[576,1024]{1,0:T(8,128)(2,1)S(1)} %bitcast.11, s32[1024]{0:T(1024)S(1)} %pad_clamp_fusion), kind=kCustom, calls=%fused_computation.1 | custom fusion | bytes 2361600 | tf_op jit(solution)/shard_map/jit(_take)/gather | solution.py:11
  16.3 2.1 %gather.15 = bf16[48,12,1024]{2,1,0:T(8,128)(2,1)S(1)} reshape(bf16[576,1024]{1,0:T(8,128)(2,1)} %gather_fusion.1) | data formatting | bytes 2359296 | tf_op jit(solution)/shard_map/jit(_take)/gather | solution.py:11
  18.5 0.3 select_select_fusion
  18.8 73.8 %all_to_all.6 = bf16[48,12,1024]{2,1,0:T(8,128)(2,1)S(1)} all-to-all(bf16[48,12,1024]{2,1,0:T(8,128)(2,1)S(1)} %select_select_fusion), channel_id=1, replica_groups=mesh['dp'=48,'fsdp'=16] {'dp'}, dimensions={0} | all-to-all | bytes 2359296 | tf_op jit(solution)/shard_map/all_to_all | solution.py:14
  92.6 0.3 convert_reduce_fusion
  92.9 0.1 div.12
  93.0 0.6 multiply_reduce_fusion
  93.7 0.1 rsqrt.12
  93.8 1.6 reshape.103
  95.3 0.0 copy-start.2
  95.3 0.0 all-gather.2.cloned.1.call-done
  95.3 5.3 %fusion.13 = f32[576,2048]{1,0:T(8,128)S(1)} fusion(bf16[1024,2048]{1,0:T(8,128)(2,1)} %all-gather.2.cloned.1.call-done, f32[576,1024]{1,0:T(8,128)} %reshape.103, f32[576]{0:T(1024)S(1)} %rsqrt.12, f32[576]{0:T(1024)S(1)} %div.12), kind=kOutput, calls=%fused_computation.31 | convolution fusion | flops 2417688576 | bytes 11276800 | tf_op jit(solution)/shard_map/dot_general | solution.py:21
  100.6 0.0 copy-done.2
  100.7 0.0 copy-start.1
  100.7 2.4 %fusion = (bf16[576,1024]{1,0:T(8,128)(2,1)S(1)}, bf16[576,1024]{1,0:T(8,128)(2,1)S(1)}, bf16[1,1,576,1024]{3,2,1,0:T(8,128)(2,1)}) fusion(bf16[1,1,576,1024]{3,2,1,0:T(8,128)(2,1)S(1)} %copy-done.2, f32[576,2048]{1,0:T(8,128)S(1)} %fusion.13), kind=kLoop, calls=%fused_computation.6 | loop fusion | flops 7667712 | bytes 9437184 | tf_op jit(solution)/shard_map/convert.2
  103.1 0.0 copy-done.1
  103.1 5.7 %convolution_convert_fusion = bf16[1024,2048]{1,0:T(8,128)(2,1)} fusion(bf16[576,1024]{1,0:T(8,128)(2,1)S(1)} %get-tuple-element.5, bf16[576,1024]{1,0:T(8,128)(2,1)S(1)} %get-tuple-element.4, f32[576,1024]{1,0:T(8,128)S(1)} %copy-done.1, f32[576]{0:T(1024)S(1)} %rsqrt.12, f32[576]{0:T(1024)S(1)} %div.12), kind=kOutput, calls=%fused_computation.2 | convolution fusion | flops 2424504320 | bytes 8917504 | tf_op jit(solution)/shard_map/dot_general | solution.py:35
  108.7 0.0 reduce-scatter.2.cloned.1.call-update
  108.7 66.4 %reduce-scatter.2.cloned.1.call-done = bf16[64,2048]{1,0:T(8,128)(2,1)} async-done(((bf16[1024,2048]{1,0:T(8,128)(2,1)}), bf16[64,2048]{1,0:T(8,128)(2,1)}) %reduce-scatter.2.cloned.1.call-update) | async-done | bytes 262160 | tf_op jit(solution)/shard_map/reduce_scatter | solution.py:34
  (4 shorter events, 0.1 us)
Async XLA Ops:
  7.2 5.7 %copy-start = (bf16[1,1,576,1024]{3,2,1,0:T(8,128)(2,1)S(1)}, bf16[1,1,576,1024]{3,2,1,0:T(8,128)(2,1)}, u32[]{:S(2)}) copy-start(bf16[1,1,576,1024]{3,2,1,0:T(8,128)(2,1)} %param.5) | copy-start | bytes 3538948
  7.2 88.2 %all-gather.2.cloned.1.call-start = ((), (), s32[]{:S(2)}) async-start(), calls=%async_computation.2 | async-start | bytes 4456448 | tf_op jit(solution)/shard_map/all_gather | solution.py:23
  7.9 167.3 %reduce-scatter.2.cloned.1.call-start = ((), (), s32[]{:S(2)}) async-start(), calls=%async_computation.3 | async-start | bytes 4456448 | tf_op jit(solution)/shard_map/reduce_scatter | solution.py:34
  95.3 5.3 %copy-start.2 = (bf16[1,1,576,1024]{3,2,1,0:T(8,128)(2,1)S(1)}, bf16[1,1,576,1024]{3,2,1,0:T(8,128)(2,1)}, u32[]{:S(2)}) copy-start(bf16[1,1,576,1024]{3,2,1,0:T(8,128)(2,1)} %param.9) | copy-start | bytes 3538948
  100.7 2.4 %copy-start.1 = (f32[576,1024]{1,0:T(8,128)S(1)}, f32[576,1024]{1,0:T(8,128)}, u32[]{:S(2)}) copy-start(f32[576,1024]{1,0:T(8,128)} %reshape.103) | copy-start | bytes 7077892
Sparse Core Ops, SparseCore 0:
  10.4 53.4 all-gather.1
  108.9 66.2 reduce-scatter.1
where the time goes:
time: 182 us
  blocking collectives  73.8 us (41%)
  waiting for transfers between devices  67.1 us (37%)
  between operations  14.2 us (8%)
  matrix products  11 us (6%)
  local copies, waits for them, and re-layouts  10.1 us (6%)
  other arithmetic  5.73 us (3%)
    all_to_all x1, blocking collectives, per_device(): lax.all_to_all(sent, 'dp', split_axis=0, concat_axis=0, tiled=True)  73.8 us
    reduce_scatter x1, waiting for transfers between devices, per_device(): lax.psum_scatter(lax.dot_general(columns, dpre, (((0,), (0,)), ((), ())),...  66.4 us
    dot_general x1, matrix products, per_device(): lax.dot_general(columns, dpre, (((0,), (0,)), ((), ())), preferred_elemen...  5.67 us
    gather x2, local copies, waits for them, and re-layouts, per_device(): picked = jnp.take(local, order, axis=0)  5.57 us
    dot_general x1, matrix products, per_device(): jnp.dot(columns, lax.all_gather(w_pw, 'fsdp', axis=0, tiled=True), prefer...  5.31 us
  transfers between devices with their start and end apart: 2, of which 1 were waited for; matrix products, arithmetic and copies ran while one was open for 7% of the time, Pallas kernels for 0%

commit v1 on v0

v1 whole, which is shorter than its diff:
```python
import jax
import jax.numpy as jnp
from jax import lax
from jax.experimental import pallas as pl
from jax.experimental.pallas import tpu as pltpu
from jax.sharding import Mesh, PartitionSpec as P


BF, F32 = jnp.bfloat16, jnp.float32


def spread(half, transposed=False):
    shape = (192, 96) if transposed else (96, 192)
    narrow = lax.broadcasted_iota(jnp.int32, shape, 1 if transposed else 0)
    wide = lax.broadcasted_iota(jnp.int32, shape, 0 if transposed else 1)
    hit = wide == narrow + (narrow // 12 + half) * 12
    return jnp.where(hit, 1.0, 0.0).astype(BF)


def pick_kernel(route_ref, valid_ref, frames_ref, out_ref):
    rows = frames_ref.shape[0]
    lane = lax.broadcasted_iota(jnp.int32, (rows, rows), 1)
    sub = lax.broadcasted_iota(jnp.int32, (rows, rows), 0)
    order = jnp.sum(jnp.where(lane == sub, route_ref[...].astype(F32), 0.0), axis=1, keepdims=True)
    hit = (lane == order.astype(jnp.int32)) & (valid_ref[...] > 0)
    chosen = jnp.where(hit, 1.0, 0.0).astype(BF)
    values = jnp.dot(chosen, frames_ref[...], preferred_element_type=F32)
    mean = jnp.mean(values, axis=-1, keepdims=True)
    centred = values - mean
    variance = jnp.mean(centred * centred, axis=-1, keepdims=True)
    normed = (centred * lax.rsqrt(variance + 1e-05)).astype(BF)
    low, high = spread(0, True), spread(1, True)
    for b in range(rows // 96):
        part = normed[b * 96:(b + 1) * 96]
        both = jnp.dot(low, part[:, :512], preferred_element_type=F32)
        both += jnp.dot(high, part[:, 512:], preferred_element_type=F32)
        out_ref[b * 192:(b + 1) * 192, :] = both.astype(BF)


def gate(normed, flip, wa_ref, wb_ref, cot_ref, gated_ref, keep_ref, send_ref):
    first = jnp.dot(normed, wa_ref[...], preferred_element_type=F32)
    second = jax.nn.sigmoid(jnp.dot(normed, wb_ref[...], preferred_element_type=F32))
    gated = first * second
    gated_ref[...] = gated.astype(BF)
    upstream = cot_ref[...].astype(F32)
    da = (upstream * second).astype(BF)
    db = (upstream * gated * (1.0 - second)).astype(BF)
    for h, slope in enumerate((da, db)):
        grad = jnp.dot(flip, slope, preferred_element_type=F32).astype(BF)
        keep_ref[0, h], keep_ref[1, h] = grad[:256], grad[256:512]
        send_ref[0, h], send_ref[1, h] = grad[512:768], grad[768:]


def first_kernel(pos_ref, got_ref, wa_ref, wb_ref, cot_ref, gated_ref, keep_ref, send_ref, normed_ref, flip_ref):
    @pl.when(pl.program_id(0) == 0)
    def _():
        low, high = spread(0), spread(1)
        for b in range(6):
            part = got_ref[b * 192:(b + 1) * 192, :]
            normed_ref[b * 96:(b + 1) * 96, :512] = jnp.dot(low, part, preferred_element_type=F32).astype(BF)
            normed_ref[b * 96:(b + 1) * 96, 512:] = jnp.dot(high, part, preferred_element_type=F32).astype(BF)
        for f in range(0, 16, 2):
            turned = normed_ref[:, f * 64:f * 64 + 128].T
            flip_ref[pos_ref[f]] = turned[:64]
            flip_ref[pos_ref[f + 1]] = turned[64:]

    flip = flip_ref[...].reshape(1024, 576)
    gate(normed_ref[...], flip, wa_ref, wb_ref, cot_ref, gated_ref, keep_ref, send_ref)


def second_kernel(pos_ref, normed_ref, flip_ref, wa_ref, wb_ref, cot_ref, _, gated_ref, keep_ref, send_ref):
    flip = flip_ref[...].reshape(1024, 576)
    gate(normed_ref[...], flip, wa_ref, wb_ref, cot_ref, gated_ref, keep_ref, send_ref)


COLS = 256
STEPS = 512 // COLS


def half_call(pos, lead, w, cot, gated=None):
    second = gated is not None
    fixed = lambda shape: pl.BlockSpec(shape, lambda j, p: (0,) * len(shape))
    wide = pl.BlockSpec((576, COLS), lambda j, p: (0, p[16] * STEPS + j))
    grad = pl.BlockSpec((2, 2, 256, COLS), lambda j, p: (0, 0, 0, j))
    in_specs = [fixed(a.shape) for a in lead]
    in_specs += [pl.BlockSpec((1024, COLS), lambda j, p: (0, j)), pl.BlockSpec((1024, COLS), lambda j, p: (0, j + STEPS)), wide]
    out_specs = [wide] + [grad] * 2
    out_shape = [jax.ShapeDtypeStruct((576, 1024), BF)] + [jax.ShapeDtypeStruct((2, 2, 256, 512), BF)] * 2
    args = [pos, *lead, w, w, cot]
    alias = {}
    if second:
        in_specs.append(pl.BlockSpec(memory_space=pl.ANY))
        alias = {len(args): 0}
        args.append(gated)
    else:
        out_specs += [fixed((576, 1024)), fixed((16, 64, 576))]
        out_shape += [jax.ShapeDtypeStruct((576, 1024), BF), jax.ShapeDtypeStruct((16, 64, 576), BF)]
    gs = pltpu.PrefetchScalarGridSpec(num_scalar_prefetch=1, grid=(STEPS,), in_specs=in_specs, out_specs=out_specs)
    return pl.pallas_call(
        second_kernel if second else first_kernel,
        grid_spec=gs,
        out_shape=out_shape,
        input_output_aliases=alias,
        compiler_params=pltpu.CompilerParams(vmem_limit_bytes=40 << 20),
        name="second" if second else "first",
    )(*args)


def add(u, v):
    return (u.astype(F32) + v.astype(F32)).astype(BF)


def add3(u, v, t):
    return (u.astype(F32) + v.astype(F32) + t.astype(F32)).astype(BF)


def body(frames, route, valid, w_pw, cotangent):
    y, c = lax.axis_index("y"), lax.axis_index("c")
    swap = [(0, 1), (1, 0)]
    shift = lambda d: [(i, (i + d) % 8) for i in range(8)]
    right = [(i, i ^ 1) for i in range(8)]
    left = [(i, (i + 1) % 8 if i % 2 else (i - 1) % 8) for i in range(8)]

    mate = lax.ppermute(w_pw, "c", swap)
    rows = jnp.where(c == 0, jnp.concatenate([w_pw, mate]), jnp.concatenate([mate, w_pw]))
    quarter = [rows[:, q * 512:(q + 1) * 512] for q in range(4)]
    mine = jnp.concatenate([jnp.where(c == 0, quarter[0], quarter[1]), jnp.where(c == 0, quarter[2], quarter[3])], axis=1)

    out = pl.pallas_call(
        pick_kernel,
        out_shape=jax.ShapeDtypeStruct((1152, 512), BF),
        compiler_params=pltpu.CompilerParams(vmem_limit_bytes=30 << 20),
        name="pick",
    )(route[0], valid[0], frames[0, 0])
    got = lax.all_to_all(out.reshape(48, 24, 512), ("z", "x"), 0, 0, tiled=True).reshape(1152, 512)

    same = jnp.zeros((4, 128, 1024), BF)
    for d in (0, 2, 6, 4):
        piece = lax.ppermute(mine, "y", shift(d)) if d else mine
        same = lax.dynamic_update_slice(same, piece[None], (((y - d) & 7) >> 1, 0, 0))
    cross = jnp.concatenate([lax.ppermute(same[:2], "y", right), lax.ppermute(same[2:], "y", left)])
    pair = jnp.where((y & 1) == 0, jnp.stack([same, cross], axis=1), jnp.stack([cross, same], axis=1))
    w_own = pair.reshape(1024, 1024)
    w_mate = lax.ppermute(w_own, "c", swap)

    f = jnp.arange(16, dtype=jnp.int32)
    pos = ((f & 1) ^ c) * 8 + (((f >> 1) & 1) ^ (y & 1)) * 4 + (f >> 2)
    pos_own = jnp.concatenate([pos, c[None]]).astype(jnp.int32)
    pos_mate = jnp.concatenate([pos, 1 - c[None]]).astype(jnp.int32)
    cot = cotangent[0, 0]
    gated, own, send_own, normed, flip = half_call(pos_own, (got,), w_own, cot)
    got_other = lax.ppermute(send_own, "c", swap)
    gated, other, send_other = half_call(pos_mate, (normed, flip), w_mate, cot, gated)
    got_own = lax.ppermute(send_other, "c", swap)
    peer = lax.ppermute(add(other[1], got_other[1]), "y", right)
    other = add3(other[0], got_other[0], peer)
    peer = lax.ppermute(add(own[1], got_own[1]), "y", left)
    own = add3(own[0], got_own[0], peer)
    both = jnp.concatenate([g.reshape(2, 4, 64, 512)[h] for g in (own, other) for h in (0, 1)], axis=2)
    parts = lax.all_to_all(both, "y", 0, 0, tiled=True, axis_index_groups=[[0, 2, 4, 6], [1, 3, 5, 7]])
    grad = jnp.sum(parts.astype(F32), axis=0).astype(BF)
    oa, ob, ma, mb = (grad[:, q * 512:(q + 1) * 512] for q in range(4))
    grad = jnp.where(c == 0, jnp.concatenate([oa, ma, ob, mb], axis=1), jnp.concatenate([ma, oa, mb, ob], axis=1))
    return gated[None, None], grad[None]


def solution(mesh):
    fine = Mesh(mesh.devices.reshape(12, 4, 8, 2), ("z", "x", "y", "c"))
    dp, fsdp = ("z", "x"), ("y", "c")
    in_specs = (P(dp, fsdp), P(dp, fsdp), P(dp, fsdp), P(fsdp), P(dp, fsdp))
    return jax.shard_map(body, mesh=fine, in_specs=in_specs, out_specs=(P(dp, fsdp), P(dp, fsdp)), check_vma=False)
```

time: 182 us -> 155 us (0.85)
  the two profiles are of different devices: /device:TPU:25 before, /device:TPU:8 now
where the time goes in v1:
time: 155 us; the launch traced here: 154 us
  starting transfers between devices  52.4 us (34%)
  waiting for transfers between devices  47.6 us (31%)
  blocking collectives  32.4 us (21%)
  Pallas kernels  15.5 us (10%)
  other arithmetic  5.14 us (3%)
    all_to_all x1, blocking collectives, body(): lax.all_to_all(both, 'y', 0, 0, tiled=True, axis_index_groups=[[0, 2, 4,...  32.4 us
    ppermute x3, waiting for transfers between devices, body(): piece = lax.ppermute(mine, 'y', shift(d)) if d else mine  20.4 us
    all_to_all x1, starting transfers between devices, body(): lax.all_to_all(out.reshape(48, 24, 512), ('z', 'x'), 0, 0, tiled=True)  18.5 us
    ppermute x3, starting transfers between devices, body(): piece = lax.ppermute(mine, 'y', shift(d)) if d else mine  14.8 us
    pallas_call x2, Pallas kernels, half_call(): pl.pallas_call(second_kernel if second else first_kernel, grid_spec=gs, o...  12.2 us
    ppermute x1, waiting for transfers between devices, body(): lax.ppermute(same[:2], 'y', right)  11.2 us
    ppermute x1, waiting for transfers between devices, body(): peer = lax.ppermute(add(own[1], got_own[1]), 'y', left)  8.87 us
    ppermute x1, starting transfers between devices, body(): peer = lax.ppermute(add(other[1], got_other[1]), 'y', right)  4.86 us
  transfers between devices with their start and end apart: 12, of which 8 were waited for; matrix products, arithmetic and copies ran while one was open for 2% of the time, Pallas kernels for 7%

profile of v1, /device:TPU:8, one launch (start us, length us, event | category | flops | bytes accessed | tf_op | source)
XLA Modules:
  0.0 154.4 jit_solution(4043011211615036085)
XLA Ops:
  0.6 0.0 copy-start.2
  0.6 0.0 copy-start.3
  0.7 0.0 copy-start.1
  0.7 2.1 %collective-permute-start = (bf16[64,2048]{1,0:T(8,128)(2,1)}, bf16[64,2048]{1,0:T(8,128)(2,1)S(1)}, u32[]{:S(2)}, u32[]{:S(2)}) collective-permute-start(bf16[64,2048]{1,0:T(8,128)(2,1)} %param.8), channel_id=1, source_target_pairs={{0,1},{1,0},{2,3},{3,2},{4,5},{5,4},{6,7},{7,6},{8,9},{9,8},{10,11... | collective-permute-start | bytes 786440 | tf_op jit(solution)/shard_map/ppermute | solution.py:124
  2.7 1.7 %collective-permute-done = bf16[64,2048]{1,0:T(8,128)(2,1)S(1)} collective-permute-done((bf16[64,2048]{1,0:T(8,128)(2,1)}, bf16[64,2048]{1,0:T(8,128)(2,1)S(1)}, u32[]{:S(2)}, u32[]{:S(2)}) %collective-permute-start) | collective-permute-done | bytes 262176 | tf_op jit(solution)/shard_map/ppermute | solution.py:124
  4.4 1.2 maximum_select_fusion.1
  5.7 4.5 %collective-permute-start.1 = (bf16[128,1024]{1,0:T(8,128)(2,1)S(1)}, bf16[128,1024]{1,0:T(8,128)(2,1)S(1)}, u32[]{:S(2)}, u32[]{:S(2)}) collective-permute-start(bf16[128,1024]{1,0:T(8,128)(2,1)S(1)} %pad_maximum_fusion.1), channel_id=1, source_target_pairs={{0,4},{2,6},{4,8},{6,10},{8,12},{10,14},{12,0},{14,2},{1,5},{3,7},... | collective-permute-start | bytes 786440 | tf_op jit(solution)/shard_map/ppermute | solution.py:139
  10.2 0.0 copy-done.2
  10.2 0.0 copy-done.3
  10.2 0.0 copy-done.1
  10.2 3.3 %pick.1 = bf16[1152,512]{1,0:T(8,128)(2,1)} custom-call(s32[1,576]{1,0:T(1,128)S(1)} %bitcast.50, s32[1,576]{1,0:T(1,128)S(1)} %bitcast.51, bf16[576,1024]{1,0:T(8,128)(2,1)S(1)} %bitcast.49), custom_call_target="tpu_custom_call" | custom-call | tf_op jit(solution)/shard_map/pick/pallas_call | solution.py:129
  13.5 18.5 %all-to-all-start = ((bf16[48,24,512]{2,1,0:T(8,128)(2,1)}), bf16[48,24,512]{2,1,0:T(8,128)(2,1)}, u32[]{:S(2)}, u32[]{:S(2)}) async-start(bf16[48,24,512]{2,1,0:T(8,128)(2,1)} %bitcast.4), calls=%async_computation | async-start | bytes 2359296 | tf_op jit(solution)/shard_map/all_to_all | solution.py:135
  32.0 3.5 %collective-permute-start.2 = (bf16[128,1024]{1,0:T(8,128)(2,1)S(1)}, bf16[128,1024]{1,0:T(8,128)(2,1)S(1)}, u32[]{:S(2)}, u32[]{:S(2)}) collective-permute-start(bf16[128,1024]{1,0:T(8,128)(2,1)S(1)} %pad_maximum_fusion.1), channel_id=1, source_target_pairs={{0,12},{2,14},{4,0},{6,2},{8,4},{10,6},{12,8},{14,10},{1,13},{3,15... | collective-permute-start | bytes 786440 | tf_op jit(solution)/shard_map/ppermute | solution.py:139
  35.5 6.8 %collective-permute-start.3 = (bf16[128,1024]{1,0:T(8,128)(2,1)S(1)}, bf16[128,1024]{1,0:T(8,128)(2,1)S(1)}, u32[]{:S(2)}, u32[]{:S(2)}) collective-permute-start(bf16[128,1024]{1,0:T(8,128)(2,1)S(1)} %pad_maximum_fusion.1), channel_id=1, source_target_pairs={{0,8},{2,10},{4,12},{6,14},{8,0},{10,2},{12,4},{14,6},{1,9},{3,11}... | collective-permute-start | bytes 786440 | tf_op jit(solution)/shard_map/ppermute | solution.py:139
  42.3 0.1 broadcast_in_dim.24
  42.5 0.0 collective-permute-done.1
  42.5 2.4 %collective-permute-done.2 = bf16[128,1024]{1,0:T(8,128)(2,1)S(1)} collective-permute-done((bf16[128,1024]{1,0:T(8,128)(2,1)S(1)}, bf16[128,1024]{1,0:T(8,128)(2,1)S(1)}, u32[]{:S(2)}, u32[]{:S(2)}) %collective-permute-start.2) | collective-permute-done | bytes 262176 | tf_op jit(solution)/shard_map/ppermute | solution.py:139
  44.9 18.0 %collective-permute-done.3 = bf16[128,1024]{1,0:T(8,128)(2,1)S(1)} collective-permute-done((bf16[128,1024]{1,0:T(8,128)(2,1)S(1)}, bf16[128,1024]{1,0:T(8,128)(2,1)S(1)}, u32[]{:S(2)}, u32[]{:S(2)}) %collective-permute-start.3) | collective-permute-done | bytes 262176 | tf_op jit(solution)/shard_map/ppermute | solution.py:139
  63.0 0.0 copy-start.4
  63.0 0.1 fusion.4
  63.1 1.9 %collective-permute-start.4 = (bf16[2,128,1024]{2,1,0:T(8,128)(2,1)S(1)}, bf16[2,128,1024]{2,1,0:T(8,128)(2,1)S(1)}, u32[]{:S(2)}, u32[]{:S(2)}) collective-permute-start(bf16[2,128,1024]{2,1,0:T(8,128)(2,1)S(1)} %get-tuple-element.18), channel_id=1, source_target_pairs={{0,2},{2,0},{4,6},{6,4},{8,10},{10,8},{12,14},{14,12},{1,3},{3,1},... | collective-permute-start | bytes 1572872 | tf_op jit(solution)/shard_map/ppermute | solution.py:141
  65.0 1.9 %collective-permute-start.5 = (bf16[2,128,1024]{2,1,0:T(8,128)(2,1)S(1)}, bf16[2,128,1024]{2,1,0:T(8,128)(2,1)S(1)}, u32[]{:S(2)}, u32[]{:S(2)}) collective-permute-start(bf16[2,128,1024]{2,1,0:T(8,128)(2,1)S(1)} %get-tuple-element.19), channel_id=1, source_target_pairs={{0,14},{2,4},{4,2},{6,8},{8,6},{10,12},{12,10},{14,0},{1,15},{3,5}... | collective-permute-start | bytes 1572872 | tf_op jit(solution)/shard_map/ppermute | solution.py:141
  66.9 11.2 %collective-permute-done.4 = bf16[2,128,1024]{2,1,0:T(8,128)(2,1)S(1)} collective-permute-done((bf16[2,128,1024]{2,1,0:T(8,128)(2,1)S(1)}, bf16[2,128,1024]{2,1,0:T(8,128)(2,1)S(1)}, u32[]{:S(2)}, u32[]{:S(2)}) %collective-permute-start.4) | collective-permute-done | bytes 524320 | tf_op jit(solution)/shard_map/ppermute | solution.py:141
  78.2 1.9 %collective-permute-done.5 = bf16[2,128,1024]{2,1,0:T(8,128)(2,1)S(1)} collective-permute-done((bf16[2,128,1024]{2,1,0:T(8,128)(2,1)S(1)}, bf16[2,128,1024]{2,1,0:T(8,128)(2,1)S(1)}, u32[]{:S(2)}, u32[]{:S(2)}) %collective-permute-start.5) | collective-permute-done | bytes 524320 | tf_op jit(solution)/shard_map/ppermute | solution.py:141
  80.1 0.1 maximum_bitcast_fusion
  80.2 0.0 copy-done.4
  80.2 0.0 copy-start
  80.2 1.9 %maximum_select_fusion = bf16[4,2,128,1024]{3,2,1,0:T(8,128)(2,1)S(1)} fusion(bf16[4,1,128,1024]{3,2,1,0:T(8,128)(2,1)S(1)} %maximum_bitcast_fusion, bf16[4,1,128,1024]{3,2,1,0:T(8,128)(2,1)} %bitcast.52, pred[]{:T(512)S(6)} %eq.4), kind=kLoop, calls=%fused_computation | loop fusion | flops 3145728 | bytes 4194305 | tf_op jit(solution)/shard_map/jit(_where)/select_n | solution.py:142
  82.2 1.9 %collective-permute-start.6 = (bf16[1024,1024]{1,0:T(8,128)(2,1)S(1)}, bf16[1024,1024]{1,0:T(8,128)(2,1)}, u32[]{:S(2)}, u32[]{:S(2)}) collective-permute-start(bf16[1024,1024]{1,0:T(8,128)(2,1)S(1)} %bitcast.44), channel_id=1, source_target_pairs={{0,1},{1,0},{2,3},{3,2},{4,5},{5,4},{6,7},{7,6},{8,9},{9,8},{10,11... | collective-permute-start | bytes 6291464 | tf_op jit(solution)/shard_map/ppermute | solution.py:144
  84.1 0.1 pad_add_fusion.1
  84.2 0.0 all-to-all-done
  84.2 0.0 copy-done
  84.2 6.8 %first.1 = (bf16[576,1024]{1,0:T(8,128)(2,1)}, bf16[2,2,256,512]{3,2,1,0:T(8,128)(2,1)S(1)}, bf16[2,2,256,512]{3,2,1,0:T(8,128)(2,1)S(1)}, bf16[576,1024]{1,0:T(8,128)(2,1)S(1)}, bf16[16,64,576]{2,1,0:T(8,128)(2,1)S(1)}) custom-call(s32[17]{0:T(128)S(1)} %get-tuple-element.30.pos_ref, bf16[1152,512]{1,0:T(8,128)(2,1)} %bitcast.5.got_ref, ...), custom_call_target="tpu_custom_call" | custom-call | tf_op jit(solution)/shard_map/first/pallas_call | solution.py:99
  91.0 0.0 collective-permute-done.6.wa_ref.wb_ref
  91.0 5.3 %second.1 = (bf16[576,1024]{1,0:T(8,128)(2,1)}, bf16[2,2,256,512]{3,2,1,0:T(8,128)(2,1)S(1)}, bf16[2,2,256,512]{3,2,1,0:T(8,128)(2,1)S(1)}) custom-call(s32[17]{0:T(128)S(1)} %get-tuple-element.31.pos_ref, bf16[576,1024]{1,0:T(8,128)(2,1)S(1)} %get-tuple-element.10.normed_ref, ...), custom_call_target="tpu_custom_call", output_to_operand_aliasing={{0}: (6, {})} | custom-call | tf_op jit(solution)/shard_map/second/pallas_call | solution.py:99
  96.4 2.4 %collective-permute-start.7 = (bf16[2,2,256,512]{3,2,1,0:T(8,128)(2,1)S(1)}, bf16[2,2,256,512]{3,2,1,0:T(8,128)(2,1)S(1)}, u32[]{:S(2)}, u32[]{:S(2)}) collective-permute-start(bf16[2,2,256,512]{3,2,1,0:T(8,128)(2,1)S(1)} %get-tuple-element.15), channel_id=1, source_target_pairs={{0,1},{1,0},{2,3},{3,2},{4,5},{5,4},{6,7},{7,6},{8,9},{9,8},{10,11... | collective-permute-start | bytes 3145736 | tf_op jit(solution)/shard_map/ppermute | solution.py:154
  98.8 1.9 %collective-permute-start.9 = (bf16[2,2,256,512]{3,2,1,0:T(8,128)(2,1)S(1)}, bf16[2,2,256,512]{3,2,1,0:T(8,128)(2,1)S(1)}, u32[]{:S(2)}, u32[]{:S(2)}) collective-permute-start(bf16[2,2,256,512]{3,2,1,0:T(8,128)(2,1)S(1)} %get-tuple-element.17), channel_id=1, source_target_pairs={{0,1},{1,0},{2,3},{3,2},{4,5},{5,4},{6,7},{7,6},{8,9},{9,8},{10,11... | collective-permute-start | bytes 3145736 | tf_op jit(solution)/shard_map/ppermute | solution.py:152
  100.7 0.3 collective-permute-done.7
  101.0 0.1 fusion.2
  101.2 2.2 %collective-permute-start.8 = (bf16[2,256,512]{2,1,0:T(8,128)(2,1)S(1)}, bf16[2,256,512]{2,1,0:T(8,128)(2,1)S(1)}, u32[]{:S(2)}, u32[]{:S(2)}) collective-permute-start(bf16[2,256,512]{2,1,0:T(8,128)(2,1)S(1)} %fusion.2), channel_id=1, source_target_pairs={{0,14},{2,4},{4,2},{6,8},{8,6},{10,12},{12,10},{14,0},{1,15},{3,5}... | collective-permute-start | bytes 1572872 | tf_op jit(solution)/shard_map/ppermute | solution.py:157
  103.4 0.0 collective-permute-done.9
  103.4 0.1 fusion.3
  103.5 4.9 %collective-permute-start.10 = (bf16[2,256,512]{2,1,0:T(8,128)(2,1)S(1)}, bf16[2,256,512]{2,1,0:T(8,128)(2,1)S(1)}, u32[]{:S(2)}, u32[]{:S(2)}) collective-permute-start(bf16[2,256,512]{2,1,0:T(8,128)(2,1)S(1)} %fusion.3), channel_id=1, source_target_pairs={{0,2},{2,0},{4,6},{6,4},{8,10},{10,8},{12,14},{14,12},{1,3},{3,1},... | collective-permute-start | bytes 1572872 | tf_op jit(solution)/shard_map/ppermute | solution.py:155
  108.4 8.9 %collective-permute-done.8 = bf16[2,256,512]{2,1,0:T(8,128)(2,1)S(1)} collective-permute-done((bf16[2,256,512]{2,1,0:T(8,128)(2,1)S(1)}, bf16[2,256,512]{2,1,0:T(8,128)(2,1)S(1)}, u32[]{:S(2)}, u32[]{:S(2)}) %collective-permute-start.8) | collective-permute-done | bytes 524320 | tf_op jit(solution)/shard_map/ppermute | solution.py:157
  117.3 0.2 fusion.1
  117.5 3.0 %collective-permute-done.10 = bf16[2,256,512]{2,1,0:T(8,128)(2,1)S(1)} collective-permute-done((bf16[2,256,512]{2,1,0:T(8,128)(2,1)S(1)}, bf16[2,256,512]{2,1,0:T(8,128)(2,1)S(1)}, u32[]{:S(2)}, u32[]{:S(2)}) %collective-permute-start.10) | collective-permute-done | bytes 524320 | tf_op jit(solution)/shard_map/ppermute | solution.py:155
  120.6 0.2 fusion
  120.8 0.1 pad_maximum_fusion
  120.9 32.4 %all_to_all.10 = bf16[4,64,2048]{2,1,0:T(8,128)(2,1)S(1)} all-to-all(bf16[4,64,2048]{2,1,0:T(8,128)(2,1)S(1)} %pad_maximum_fusion), channel_id=1, replica_groups={{0,4,8,12},{2,6,10,14},{1,5,9,13},{3,7,11,15},{16,20,24,28},{18,22,26,3..., dimensions={0} | all-to-all | bytes 2097152 | tf_op jit(solution)/shard_map/all_to_all | solution.py:160
  153.4 0.2 reduce_sum.12
  153.6 0.8 maximum_select_fusion.2
  (10 shorter events, 0.2 us)
Async XLA Ops:
  0.6 9.6 %copy-start.2 = (s32[1,1,576]{2,1,0:T(1,128)S(1)}, s32[1,1,576]{2,1,0:T(1,128)}, u32[]{:S(2)}) copy-start(s32[1,1,576]{2,1,0:T(1,128)} %param.6) | copy-start | bytes 6916
  0.6 9.6 %copy-start.3 = (s32[1,1,576]{2,1,0:T(1,128)S(1)}, s32[1,1,576]{2,1,0:T(1,128)}, u32[]{:S(2)}) copy-start(s32[1,1,576]{2,1,0:T(1,128)} %param.7) | copy-start | bytes 6916
  0.7 9.6 %copy-start.1 = (bf16[1,1,576,1024]{3,2,1,0:T(8,128)(2,1)S(1)}, bf16[1,1,576,1024]{3,2,1,0:T(8,128)(2,1)}, u32[]{:S(2)}) copy-start(bf16[1,1,576,1024]{3,2,1,0:T(8,128)(2,1)} %param.5) | copy-start | bytes 3538948
  0.7 3.8 %collective-permute-start = (bf16[64,2048]{1,0:T(8,128)(2,1)}, bf16[64,2048]{1,0:T(8,128)(2,1)S(1)}, u32[]{:S(2)}, u32[]{:S(2)}) collective-permute-start(bf16[64,2048]{1,0:T(8,128)(2,1)} %param.8), channel_id=1, source_target_pairs={{0,1},{1,0},{2,3},{3,2},{4,5},{5,4},{6,7},{7,6},{8,9},{9,8},{10,11... | collective-permute-start | bytes 786440 | tf_op jit(solution)/shard_map/ppermute | solution.py:124
  5.7 36.8 %collective-permute-start.1 = (bf16[128,1024]{1,0:T(8,128)(2,1)S(1)}, bf16[128,1024]{1,0:T(8,128)(2,1)S(1)}, u32[]{:S(2)}, u32[]{:S(2)}) collective-permute-start(bf16[128,1024]{1,0:T(8,128)(2,1)S(1)} %pad_maximum_fusion.1), channel_id=1, source_target_pairs={{0,4},{2,6},{4,8},{6,10},{8,12},{10,14},{12,0},{14,2},{1,5},{3,7},... | collective-permute-start | bytes 786440 | tf_op jit(solution)/shard_map/ppermute | solution.py:139
  13.5 70.7 %all-to-all-start = ((bf16[48,24,512]{2,1,0:T(8,128)(2,1)}), bf16[48,24,512]{2,1,0:T(8,128)(2,1)}, u32[]{:S(2)}, u32[]{:S(2)}) async-start(bf16[48,24,512]{2,1,0:T(8,128)(2,1)} %bitcast.4), calls=%async_computation | async-start | bytes 2359296 | tf_op jit(solution)/shard_map/all_to_all | solution.py:135
  32.0 12.9 %collective-permute-start.2 = (bf16[128,1024]{1,0:T(8,128)(2,1)S(1)}, bf16[128,1024]{1,0:T(8,128)(2,1)S(1)}, u32[]{:S(2)}, u32[]{:S(2)}) collective-permute-start(bf16[128,1024]{1,0:T(8,128)(2,1)S(1)} %pad_maximum_fusion.1), channel_id=1, source_target_pairs={{0,12},{2,14},{4,0},{6,2},{8,4},{10,6},{12,8},{14,10},{1,13},{3,15... | collective-permute-start | bytes 786440 | tf_op jit(solution)/shard_map/ppermute | solution.py:139
  35.5 27.5 %collective-permute-start.3 = (bf16[128,1024]{1,0:T(8,128)(2,1)S(1)}, bf16[128,1024]{1,0:T(8,128)(2,1)S(1)}, u32[]{:S(2)}, u32[]{:S(2)}) collective-permute-start(bf16[128,1024]{1,0:T(8,128)(2,1)S(1)} %pad_maximum_fusion.1), channel_id=1, source_target_pairs={{0,8},{2,10},{4,12},{6,14},{8,0},{10,2},{12,4},{14,6},{1,9},{3,11}... | collective-permute-start | bytes 786440 | tf_op jit(solution)/shard_map/ppermute | solution.py:139
  63.0 17.2 %copy-start.4 = (bf16[4,128,1024]{2,1,0:T(8,128)(2,1)}, bf16[4,128,1024]{2,1,0:T(8,128)(2,1)S(1)}, u32[]{:S(2)}) copy-start(bf16[4,128,1024]{2,1,0:T(8,128)(2,1)S(1)} %bitcast_dynamic-update-slice_fusion) | copy-start | bytes 3145732
  63.1 15.1 %collective-permute-start.4 = (bf16[2,128,1024]{2,1,0:T(8,128)(2,1)S(1)}, bf16[2,128,1024]{2,1,0:T(8,128)(2,1)S(1)}, u32[]{:S(2)}, u32[]{:S(2)}) collective-permute-start(bf16[2,128,1024]{2,1,0:T(8,128)(2,1)S(1)} %get-tuple-element.18), channel_id=1, source_target_pairs={{0,2},{2,0},{4,6},{6,4},{8,10},{10,8},{12,14},{14,12},{1,3},{3,1},... | collective-permute-start | bytes 1572872 | tf_op jit(solution)/shard_map/ppermute | solution.py:141
  65.0 15.1 %collective-permute-start.5 = (bf16[2,128,1024]{2,1,0:T(8,128)(2,1)S(1)}, bf16[2,128,1024]{2,1,0:T(8,128)(2,1)S(1)}, u32[]{:S(2)}, u32[]{:S(2)}) collective-permute-start(bf16[2,128,1024]{2,1,0:T(8,128)(2,1)S(1)} %get-tuple-element.19), channel_id=1, source_target_pairs={{0,14},{2,4},{4,2},{6,8},{8,6},{10,12},{12,10},{14,0},{1,15},{3,5}... | collective-permute-start | bytes 1572872 | tf_op jit(solution)/shard_map/ppermute | solution.py:141
  80.2 4.0 %copy-start = (bf16[1,1,576,1024]{3,2,1,0:T(8,128)(2,1)S(1)}, bf16[1,1,576,1024]{3,2,1,0:T(8,128)(2,1)}, u32[]{:S(2)}) copy-start(bf16[1,1,576,1024]{3,2,1,0:T(8,128)(2,1)} %param.9) | copy-start | bytes 3538948
  82.2 8.8 %collective-permute-start.6 = (bf16[1024,1024]{1,0:T(8,128)(2,1)S(1)}, bf16[1024,1024]{1,0:T(8,128)(2,1)}, u32[]{:S(2)}, u32[]{:S(2)}) collective-permute-start(bf16[1024,1024]{1,0:T(8,128)(2,1)S(1)} %bitcast.44), channel_id=1, source_target_pairs={{0,1},{1,0},{2,3},{3,2},{4,5},{5,4},{6,7},{7,6},{8,9},{9,8},{10,11... | collective-permute-start | bytes 6291464 | tf_op jit(solution)/shard_map/ppermute | solution.py:144
  96.4 4.7 %collective-permute-start.7 = (bf16[2,2,256,512]{3,2,1,0:T(8,128)(2,1)S(1)}, bf16[2,2,256,512]{3,2,1,0:T(8,128)(2,1)S(1)}, u32[]{:S(2)}, u32[]{:S(2)}) collective-permute-start(bf16[2,2,256,512]{3,2,1,0:T(8,128)(2,1)S(1)} %get-tuple-element.15), channel_id=1, source_target_pairs={{0,1},{1,0},{2,3},{3,2},{4,5},{5,4},{6,7},{7,6},{8,9},{9,8},{10,11... | collective-permute-start | bytes 3145736 | tf_op jit(solution)/shard_map/ppermute | solution.py:154
  98.8 4.6 %collective-permute-start.9 = (bf16[2,2,256,512]{3,2,1,0:T(8,128)(2,1)S(1)}, bf16[2,2,256,512]{3,2,1,0:T(8,128)(2,1)S(1)}, u32[]{:S(2)}, u32[]{:S(2)}) collective-permute-start(bf16[2,2,256,512]{3,2,1,0:T(8,128)(2,1)S(1)} %get-tuple-element.17), channel_id=1, source_target_pairs={{0,1},{1,0},{2,3},{3,2},{4,5},{5,4},{6,7},{7,6},{8,9},{9,8},{10,11... | collective-permute-start | bytes 3145736 | tf_op jit(solution)/shard_map/ppermute | solution.py:152
  101.2 16.1 %collective-permute-start.8 = (bf16[2,256,512]{2,1,0:T(8,128)(2,1)S(1)}, bf16[2,256,512]{2,1,0:T(8,128)(2,1)S(1)}, u32[]{:S(2)}, u32[]{:S(2)}) collective-permute-start(bf16[2,256,512]{2,1,0:T(8,128)(2,1)S(1)} %fusion.2), channel_id=1, source_target_pairs={{0,14},{2,4},{4,2},{6,8},{8,6},{10,12},{12,10},{14,0},{1,15},{3,5}... | collective-permute-start | bytes 1572872 | tf_op jit(solution)/shard_map/ppermute | solution.py:157
  103.5 17.0 %collective-permute-start.10 = (bf16[2,256,512]{2,1,0:T(8,128)(2,1)S(1)}, bf16[2,256,512]{2,1,0:T(8,128)(2,1)S(1)}, u32[]{:S(2)}, u32[]{:S(2)}) collective-permute-start(bf16[2,256,512]{2,1,0:T(8,128)(2,1)S(1)} %fusion.3), channel_id=1, source_target_pairs={{0,2},{2,0},{4,6},{6,4},{8,10},{10,8},{12,14},{14,12},{1,3},{3,1},... | collective-permute-start | bytes 1572872 | tf_op jit(solution)/shard_map/ppermute | solution.py:155

commit v2 on v1

--- a/solution.py
+++ b/solution.py
@@ -47,8 +47,9 @@
     db = (upstream * gated * (1.0 - second)).astype(BF)
     for h, slope in enumerate((da, db)):
         grad = jnp.dot(flip, slope, preferred_element_type=F32).astype(BF)
-        keep_ref[0, h], keep_ref[1, h] = grad[:256], grad[256:512]
-        send_ref[0, h], send_ref[1, h] = grad[512:768], grad[768:]
+        for d in range(8):
+            keep_ref[d, h] = grad[d * 64:d * 64 + 64]
+            send_ref[d, h] = grad[d * 64 + 512:d * 64 + 576]
 
 
 def first_kernel(pos_ref, got_ref, wa_ref, wb_ref, cot_ref, gated_ref, keep_ref, send_ref, normed_ref, flip_ref):
@@ -81,11 +82,11 @@
     second = gated is not None
     fixed = lambda shape: pl.BlockSpec(shape, lambda j, p: (0,) * len(shape))
     wide = pl.BlockSpec((576, COLS), lambda j, p: (0, p[16] * STEPS + j))
-    grad = pl.BlockSpec((2, 2, 256, COLS), lambda j, p: (0, 0, 0, j))
+    grad = pl.BlockSpec((8, 2, 64, COLS), lambda j, p: (0, 0, 0, j))
     in_specs = [fixed(a.shape) for a in lead]
     in_specs += [pl.BlockSpec((1024, COLS), lambda j, p: (0, j)), pl.BlockSpec((1024, COLS), lambda j, p: (0, j + STEPS)), wide]
     out_specs = [wide] + [grad] * 2
-    out_shape = [jax.ShapeDtypeStruct((576, 1024), BF)] + [jax.ShapeDtypeStruct((2, 2, 256, 512), BF)] * 2
+    out_shape = [jax.ShapeDtypeStruct((576, 1024), BF)] + [jax.ShapeDtypeStruct((8, 2, 64, 512), BF)] * 2
     args = [pos, *lead, w, w, cot]
     alias = {}
     if second:
@@ -106,20 +107,21 @@
     )(*args)
 
 
-def add(u, v):
-    return (u.astype(F32) + v.astype(F32)).astype(BF)
+def total(*parts):
+    acc = parts[0].astype(F32)
+    for part in parts[1:]:
+        acc = acc + part.astype(F32)
+    return acc.astype(BF)
 
 
-def add3(u, v, t):
-    return (u.astype(F32) + v.astype(F32) + t.astype(F32)).astype(BF)
+def after(value, other):
+    return lax.optimization_barrier((value, other))[0]
 
 
 def body(frames, route, valid, w_pw, cotangent):
     y, c = lax.axis_index("y"), lax.axis_index("c")
     swap = [(0, 1), (1, 0)]
     shift = lambda d: [(i, (i + d) % 8) for i in range(8)]
-    right = [(i, i ^ 1) for i in range(8)]
-    left = [(i, (i + 1) % 8 if i % 2 else (i - 1) % 8) for i in range(8)]
 
     mate = lax.ppermute(w_pw, "c", swap)
     rows = jnp.where(c == 0, jnp.concatenate([w_pw, mate]), jnp.concatenate([mate, w_pw]))
@@ -134,17 +136,21 @@
     )(route[0], valid[0], frames[0, 0])
     got = lax.all_to_all(out.reshape(48, 24, 512), ("z", "x"), 0, 0, tiled=True).reshape(1152, 512)
 
-    same = jnp.zeros((4, 128, 1024), BF)
-    for d in (0, 2, 6, 4):
-        piece = lax.ppermute(mine, "y", shift(d)) if d else mine
-        same = lax.dynamic_update_slice(same, piece[None], (((y - d) & 7) >> 1, 0, 0))
-    cross = jnp.concatenate([lax.ppermute(same[:2], "y", right), lax.ppermute(same[2:], "y", left)])
-    pair = jnp.where((y & 1) == 0, jnp.stack([same, cross], axis=1), jnp.stack([cross, same], axis=1))
-    w_own = pair.reshape(1024, 1024)
+    w_own = jnp.zeros((8, 128, 1024), BF)
+    place = lambda buf, piece, d, at=0: lax.dynamic_update_slice(buf, piece[None], ((y + d) & 7, at, 0))
+    w_own = place(w_own, mine, 0)
+    up = down = mine
+    for step in range(1, 4):
+        up = lax.ppermute(up, "y", shift(1))
+        down = lax.ppermute(down, "y", shift(-1))
+        w_own = place(place(w_own, up, -step), down, step)
+    up = lax.ppermute(up[:64], "y", shift(1))
+    down = lax.ppermute(down[64:], "y", shift(-1))
+    w_own = place(place(w_own, up, 4), down, 4, 64).reshape(1024, 1024)
     w_mate = lax.ppermute(w_own, "c", swap)
 
     f = jnp.arange(16, dtype=jnp.int32)
-    pos = ((f & 1) ^ c) * 8 + (((f >> 1) & 1) ^ (y & 1)) * 4 + (f >> 2)
+    pos = ((f & 1) ^ c) * 8 + (((f >> 1) - y) & 7)
     pos_own = jnp.concatenate([pos, c[None]]).astype(jnp.int32)
     pos_mate = jnp.concatenate([pos, 1 - c[None]]).astype(jnp.int32)
     cot = cotangent[0, 0]
@@ -152,14 +158,25 @@
     got_other = lax.ppermute(send_own, "c", swap)
     gated, other, send_other = half_call(pos_mate, (normed, flip), w_mate, cot, gated)
     got_own = lax.ppermute(send_other, "c", swap)
-    peer = lax.ppermute(add(other[1], got_other[1]), "y", right)
-    other = add3(other[0], got_other[0], peer)
-    peer = lax.ppermute(add(own[1], got_own[1]), "y", left)
-    own = add3(own[0], got_own[0], peer)
-    both = jnp.concatenate([g.reshape(2, 4, 64, 512)[h] for g in (own, other) for h in (0, 1)], axis=2)
-    parts = lax.all_to_all(both, "y", 0, 0, tiled=True, axis_index_groups=[[0, 2, 4, 6], [1, 3, 5, 7]])
-    grad = jnp.sum(parts.astype(F32), axis=0).astype(BF)
-    oa, ob, ma, mb = (grad[:, q * 512:(q + 1) * 512] for q in range(4))
+    near, far = (lambda d: (own[d], got_own[d])), (lambda d: (other[d], got_other[d]))
+    up = lax.ppermute(total(*far(4)), "y", shift(1))
+    down = lax.ppermute(total(*near(4)), "y", shift(-1))
+    for step in range(2, 5):
+        d = 5 - step
+        if step == 2:
+            up = jnp.concatenate([total(*near(d)), total(*far(d), up)])
+            down = after(down, up)
+            down = jnp.concatenate([total(*near(8 - d), down), total(*far(8 - d))])
+        else:
+            up = after(up, down_sent)
+            up = jnp.concatenate([total(*near(d), up[:2]), total(*far(d), up[2:])])
+            down = after(down, up)
+            down = jnp.concatenate([total(*near(8 - d), down[:2]), total(*far(8 - d), down[2:])])
+        down_sent = down
+        up = lax.ppermute(up, "y", shift(1))
+        down = lax.ppermute(down, "y", shift(-1))
+    oa, ob = total(*near(0), up[:2], down[:2])
+    ma, mb = total(*far(0), up[2:], down[2:])
     grad = jnp.where(c == 0, jnp.concatenate([oa, ma, ob, mb], axis=1), jnp.concatenate([ma, oa, mb, ob], axis=1))
     return gated[None, None], grad[None]
 

time: 155 us -> 145 us (0.935)
  the two profiles are of different devices: /device:TPU:8 before, /device:TPU:4 now
where the time goes in v2:
time: 145 us; the launch traced here: 144 us
  starting transfers between devices  83.9 us (58%)
  waiting for transfers between devices  38.2 us (26%)
  Pallas kernels  15.5 us (11%)
  other arithmetic  3.76 us (3%)
    ppermute x6, starting transfers between devices, body(): down = lax.ppermute(down, 'y', shift(-1))  29.8 us
    all_to_all x1, starting transfers between devices, body(): lax.all_to_all(out.reshape(48, 24, 512), ('z', 'x'), 0, 0, tiled=True)  18.6 us
    ppermute x6, waiting for transfers between devices, body(): up = lax.ppermute(up, 'y', shift(1))  16.7 us
    ppermute x6, starting transfers between devices, body(): up = lax.ppermute(up, 'y', shift(1))  13.3 us
    all_to_all x1, waiting for transfers between devices, body(): lax.all_to_all(out.reshape(48, 24, 512), ('z', 'x'), 0, 0, tiled=True)  12.5 us
    pallas_call x2, Pallas kernels, half_call(): pl.pallas_call(second_kernel if second else first_kernel, grid_spec=gs, o...  12.2 us
    ppermute x1, starting transfers between devices, body(): down = lax.ppermute(down[64:], 'y', shift(-1))  5.13 us
    ppermute x1, starting transfers between devices, body(): down = lax.ppermute(total(*near(4)), 'y', shift(-1))  4.9 us
  transfers between devices with their start and end apart: 21, of which 13 were waited for; matrix products, arithmetic and copies ran while one was open for 2% of the time, Pallas kernels for 11%

profile of v2, /device:TPU:4, one launch (start us, length us, event | category | flops | bytes accessed | tf_op | source)
XLA Modules:
  0.0 143.9 jit_solution(8164977605187761780)
XLA Ops:
  0.6 0.0 copy-start.2
  0.6 0.0 copy-start.3
  0.7 2.1 %collective-permute-start = (bf16[64,2048]{1,0:T(8,128)(2,1)}, bf16[64,2048]{1,0:T(8,128)(2,1)S(1)}, u32[]{:S(2)}, u32[]{:S(2)}) collective-permute-start(bf16[64,2048]{1,0:T(8,128)(2,1)} %param.8), channel_id=1, source_target_pairs={{0,1},{1,0},{2,3},{3,2},{4,5},{5,4},{6,7},{7,6},{8,9},{9,8},{10,11... | collective-permute-start | bytes 786440 | tf_op jit(solution)/shard_map/ppermute | solution.py:126
  2.7 1.7 %collective-permute-done = bf16[64,2048]{1,0:T(8,128)(2,1)S(1)} collective-permute-done((bf16[64,2048]{1,0:T(8,128)(2,1)}, bf16[64,2048]{1,0:T(8,128)(2,1)S(1)}, u32[]{:S(2)}, u32[]{:S(2)}) %collective-permute-start) | collective-permute-done | bytes 262176 | tf_op jit(solution)/shard_map/ppermute | solution.py:126
  4.4 1.2 maximum_select_fusion
  5.7 0.7 pad_maximum_fusion
  6.4 3.5 %collective-permute-start.1 = (bf16[128,1024]{1,0:T(8,128)(2,1)}, bf16[128,1024]{1,0:T(8,128)(2,1)}, u32[]{:S(2)}, u32[]{:S(2)}) collective-permute-start(bf16[128,1024]{1,0:T(8,128)(2,1)} %pad_maximum_fusion), channel_id=1, source_target_pairs={{0,2},{2,4},{4,6},{6,8},{8,10},{10,12},{12,14},{14,0},{1,3},{3,5},... | collective-permute-start | bytes 786440 | tf_op jit(solution)/shard_map/ppermute | solution.py:144
  9.9 3.8 %collective-permute-start.2 = (bf16[128,1024]{1,0:T(8,128)(2,1)}, bf16[128,1024]{1,0:T(8,128)(2,1)S(1)}, u32[]{:S(2)}, u32[]{:S(2)}) collective-permute-start(bf16[128,1024]{1,0:T(8,128)(2,1)} %pad_maximum_fusion), channel_id=1, source_target_pairs={{0,14},{2,0},{4,2},{6,4},{8,6},{10,8},{12,10},{14,12},{1,15},{3,1}... | collective-permute-start | bytes 786440 | tf_op jit(solution)/shard_map/ppermute | solution.py:145
  13.7 3.3 %pick.1 = bf16[1152,512]{1,0:T(8,128)(2,1)} custom-call(s32[1,576]{1,0:T(1,128)S(1)} %bitcast.93, s32[1,576]{1,0:T(1,128)S(1)} %bitcast.94, bf16[576,1024]{1,0:T(8,128)(2,1)S(1)} %bitcast.92), custom_call_target="tpu_custom_call" | custom-call | tf_op jit(solution)/shard_map/pick/pallas_call | solution.py:131
  17.0 18.6 %all-to-all-start = ((bf16[48,24,512]{2,1,0:T(8,128)(2,1)}), bf16[48,24,512]{2,1,0:T(8,128)(2,1)}, u32[]{:S(2)}, u32[]{:S(2)}) async-start(bf16[48,24,512]{2,1,0:T(8,128)(2,1)} %bitcast.4), calls=%async_computation | async-start | bytes 2359296 | tf_op jit(solution)/shard_map/all_to_all | solution.py:137
  35.6 0.3 broadcast_in_dim.39
  35.9 0.0 copy-start
  35.9 0.0 collective-permute-done.1
  35.9 2.2 %collective-permute-start.3 = (bf16[128,1024]{1,0:T(8,128)(2,1)}, bf16[128,1024]{1,0:T(8,128)(2,1)S(1)}, u32[]{:S(2)}, u32[]{:S(2)}) collective-permute-start(bf16[128,1024]{1,0:T(8,128)(2,1)} %collective-permute-done.1), channel_id=1, source_target_pairs={{0,2},{2,4},{4,6},{6,8},{8,10},{10,12},{12,14},{14,0},{1,3},{3,5},... | collective-permute-start | bytes 786440 | tf_op jit(solution)/shard_map/ppermute | solution.py:144
  38.1 0.0 collective-permute-done.2
  38.1 5.0 %collective-permute-start.4 = (bf16[128,1024]{1,0:T(8,128)(2,1)S(1)}, bf16[128,1024]{1,0:T(8,128)(2,1)S(1)}, u32[]{:S(2)}, u32[]{:S(2)}) collective-permute-start(bf16[128,1024]{1,0:T(8,128)(2,1)S(1)} %collective-permute-done.2), channel_id=1, source_target_pairs={{0,14},{2,0},{4,2},{6,4},{8,6},{10,8},{12,10},{14,12},{1,15},{3,1}... | collective-permute-start | bytes 786440 | tf_op jit(solution)/shard_map/ppermute | solution.py:145
  43.1 1.0 bitcast_dynamic-update-slice_fusion.5
  44.2 2.7 %collective-permute-done.3 = bf16[128,1024]{1,0:T(8,128)(2,1)S(1)} collective-permute-done((bf16[128,1024]{1,0:T(8,128)(2,1)}, bf16[128,1024]{1,0:T(8,128)(2,1)S(1)}, u32[]{:S(2)}, u32[]{:S(2)}) %collective-permute-start.3) | collective-permute-done | bytes 262176 | tf_op jit(solution)/shard_map/ppermute | solution.py:144
  46.9 1.9 %collective-permute-start.5 = (bf16[128,1024]{1,0:T(8,128)(2,1)S(1)}, bf16[128,1024]{1,0:T(8,128)(2,1)S(1)}, u32[]{:S(2)}, u32[]{:S(2)}) collective-permute-start(bf16[128,1024]{1,0:T(8,128)(2,1)S(1)} %collective-permute-done.3), channel_id=1, source_target_pairs={{0,2},{2,4},{4,6},{6,8},{8,10},{10,12},{12,14},{14,0},{1,3},{3,5},... | collective-permute-start | bytes 786440 | tf_op jit(solution)/shard_map/ppermute | solution.py:144
  48.8 0.0 collective-permute-done.4
  48.8 5.1 %collective-permute-start.6 = (bf16[128,1024]{1,0:T(8,128)(2,1)S(1)}, bf16[128,1024]{1,0:T(8,128)(2,1)S(1)}, u32[]{:S(2)}, u32[]{:S(2)}) collective-permute-start(bf16[128,1024]{1,0:T(8,128)(2,1)S(1)} %collective-permute-done.4), channel_id=1, source_target_pairs={{0,14},{2,0},{4,2},{6,4},{8,6},{10,8},{12,10},{14,12},{1,15},{3,1}... | collective-permute-start | bytes 786440 | tf_op jit(solution)/shard_map/ppermute | solution.py:145
  54.0 2.7 %collective-permute-done.5 = bf16[128,1024]{1,0:T(8,128)(2,1)S(1)} collective-permute-done((bf16[128,1024]{1,0:T(8,128)(2,1)S(1)}, bf16[128,1024]{1,0:T(8,128)(2,1)S(1)}, u32[]{:S(2)}, u32[]{:S(2)}) %collective-permute-start.5) | collective-permute-done | bytes 262176 | tf_op jit(solution)/shard_map/ppermute | solution.py:144
  56.7 1.9 %collective-permute-start.7 = (bf16[64,1024]{1,0:T(8,128)(2,1)S(1)}, bf16[64,1024]{1,0:T(8,128)(2,1)S(1)}, u32[]{:S(2)}, u32[]{:S(2)}) collective-permute-start(bf16[64,1024]{1,0:T(8,128)(2,1)S(1)} %slice.204), channel_id=1, source_target_pairs={{0,2},{2,4},{4,6},{6,8},{8,10},{10,12},{12,14},{14,0},{1,3},{3,5},... | collective-permute-start | bytes 393224 | tf_op jit(solution)/shard_map/ppermute | solution.py:147
  58.7 0.0 collective-permute-done.6
  58.7 5.1 %collective-permute-start.8 = (bf16[64,1024]{1,0:T(8,128)(2,1)S(1)}, bf16[64,1024]{1,0:T(8,128)(2,1)S(1)}, u32[]{:S(2)}, u32[]{:S(2)}) collective-permute-start(bf16[64,1024]{1,0:T(8,128)(2,1)S(1)} %slice.205), channel_id=1, source_target_pairs={{0,14},{2,0},{4,2},{6,4},{8,6},{10,8},{12,10},{14,12},{1,15},{3,1}... | collective-permute-start | bytes 393224 | tf_op jit(solution)/shard_map/ppermute | solution.py:148
  63.9 0.9 collective-permute-done.7
  64.8 1.5 %collective-permute-done.8 = bf16[64,1024]{1,0:T(8,128)(2,1)S(1)} collective-permute-done((bf16[64,1024]{1,0:T(8,128)(2,1)S(1)}, bf16[64,1024]{1,0:T(8,128)(2,1)S(1)}, u32[]{:S(2)}, u32[]{:S(2)}) %collective-permute-start.8) | collective-permute-done | bytes 131104 | tf_op jit(solution)/shard_map/ppermute | solution.py:148
  66.4 1.9 %collective-permute-start.9 = (bf16[1024,1024]{1,0:T(8,128)(2,1)S(1)}, bf16[1024,1024]{1,0:T(8,128)(2,1)}, u32[]{:S(2)}, u32[]{:S(2)}) collective-permute-start(bf16[1024,1024]{1,0:T(8,128)(2,1)S(1)} %bitcast.87), channel_id=1, source_target_pairs={{0,1},{1,0},{2,3},{3,2},{4,5},{5,4},{6,7},{7,6},{8,9},{9,8},{10,11... | collective-permute-start | bytes 6291464 | tf_op jit(solution)/shard_map/ppermute | solution.py:150
  68.3 0.1 pad_add_fusion.1
  68.4 12.5 %all-to-all-done = bf16[48,24,512]{2,1,0:T(8,128)(2,1)} async-done(((bf16[48,24,512]{2,1,0:T(8,128)(2,1)}), bf16[48,24,512]{2,1,0:T(8,128)(2,1)}, u32[]{:S(2)}, u32[]{:S(2)}) %all-to-all-start) | async-done | bytes 1179680 | tf_op jit(solution)/shard_map/all_to_all | solution.py:137
  80.8 0.0 copy-done
  80.8 6.8 %first.1 = (bf16[576,1024]{1,0:T(8,128)(2,1)}, bf16[8,2,64,512]{3,2,1,0:T(8,128)(2,1)S(1)}, bf16[8,2,64,512]{3,2,1,0:T(8,128)(2,1)S(1)}, bf16[576,1024]{1,0:T(8,128)(2,1)S(1)}, bf16[16,64,576]{2,1,0:T(8,128)(2,1)S(1)}) custom-call(s32[17]{0:T(128)S(1)} %get-tuple-element.48.pos_ref, bf16[1152,512]{1,0:T(8,128)(2,1)} %bitcast.5.got_ref, ...), custom_call_target="tpu_custom_call" | custom-call | tf_op jit(solution)/shard_map/first/pallas_call | solution.py:100
  87.7 1.9 %collective-permute-start.11 = (bf16[8,2,64,512]{3,2,1,0:T(8,128)(2,1)S(1)}, bf16[8,2,64,512]{3,2,1,0:T(8,128)(2,1)S(1)}, u32[]{:S(2)}, u32[]{:S(2)}) collective-permute-start(bf16[8,2,64,512]{3,2,1,0:T(8,128)(2,1)S(1)} %get-tuple-element.22), channel_id=1, source_target_pairs={{0,1},{1,0},{2,3},{3,2},{4,5},{5,4},{6,7},{7,6},{8,9},{9,8},{10,11... | collective-permute-start | bytes 3145736 | tf_op jit(solution)/shard_map/ppermute | solution.py:158
  89.6 0.0 collective-permute-done.9.wa_ref.wb_ref
  89.6 5.4 %second.1 = (bf16[576,1024]{1,0:T(8,128)(2,1)}, bf16[8,2,64,512]{3,2,1,0:T(8,128)(2,1)S(1)}, bf16[8,2,64,512]{3,2,1,0:T(8,128)(2,1)S(1)}) custom-call(s32[17]{0:T(128)S(1)} %get-tuple-element.49.pos_ref, bf16[576,1024]{1,0:T(8,128)(2,1)S(1)} %get-tuple-element.15.normed_ref, ...), custom_call_target="tpu_custom_call", output_to_operand_aliasing={{0}: (6, {})} | custom-call | tf_op jit(solution)/shard_map/second/pallas_call | solution.py:100
  95.0 2.4 %collective-permute-start.10 = (bf16[8,2,64,512]{3,2,1,0:T(8,128)(2,1)S(1)}, bf16[8,2,64,512]{3,2,1,0:T(8,128)(2,1)S(1)}, u32[]{:S(2)}, u32[]{:S(2)}) collective-permute-start(bf16[8,2,64,512]{3,2,1,0:T(8,128)(2,1)S(1)} %get-tuple-element.20), channel_id=1, source_target_pairs={{0,1},{1,0},{2,3},{3,2},{4,5},{5,4},{6,7},{7,6},{8,9},{9,8},{10,11... | collective-permute-start | bytes 3145736 | tf_op jit(solution)/shard_map/ppermute | solution.py:160
  97.4 0.0 collective-permute-done.11
  97.4 0.1 fusion.15
  97.5 1.9 %collective-permute-start.12 = (bf16[2,64,512]{2,1,0:T(8,128)(2,1)S(1)}, bf16[2,64,512]{2,1,0:T(8,128)(2,1)S(1)}, u32[]{:S(2)}, u32[]{:S(2)}) collective-permute-start(bf16[2,64,512]{2,1,0:T(8,128)(2,1)S(1)} %get-tuple-element.30), channel_id=1, source_target_pairs={{0,2},{2,4},{4,6},{6,8},{8,10},{10,12},{12,14},{14,0},{1,3},{3,5},... | collective-permute-start | bytes 393224 | tf_op jit(solution)/shard_map/ppermute | solution.py:162
  99.4 0.3 collective-permute-done.10
  99.6 0.1 fusion.14
  99.7 4.9 %collective-permute-start.14 = (bf16[2,64,512]{2,1,0:T(8,128)(2,1)S(1)}, bf16[2,64,512]{2,1,0:T(8,128)(2,1)S(1)}, u32[]{:S(2)}, u32[]{:S(2)}) collective-permute-start(bf16[2,64,512]{2,1,0:T(8,128)(2,1)S(1)} %get-tuple-element.29), channel_id=1, source_target_pairs={{0,14},{2,0},{4,2},{6,4},{8,6},{10,8},{12,10},{14,12},{1,15},{3,1}... | collective-permute-start | bytes 393224 | tf_op jit(solution)/shard_map/ppermute | solution.py:163
  104.6 1.4 collective-permute-done.12
  106.0 0.1 fusion.9
  106.1 1.9 %collective-permute-start.13 = (bf16[4,64,512]{2,1,0:T(8,128)(2,1)S(1)}, bf16[4,64,512]{2,1,0:T(8,128)(2,1)S(1)}, u32[]{:S(2)}, u32[]{:S(2)}) collective-permute-start(bf16[4,64,512]{2,1,0:T(8,128)(2,1)S(1)} %pad_maximum_fusion.1), channel_id=1, source_target_pairs={{0,2},{2,4},{4,6},{6,8},{8,10},{10,12},{12,14},{14,0},{1,3},{3,5},... | collective-permute-start | bytes 786440 | tf_op jit(solution)/shard_map/ppermute | solution.py:176
  108.0 0.0 collective-permute-done.14
  108.0 0.1 fusion.8
  108.1 5.1 %collective-permute-start.16 = (bf16[4,64,512]{2,1,0:T(8,128)(2,1)S(1)}, bf16[4,64,512]{2,1,0:T(8,128)(2,1)S(1)}, u32[]{:S(2)}, u32[]{:S(2)}) collective-permute-start(bf16[4,64,512]{2,1,0:T(8,128)(2,1)S(1)} %pad_maximum_fusion.2), channel_id=1, source_target_pairs={{0,14},{2,0},{4,2},{6,4},{8,6},{10,8},{12,10},{14,12},{1,15},{3,1}... | collective-permute-start | bytes 786440 | tf_op jit(solution)/shard_map/ppermute | solution.py:177
  113.2 3.3 %collective-permute-done.13 = bf16[4,64,512]{2,1,0:T(8,128)(2,1)S(1)} collective-permute-done((bf16[4,64,512]{2,1,0:T(8,128)(2,1)S(1)}, bf16[4,64,512]{2,1,0:T(8,128)(2,1)S(1)}, u32[]{:S(2)}, u32[]{:S(2)}) %collective-permute-start.13) | collective-permute-done | bytes 262176 | tf_op jit(solution)/shard_map/ppermute | solution.py:176
  116.5 0.1 fusion.10
  116.7 1.9 %collective-permute-start.15 = (bf16[4,64,512]{2,1,0:T(8,128)(2,1)S(1)}, bf16[4,64,512]{2,1,0:T(8,128)(2,1)S(1)}, u32[]{:S(2)}, u32[]{:S(2)}) collective-permute-start(bf16[4,64,512]{2,1,0:T(8,128)(2,1)S(1)} %pad_maximum_fusion.3), channel_id=1, source_target_pairs={{0,2},{2,4},{4,6},{6,8},{8,10},{10,12},{12,14},{14,0},{1,3},{3,5},... | collective-permute-start | bytes 786440 | tf_op jit(solution)/shard_map/ppermute | solution.py:176
  118.6 0.0 collective-permute-done.16
  118.6 0.1 fusion.6
  118.8 5.1 %collective-permute-start.18 = (bf16[4,64,512]{2,1,0:T(8,128)(2,1)S(1)}, bf16[4,64,512]{2,1,0:T(8,128)(2,1)S(1)}, u32[]{:S(2)}, u32[]{:S(2)}) collective-permute-start(bf16[4,64,512]{2,1,0:T(8,128)(2,1)S(1)} %pad_maximum_fusion.4), channel_id=1, source_target_pairs={{0,14},{2,0},{4,2},{6,4},{8,6},{10,8},{12,10},{14,12},{1,15},{3,1}... | collective-permute-start | bytes 786440 | tf_op jit(solution)/shard_map/ppermute | solution.py:177
  123.9 2.4 %collective-permute-done.15 = bf16[4,64,512]{2,1,0:T(8,128)(2,1)S(1)} collective-permute-done((bf16[4,64,512]{2,1,0:T(8,128)(2,1)S(1)}, bf16[4,64,512]{2,1,0:T(8,128)(2,1)S(1)}, u32[]{:S(2)}, u32[]{:S(2)}) %collective-permute-start.15) | collective-permute-done | bytes 262176 | tf_op jit(solution)/shard_map/ppermute | solution.py:176
  126.3 0.1 fusion.11
  126.4 1.3 collective-permute-done.18
  127.8 0.1 fusion.3
  127.9 5.6 %collective-permute-start.19 = (bf16[4,64,512]{2,1,0:T(8,128)(2,1)S(1)}, bf16[4,64,512]{2,1,0:T(8,128)(2,1)S(1)}, u32[]{:S(2)}, u32[]{:S(2)}) collective-permute-start(bf16[4,64,512]{2,1,0:T(8,128)(2,1)S(1)} %pad_maximum_fusion.6), channel_id=1, source_target_pairs={{0,14},{2,0},{4,2},{6,4},{8,6},{10,8},{12,10},{14,12},{1,15},{3,1}... | collective-permute-start | bytes 786440 | tf_op jit(solution)/shard_map/ppermute | solution.py:177
  133.5 1.9 %collective-permute-start.17 = (bf16[4,64,512]{2,1,0:T(8,128)(2,1)S(1)}, bf16[4,64,512]{2,1,0:T(8,128)(2,1)S(1)}, u32[]{:S(2)}, u32[]{:S(2)}) collective-permute-start(bf16[4,64,512]{2,1,0:T(8,128)(2,1)S(1)} %pad_maximum_fusion.5), channel_id=1, source_target_pairs={{0,2},{2,4},{4,6},{6,8},{8,10},{10,12},{12,14},{14,0},{1,3},{3,5},... | collective-permute-start | bytes 786440 | tf_op jit(solution)/shard_map/ppermute | solution.py:176
  135.4 1.9 %collective-permute-done.19 = bf16[4,64,512]{2,1,0:T(8,128)(2,1)S(1)} collective-permute-done((bf16[4,64,512]{2,1,0:T(8,128)(2,1)S(1)}, bf16[4,64,512]{2,1,0:T(8,128)(2,1)S(1)}, u32[]{:S(2)}, u32[]{:S(2)}) %collective-permute-start.19) | collective-permute-done | bytes 262176 | tf_op jit(solution)/shard_map/ppermute | solution.py:177
  137.4 5.6 %collective-permute-done.17 = bf16[4,64,512]{2,1,0:T(8,128)(2,1)S(1)} collective-permute-done((bf16[4,64,512]{2,1,0:T(8,128)(2,1)S(1)}, bf16[4,64,512]{2,1,0:T(8,128)(2,1)S(1)}, u32[]{:S(2)}, u32[]{:S(2)}) %collective-permute-start.17) | collective-permute-done | bytes 262176 | tf_op jit(solution)/shard_map/ppermute | solution.py:176
  143.0 0.1 fusion.13
  143.2 0.8 maximum_select_fusion.1
  (23 shorter events, 0.4 us)
Async XLA Ops:
  0.6 13.1 %copy-start.2 = (s32[1,1,576]{2,1,0:T(1,128)S(1)}, s32[1,1,576]{2,1,0:T(1,128)}, u32[]{:S(2)}) copy-start(s32[1,1,576]{2,1,0:T(1,128)} %param.6) | copy-start | bytes 6916
  0.6 13.1 %copy-start.3 = (s32[1,1,576]{2,1,0:T(1,128)S(1)}, s32[1,1,576]{2,1,0:T(1,128)}, u32[]{:S(2)}) copy-start(s32[1,1,576]{2,1,0:T(1,128)} %param.7) | copy-start | bytes 6916
  0.7 13.1 %copy-start.1 = (bf16[1,1,576,1024]{3,2,1,0:T(8,128)(2,1)S(1)}, bf16[1,1,576,1024]{3,2,1,0:T(8,128)(2,1)}, u32[]{:S(2)}) copy-start(bf16[1,1,576,1024]{3,2,1,0:T(8,128)(2,1)} %param.5) | copy-start | bytes 3538948
  0.7 3.8 %collective-permute-start = (bf16[64,2048]{1,0:T(8,128)(2,1)}, bf16[64,2048]{1,0:T(8,128)(2,1)S(1)}, u32[]{:S(2)}, u32[]{:S(2)}) collective-permute-start(bf16[64,2048]{1,0:T(8,128)(2,1)} %param.8), channel_id=1, source_target_pairs={{0,1},{1,0},{2,3},{3,2},{4,5},{5,4},{6,7},{7,6},{8,9},{9,8},{10,11... | collective-permute-start | bytes 786440 | tf_op jit(solution)/shard_map/ppermute | solution.py:126
  6.4 29.5 %collective-permute-start.1 = (bf16[128,1024]{1,0:T(8,128)(2,1)}, bf16[128,1024]{1,0:T(8,128)(2,1)}, u32[]{:S(2)}, u32[]{:S(2)}) collective-permute-start(bf16[128,1024]{1,0:T(8,128)(2,1)} %pad_maximum_fusion), channel_id=1, source_target_pairs={{0,2},{2,4},{4,6},{6,8},{8,10},{10,12},{12,14},{14,0},{1,3},{3,5},... | collective-permute-start | bytes 786440 | tf_op jit(solution)/shard_map/ppermute | solution.py:144
  9.9 28.2 %collective-permute-start.2 = (bf16[128,1024]{1,0:T(8,128)(2,1)}, bf16[128,1024]{1,0:T(8,128)(2,1)S(1)}, u32[]{:S(2)}, u32[]{:S(2)}) collective-permute-start(bf16[128,1024]{1,0:T(8,128)(2,1)} %pad_maximum_fusion), channel_id=1, source_target_pairs={{0,14},{2,0},{4,2},{6,4},{8,6},{10,8},{12,10},{14,12},{1,15},{3,1}... | collective-permute-start | bytes 786440 | tf_op jit(solution)/shard_map/ppermute | solution.py:145
  17.0 63.8 %all-to-all-start = ((bf16[48,24,512]{2,1,0:T(8,128)(2,1)}), bf16[48,24,512]{2,1,0:T(8,128)(2,1)}, u32[]{:S(2)}, u32[]{:S(2)}) async-start(bf16[48,24,512]{2,1,0:T(8,128)(2,1)} %bitcast.4), calls=%async_computation | async-start | bytes 2359296 | tf_op jit(solution)/shard_map/all_to_all | solution.py:137
  35.9 44.9 %copy-start = (bf16[1,1,576,1024]{3,2,1,0:T(8,128)(2,1)S(1)}, bf16[1,1,576,1024]{3,2,1,0:T(8,128)(2,1)}, u32[]{:S(2)}) copy-start(bf16[1,1,576,1024]{3,2,1,0:T(8,128)(2,1)} %param.9) | copy-start | bytes 3538948
  35.9 10.9 %collective-permute-start.3 = (bf16[128,1024]{1,0:T(8,128)(2,1)}, bf16[128,1024]{1,0:T(8,128)(2,1)S(1)}, u32[]{:S(2)}, u32[]{:S(2)}) collective-permute-start(bf16[128,1024]{1,0:T(8,128)(2,1)} %collective-permute-done.1), channel_id=1, source_target_pairs={{0,2},{2,4},{4,6},{6,8},{8,10},{10,12},{12,14},{14,0},{1,3},{3,5},... | collective-permute-start | bytes 786440 | tf_op jit(solution)/shard_map/ppermute | solution.py:144
  38.1 10.7 %collective-permute-start.4 = (bf16[128,1024]{1,0:T(8,128)(2,1)S(1)}, bf16[128,1024]{1,0:T(8,128)(2,1)S(1)}, u32[]{:S(2)}, u32[]{:S(2)}) collective-permute-start(bf16[128,1024]{1,0:T(8,128)(2,1)S(1)} %collective-permute-done.2), channel_id=1, source_target_pairs={{0,14},{2,0},{4,2},{6,4},{8,6},{10,8},{12,10},{14,12},{1,15},{3,1}... | collective-permute-start | bytes 786440 | tf_op jit(solution)/shard_map/ppermute | solution.py:145
  46.9 9.8 %collective-permute-start.5 = (bf16[128,1024]{1,0:T(8,128)(2,1)S(1)}, bf16[128,1024]{1,0:T(8,128)(2,1)S(1)}, u32[]{:S(2)}, u32[]{:S(2)}) collective-permute-start(bf16[128,1024]{1,0:T(8,128)(2,1)S(1)} %collective-permute-done.3), channel_id=1, source_target_pairs={{0,2},{2,4},{4,6},{6,8},{8,10},{10,12},{12,14},{14,0},{1,3},{3,5},... | collective-permute-start | bytes 786440 | tf_op jit(solution)/shard_map/ppermute | solution.py:144
  48.8 9.9 %collective-permute-start.6 = (bf16[128,1024]{1,0:T(8,128)(2,1)S(1)}, bf16[128,1024]{1,0:T(8,128)(2,1)S(1)}, u32[]{:S(2)}, u32[]{:S(2)}) collective-permute-start(bf16[128,1024]{1,0:T(8,128)(2,1)S(1)} %collective-permute-done.4), channel_id=1, source_target_pairs={{0,14},{2,0},{4,2},{6,4},{8,6},{10,8},{12,10},{14,12},{1,15},{3,1}... | collective-permute-start | bytes 786440 | tf_op jit(solution)/shard_map/ppermute | solution.py:145
  56.7 8.1 %collective-permute-start.7 = (bf16[64,1024]{1,0:T(8,128)(2,1)S(1)}, bf16[64,1024]{1,0:T(8,128)(2,1)S(1)}, u32[]{:S(2)}, u32[]{:S(2)}) collective-permute-start(bf16[64,1024]{1,0:T(8,128)(2,1)S(1)} %slice.204), channel_id=1, source_target_pairs={{0,2},{2,4},{4,6},{6,8},{8,10},{10,12},{12,14},{14,0},{1,3},{3,5},... | collective-permute-start | bytes 393224 | tf_op jit(solution)/shard_map/ppermute | solution.py:147
  58.7 7.6 %collective-permute-start.8 = (bf16[64,1024]{1,0:T(8,128)(2,1)S(1)}, bf16[64,1024]{1,0:T(8,128)(2,1)S(1)}, u32[]{:S(2)}, u32[]{:S(2)}) collective-permute-start(bf16[64,1024]{1,0:T(8,128)(2,1)S(1)} %slice.205), channel_id=1, source_target_pairs={{0,14},{2,0},{4,2},{6,4},{8,6},{10,8},{12,10},{14,12},{1,15},{3,1}... | collective-permute-start | bytes 393224 | tf_op jit(solution)/shard_map/ppermute | solution.py:148
  66.4 23.2 %collective-permute-start.9 = (bf16[1024,1024]{1,0:T(8,128)(2,1)S(1)}, bf16[1024,1024]{1,0:T(8,128)(2,1)}, u32[]{:S(2)}, u32[]{:S(2)}) collective-permute-start(bf16[1024,1024]{1,0:T(8,128)(2,1)S(1)} %bitcast.87), channel_id=1, source_target_pairs={{0,1},{1,0},{2,3},{3,2},{4,5},{5,4},{6,7},{7,6},{8,9},{9,8},{10,11... | collective-permute-start | bytes 6291464 | tf_op jit(solution)/shard_map/ppermute | solution.py:150
  87.7 9.7 %collective-permute-start.11 = (bf16[8,2,64,512]{3,2,1,0:T(8,128)(2,1)S(1)}, bf16[8,2,64,512]{3,2,1,0:T(8,128)(2,1)S(1)}, u32[]{:S(2)}, u32[]{:S(2)}) collective-permute-start(bf16[8,2,64,512]{3,2,1,0:T(8,128)(2,1)S(1)} %get-tuple-element.22), channel_id=1, source_target_pairs={{0,1},{1,0},{2,3},{3,2},{4,5},{5,4},{6,7},{7,6},{8,9},{9,8},{10,11... | collective-permute-start | bytes 3145736 | tf_op jit(solution)/shard_map/ppermute | solution.py:158
  95.0 4.7 %collective-permute-start.10 = (bf16[8,2,64,512]{3,2,1,0:T(8,128)(2,1)S(1)}, bf16[8,2,64,512]{3,2,1,0:T(8,128)(2,1)S(1)}, u32[]{:S(2)}, u32[]{:S(2)}) collective-permute-start(bf16[8,2,64,512]{3,2,1,0:T(8,128)(2,1)S(1)} %get-tuple-element.20), channel_id=1, source_target_pairs={{0,1},{1,0},{2,3},{3,2},{4,5},{5,4},{6,7},{7,6},{8,9},{9,8},{10,11... | collective-permute-start | bytes 3145736 | tf_op jit(solution)/shard_map/ppermute | solution.py:160
  97.5 8.5 %collective-permute-start.12 = (bf16[2,64,512]{2,1,0:T(8,128)(2,1)S(1)}, bf16[2,64,512]{2,1,0:T(8,128)(2,1)S(1)}, u32[]{:S(2)}, u32[]{:S(2)}) collective-permute-start(bf16[2,64,512]{2,1,0:T(8,128)(2,1)S(1)} %get-tuple-element.30), channel_id=1, source_target_pairs={{0,2},{2,4},{4,6},{6,8},{8,10},{10,12},{12,14},{14,0},{1,3},{3,5},... | collective-permute-start | bytes 393224 | tf_op jit(solution)/shard_map/ppermute | solution.py:162
  99.7 8.3 %collective-permute-start.14 = (bf16[2,64,512]{2,1,0:T(8,128)(2,1)S(1)}, bf16[2,64,512]{2,1,0:T(8,128)(2,1)S(1)}, u32[]{:S(2)}, u32[]{:S(2)}) collective-permute-start(bf16[2,64,512]{2,1,0:T(8,128)(2,1)S(1)} %get-tuple-element.29), channel_id=1, source_target_pairs={{0,14},{2,0},{4,2},{6,4},{8,6},{10,8},{12,10},{14,12},{1,15},{3,1}... | collective-permute-start | bytes 393224 | tf_op jit(solution)/shard_map/ppermute | solution.py:163
  106.1 10.5 %collective-permute-start.13 = (bf16[4,64,512]{2,1,0:T(8,128)(2,1)S(1)}, bf16[4,64,512]{2,1,0:T(8,128)(2,1)S(1)}, u32[]{:S(2)}, u32[]{:S(2)}) collective-permute-start(bf16[4,64,512]{2,1,0:T(8,128)(2,1)S(1)} %pad_maximum_fusion.1), channel_id=1, source_target_pairs={{0,2},{2,4},{4,6},{6,8},{8,10},{10,12},{12,14},{14,0},{1,3},{3,5},... | collective-permute-start | bytes 786440 | tf_op jit(solution)/shard_map/ppermute | solution.py:176
  108.1 10.5 %collective-permute-start.16 = (bf16[4,64,512]{2,1,0:T(8,128)(2,1)S(1)}, bf16[4,64,512]{2,1,0:T(8,128)(2,1)S(1)}, u32[]{:S(2)}, u32[]{:S(2)}) collective-permute-start(bf16[4,64,512]{2,1,0:T(8,128)(2,1)S(1)} %pad_maximum_fusion.2), channel_id=1, source_target_pairs={{0,14},{2,0},{4,2},{6,4},{8,6},{10,8},{12,10},{14,12},{1,15},{3,1}... | collective-permute-start | bytes 786440 | tf_op jit(solution)/shard_map/ppermute | solution.py:177
  116.7 9.6 %collective-permute-start.15 = (bf16[4,64,512]{2,1,0:T(8,128)(2,1)S(1)}, bf16[4,64,512]{2,1,0:T(8,128)(2,1)S(1)}, u32[]{:S(2)}, u32[]{:S(2)}) collective-permute-start(bf16[4,64,512]{2,1,0:T(8,128)(2,1)S(1)} %pad_maximum_fusion.3), channel_id=1, source_target_pairs={{0,2},{2,4},{4,6},{6,8},{8,10},{10,12},{12,14},{14,0},{1,3},{3,5},... | collective-permute-start | bytes 786440 | tf_op jit(solution)/shard_map/ppermute | solution.py:176
  118.8 9.0 %collective-permute-start.18 = (bf16[4,64,512]{2,1,0:T(8,128)(2,1)S(1)}, bf16[4,64,512]{2,1,0:T(8,128)(2,1)S(1)}, u32[]{:S(2)}, u32[]{:S(2)}) collective-permute-start(bf16[4,64,512]{2,1,0:T(8,128)(2,1)S(1)} %pad_maximum_fusion.4), channel_id=1, source_target_pairs={{0,14},{2,0},{4,2},{6,4},{8,6},{10,8},{12,10},{14,12},{1,15},{3,1}... | collective-permute-start | bytes 786440 | tf_op jit(solution)/shard_map/ppermute | solution.py:177
  127.9 9.5 %collective-permute-start.19 = (bf16[4,64,512]{2,1,0:T(8,128)(2,1)S(1)}, bf16[4,64,512]{2,1,0:T(8,128)(2,1)S(1)}, u32[]{:S(2)}, u32[]{:S(2)}) collective-permute-start(bf16[4,64,512]{2,1,0:T(8,128)(2,1)S(1)} %pad_maximum_fusion.6), channel_id=1, source_target_pairs={{0,14},{2,0},{4,2},{6,4},{8,6},{10,8},{12,10},{14,12},{1,15},{3,1}... | collective-permute-start | bytes 786440 | tf_op jit(solution)/shard_map/ppermute | solution.py:177
  133.5 9.5 %collective-permute-start.17 = (bf16[4,64,512]{2,1,0:T(8,128)(2,1)S(1)}, bf16[4,64,512]{2,1,0:T(8,128)(2,1)S(1)}, u32[]{:S(2)}, u32[]{:S(2)}) collective-permute-start(bf16[4,64,512]{2,1,0:T(8,128)(2,1)S(1)} %pad_maximum_fusion.5), channel_id=1, source_target_pairs={{0,2},{2,4},{4,6},{6,8},{8,10},{10,12},{12,14},{14,0},{1,3},{3,5},... | collective-permute-start | bytes 786440 | tf_op jit(solution)/shard_map/ppermute | solution.py:176

commit v3 on v2

v3 whole, which is shorter than its diff:
```python
import jax
import jax.numpy as jnp
from jax import lax
from jax.experimental import pallas as pl
from jax.experimental.pallas import tpu as pltpu
from jax.sharding import Mesh, PartitionSpec as P


BF, F32 = jnp.bfloat16, jnp.float32
COLS = 256
STEPS = 1024 // COLS


def spread(half, transposed=False):
    shape = (192, 96) if transposed else (96, 192)
    narrow = lax.broadcasted_iota(jnp.int32, shape, 1 if transposed else 0)
    wide = lax.broadcasted_iota(jnp.int32, shape, 0 if transposed else 1)
    hit = wide == narrow + (narrow // 12 + half) * 12
    return jnp.where(hit, 1.0, 0.0).astype(BF)


def pick_kernel(route_hbm, valid_hbm, frames_hbm, out_ref, route_ref, valid_ref, frames_ref, sems):
    copies = [
        pltpu.make_async_copy(src, dst, sems.at[i])
        for i, (src, dst) in enumerate(((route_hbm, route_ref), (valid_hbm, valid_ref), (frames_hbm, frames_ref)))
    ]
    for copy in copies:
        copy.start()
    rows = frames_ref.shape[0]
    lane = lax.broadcasted_iota(jnp.int32, (rows, rows), 1)
    sub = lax.broadcasted_iota(jnp.int32, (rows, rows), 0)
    copies[0].wait()
    order = jnp.sum(jnp.where(lane == sub, route_ref[...].astype(F32), 0.0), axis=1, keepdims=True)
    copies[1].wait()
    hit = (lane == order.astype(jnp.int32)) & (valid_ref[...] > 0)
    chosen = jnp.where(hit, 1.0, 0.0).astype(BF)
    copies[2].wait()
    values = jnp.dot(chosen, frames_ref[...], preferred_element_type=F32)
    mean = jnp.mean(values, axis=-1, keepdims=True)
    centred = values - mean
    variance = jnp.mean(centred * centred, axis=-1, keepdims=True)
    normed = (centred * lax.rsqrt(variance + 1e-05)).astype(BF)
    even = jnp.concatenate([normed[:, j * 128:j * 128 + 64] for j in range(8)], axis=1)
    odd = jnp.concatenate([normed[:, j * 128 + 64:j * 128 + 128] for j in range(8)], axis=1)
    low, high = spread(0, True), spread(1, True)
    for b in range(rows // 96):
        both = jnp.dot(low, even[b * 96:(b + 1) * 96], preferred_element_type=F32)
        both += jnp.dot(high, odd[b * 96:(b + 1) * 96], preferred_element_type=F32)
        out_ref[b * 192:(b + 1) * 192, :] = both.astype(BF)


def main_kernel(
    pos_ref, got_ref, own_a, own_b, mate_a, mate_b, cot_ref,
    gated_ref, keep_ref, far_ref, send_ref, normed_ref, flip_ref,
):
    @pl.when(pl.program_id(0) == 0)
    def _():
        for h in range(2):
            chosen = spread(h)
            for b in range(6):
                part = got_ref[b * 192:(b + 1) * 192, :]
                normed_ref[h, b * 96:(b + 1) * 96, :] = jnp.dot(chosen, part, preferred_element_type=F32).astype(BF)
            for j in range(4):
                turned = normed_ref[h, :, j * 128:j * 128 + 128].T
                flip_ref[pos_ref[4 * j + h]] = turned[:64]
                flip_ref[pos_ref[4 * j + 2 + h]] = turned[64:]

    core = pos_ref[16]
    own, mate = normed_ref[core], normed_ref[1 - core]
    dot = lambda u, v: jnp.dot(u, v, preferred_element_type=F32)
    first = dot(own, own_a[...]) + dot(mate, mate_a[...])
    second = jax.nn.sigmoid(dot(own, own_b[...]) + dot(mate, mate_b[...]))
    gated = first * second
    gated_ref[...] = gated.astype(BF)
    upstream = cot_ref[...].astype(F32)
    flip = flip_ref[...].reshape(1024, 576)
    da = (upstream * second).astype(BF)
    db = (upstream * gated * (1.0 - second)).astype(BF)
    for h, slope in enumerate((da, db)):
        grad = dot(flip, slope).astype(BF)
        for d in range(8):
            keep_ref[d, h] = grad[d * 64:d * 64 + 64]
            block = grad[d * 64 + 512:d * 64 + 576]
            if d == 4:
                far_ref[h] = block
            else:
                send_ref[d - (d > 4), h] = block


def main_call(pos, got, own, mate, cot):
    half = lambda shift: pl.BlockSpec((512, COLS), lambda j, p: (0, j + shift))
    wide = pl.BlockSpec((576, COLS), lambda j, p: (0, j))
    gs = pltpu.PrefetchScalarGridSpec(
        num_scalar_prefetch=1,
        grid=(STEPS,),
        in_specs=[pl.BlockSpec((1152, 512), lambda j, p: (0, 0)), half(0), half(STEPS), half(0), half(STEPS), wide],
        out_specs=[
            wide,
            pl.BlockSpec((8, 2, 64, COLS), lambda j, p: (0, 0, 0, j)),
            pl.BlockSpec((2, 64, COLS), lambda j, p: (0, 0, j)),
            pl.BlockSpec((7, 2, 64, COLS), lambda j, p: (0, 0, 0, j)),
        ],
        scratch_shapes=[pltpu.VMEM((2, 576, 512), BF), pltpu.VMEM((16, 64, 576), BF)],
    )
    return pl.pallas_call(
        main_kernel,
        grid_spec=gs,
        out_shape=[
            jax.ShapeDtypeStruct((576, 1024), BF),
            jax.ShapeDtypeStruct((8, 2, 64, 1024), BF),
            jax.ShapeDtypeStruct((2, 64, 1024), BF),
            jax.ShapeDtypeStruct((7, 2, 64, 1024), BF),
        ],
        compiler_params=pltpu.CompilerParams(vmem_limit_bytes=40 << 20),
        name="main",
    )(pos, got, own, own, mate, mate, cot)


def total(*parts):
    acc = parts[0].astype(F32)
    for part in parts[1:]:
        acc = acc + part.astype(F32)
    return acc.astype(BF)


def stay(value):
    return pltpu.with_memory_space_constraint(value, pltpu.HBM)


def after(value, other):
    return lax.optimization_barrier((value, other))[0]


def body(frames, route, valid, w_pw, cotangent):
    y, c = lax.axis_index("y"), lax.axis_index("c")
    swap = [(0, 1), (1, 0)]
    ring = lambda d: [(i, (i + d) % 8) for i in range(8)]

    def pass_on(up, down):
        up = lax.ppermute(up, "y", ring(1))
        down = lax.ppermute(down, "y", ring(-1))
        return up, down

    up, down = pass_on(w_pw, w_pw)
    anywhere = pl.BlockSpec(memory_space=pltpu.HBM)
    out = pl.pallas_call(
        pick_kernel,
        in_specs=[anywhere] * 3,
        out_shape=jax.ShapeDtypeStruct((1152, 512), BF),
        scratch_shapes=[
            pltpu.VMEM((1, 576), jnp.int32),
            pltpu.VMEM((1, 576), jnp.int32),
            pltpu.VMEM((576, 1024), BF),
            pltpu.SemaphoreType.DMA((3,)),
        ],
        compiler_params=pltpu.CompilerParams(vmem_limit_bytes=30 << 20),
        name="pick",
    )(stay(route[0]), stay(valid[0]), stay(frames[0, 0]))
    got = lax.all_to_all(out.reshape(48, 24, 512), ("z", "x"), 0, 0, tiled=True).reshape(1152, 512)

    own = jnp.zeros((8, 64, 2048), BF)
    place = lambda buf, piece, d, at=0: lax.dynamic_update_slice(buf, piece[None], ((y + d) & 7, at, 0))
    own = place(own, w_pw, 0)
    for step in range(2, 5):
        own = place(place(own, up, 1 - step), down, step - 1)
        up, down = pass_on(up if step < 4 else up[:32], down if step < 4 else down[32:])
    own = place(place(own, up, 4), down, 4, 32).reshape(512, 2048)
    mate = lax.ppermute(own, "c", swap)

    f = jnp.arange(16, dtype=jnp.int32)
    pos = ((f & 1) ^ c) * 8 + (((f >> 1) - y) & 7)
    pos = jnp.concatenate([pos, c[None]]).astype(jnp.int32)
    gated, keep, far, rest = main_call(pos, got, own, mate, stay(cotangent[0, 0]))

    far = lax.ppermute(far, "c", swap)
    rest = lax.ppermute(rest, "c", swap)
    piece = lambda d: (keep[d], rest[d - (d > 4)])
    mid = total(keep[4], far)
    up, down = pass_on(mid[0], mid[1])
    k, g = piece(3)
    up = jnp.stack([total(k[0], g[0], up), total(k[1], g[1])])
    k, g = piece(5)
    down = after(down, up)
    down = jnp.stack([total(k[0], g[0]), total(k[1], g[1], down)])
    for d in (2, 1, 0):
        sent = down
        up, down = pass_on(up, down)
        if d:
            up = total(*piece(d), after(up, sent))
            down = total(*piece(8 - d), after(down, up))
    grad = total(*piece(0), up, down)
    grad = jnp.concatenate([grad[0], grad[1]], axis=1)
    return gated[None, None], grad[None]


def solution(mesh):
    fine = Mesh(mesh.devices.reshape(12, 4, 8, 2), ("z", "x", "y", "c"))
    dp, fsdp = ("z", "x"), ("y", "c")
    in_specs = (P(dp, fsdp), P(dp, fsdp), P(dp, fsdp), P(fsdp), P(dp, fsdp))
    return jax.shard_map(body, mesh=fine, in_specs=in_specs, out_specs=(P(dp, fsdp), P(dp, fsdp)), check_vma=False)
```

time: 145 us -> 140 us (0.966)
  other arithmetic: 3.76 us -> 1.77 us
  waiting for transfers between devices: 38.2 us -> 36.4 us
    all_to_all x1, waiting for transfers between devices: 12.5 us -> 5.43 us  [body(): lax.all_to_all(out.reshape(48, 24, 512), ('z', 'x'), 0, 0, tiled=True)]
    ppermute x20 -> x19, waiting for transfers between devices: 25.8 us -> 31 us  [the longest x8 19.2 us: pass_on(): up = lax.ppermute(up, 'y', ring(1))]
    select_n x3 -> x0, other arithmetic: 1.97 us -> none  [the longest x1 1.18 us: body(): jnp.where(c == 0, jnp.concatenate([w_pw, mate]), jnp.concatenate([mate, w...]
    ppermute x20 -> x19, starting transfers between devices: 65.3 us -> 64.2 us  [the longest x8 42.6 us: pass_on(): down = lax.ppermute(down, 'y', ring(-1))]
    pallas_call x3 -> x2, Pallas kernels: 15.5 us -> 14.7 us  [the longest x1 9.96 us: main_call(): pl.pallas_call(main_kernel, grid_spec=gs, out_shape=[jax.ShapeDtypeStruct...]
  transfers between devices with their start and end apart: 21 -> 20, of which waited for: 13 -> 12; matrix products, arithmetic and copies ran while one was open for 2% -> 2% of each run, Pallas kernels for 11% -> 3%
where the time goes in v3:
time: 140 us; the launch traced here: 139 us
  starting transfers between devices  82.8 us (59%)
  waiting for transfers between devices  36.4 us (26%)
  Pallas kernels  14.7 us (10%)
  local copies, waits for them, and re-layouts  2.41 us (2%)
  other arithmetic  1.77 us (1%)
    ppermute x8, starting transfers between devices, pass_on(): down = lax.ppermute(down, 'y', ring(-1))  42.6 us
    ppermute x8, waiting for transfers between devices, pass_on(): up = lax.ppermute(up, 'y', ring(1))  19.2 us
    all_to_all x1, starting transfers between devices, body(): lax.all_to_all(out.reshape(48, 24, 512), ('z', 'x'), 0, 0, tiled=True)  18.6 us
    ppermute x8, starting transfers between devices, pass_on(): up = lax.ppermute(up, 'y', ring(1))  15.4 us
    pallas_call x1, Pallas kernels, main_call(): pl.pallas_call(main_kernel, grid_spec=gs, out_shape=[jax.ShapeDtypeStruct...  9.96 us
    ppermute x8, waiting for transfers between devices, pass_on(): down = lax.ppermute(down, 'y', ring(-1))  5.85 us
    all_to_all x1, waiting for transfers between devices, body(): lax.all_to_all(out.reshape(48, 24, 512), ('z', 'x'), 0, 0, tiled=True)  5.43 us
    pallas_call x1, Pallas kernels, body(): pl.pallas_call(pick_kernel, in_specs=[anywhere] * 3, out_shape=jax.ShapeD...  4.79 us
  transfers between devices with their start and end apart: 20, of which 12 were waited for; matrix products, arithmetic and copies ran while one was open for 2% of the time, Pallas kernels for 3%

profile of v3, /device:TPU:4, one launch (start us, length us, event | category | flops | bytes accessed | tf_op | source)
XLA Modules:
  0.0 139.2 jit_solution(5507140241522549801)
XLA Ops:
  0.6 5.4 %collective-permute-start.1 = (bf16[64,2048]{1,0:T(8,128)(2,1)}, bf16[64,2048]{1,0:T(8,128)(2,1)}, u32[]{:S(2)}, u32[]{:S(2)}) collective-permute-start(bf16[64,2048]{1,0:T(8,128)(2,1)} %param.8), channel_id=1, source_target_pairs={{0,14},{2,0},{4,2},{6,4},{8,6},{10,8},{12,10},{14,12},{1,15},{3,1}... | collective-permute-start | bytes 786440 | tf_op jit(solution)/shard_map/ppermute | solution.py:141
  6.0 1.9 %collective-permute-start = (bf16[64,2048]{1,0:T(8,128)(2,1)}, bf16[64,2048]{1,0:T(8,128)(2,1)}, u32[]{:S(2)}, u32[]{:S(2)}) collective-permute-start(bf16[64,2048]{1,0:T(8,128)(2,1)} %param.8), channel_id=1, source_target_pairs={{0,2},{2,4},{4,6},{6,8},{8,10},{10,12},{12,14},{14,0},{1,3},{3,5},... | collective-permute-start | bytes 786440 | tf_op jit(solution)/shard_map/ppermute | solution.py:140
  8.0 4.8 %pick.1 = bf16[1152,512]{1,0:T(8,128)(2,1)} custom-call(s32[1,576]{1,0:T(1,128)} %bitcast.88, s32[1,576]{1,0:T(1,128)} %bitcast.89, bf16[576,1024]{1,0:T(8,128)(2,1)} %bitcast.86), custom_call_target="tpu_custom_call" | custom-call | tf_op jit(solution)/shard_map/pick/pallas_call | solution.py:146
  12.7 0.0 copy-start
  12.8 18.6 %all-to-all-start = ((bf16[48,24,512]{2,1,0:T(8,128)(2,1)}), bf16[48,24,512]{2,1,0:T(8,128)(2,1)S(1)}, u32[]{:S(2)}, u32[]{:S(2)}) async-start(bf16[48,24,512]{2,1,0:T(8,128)(2,1)} %bitcast.4), calls=%async_computation | async-start | bytes 2359296 | tf_op jit(solution)/shard_map/all_to_all | solution.py:159
  31.4 0.2 broadcast_in_dim.40
  31.6 0.0 copy-done
  31.7 0.0 collective-permute-done.1
  31.7 5.1 %collective-permute-start.3 = (bf16[64,2048]{1,0:T(8,128)(2,1)}, bf16[64,2048]{1,0:T(8,128)(2,1)S(1)}, u32[]{:S(2)}, u32[]{:S(2)}) collective-permute-start(bf16[64,2048]{1,0:T(8,128)(2,1)} %collective-permute-done.1), channel_id=1, source_target_pairs={{0,14},{2,0},{4,2},{6,4},{8,6},{10,8},{12,10},{14,12},{1,15},{3,1}... | collective-permute-start | bytes 786440 | tf_op jit(solution)/shard_map/ppermute | solution.py:141
  36.8 0.0 collective-permute-done
  36.9 1.9 %collective-permute-start.2 = (bf16[64,2048]{1,0:T(8,128)(2,1)}, bf16[64,2048]{1,0:T(8,128)(2,1)S(1)}, u32[]{:S(2)}, u32[]{:S(2)}) collective-permute-start(bf16[64,2048]{1,0:T(8,128)(2,1)} %collective-permute-done), channel_id=1, source_target_pairs={{0,2},{2,4},{4,6},{6,8},{8,10},{10,12},{12,14},{14,0},{1,3},{3,5},... | collective-permute-start | bytes 786440 | tf_op jit(solution)/shard_map/ppermute | solution.py:140
  38.8 1.0 bitcast_dynamic-update-slice_fusion.5
  39.8 1.0 bitcast_dynamic-update-slice_fusion.4
  40.7 0.8 collective-permute-done.3
  41.6 5.5 %collective-permute-start.5 = (bf16[64,2048]{1,0:T(8,128)(2,1)S(1)}, bf16[64,2048]{1,0:T(8,128)(2,1)S(1)}, u32[]{:S(2)}, u32[]{:S(2)}) collective-permute-start(bf16[64,2048]{1,0:T(8,128)(2,1)S(1)} %collective-permute-done.3), channel_id=1, source_target_pairs={{0,14},{2,0},{4,2},{6,4},{8,6},{10,8},{12,10},{14,12},{1,15},{3,1}... | collective-permute-start | bytes 786440 | tf_op jit(solution)/shard_map/ppermute | solution.py:141
  47.1 0.0 collective-permute-done.2
  47.1 1.9 %collective-permute-start.4 = (bf16[64,2048]{1,0:T(8,128)(2,1)S(1)}, bf16[64,2048]{1,0:T(8,128)(2,1)S(1)}, u32[]{:S(2)}, u32[]{:S(2)}) collective-permute-start(bf16[64,2048]{1,0:T(8,128)(2,1)S(1)} %collective-permute-done.2), channel_id=1, source_target_pairs={{0,2},{2,4},{4,6},{6,8},{8,10},{10,12},{12,14},{14,0},{1,3},{3,5},... | collective-permute-start | bytes 786440 | tf_op jit(solution)/shard_map/ppermute | solution.py:140
  49.1 1.9 %collective-permute-done.5 = bf16[64,2048]{1,0:T(8,128)(2,1)S(1)} collective-permute-done((bf16[64,2048]{1,0:T(8,128)(2,1)S(1)}, bf16[64,2048]{1,0:T(8,128)(2,1)S(1)}, u32[]{:S(2)}, u32[]{:S(2)}) %collective-permute-start.5) | collective-permute-done | bytes 262176 | tf_op jit(solution)/shard_map/ppermute | solution.py:141
  50.9 5.6 %collective-permute-start.7 = (bf16[32,2048]{1,0:T(8,128)(2,1)S(1)}, bf16[32,2048]{1,0:T(8,128)(2,1)S(1)}, u32[]{:S(2)}, u32[]{:S(2)}) collective-permute-start(bf16[32,2048]{1,0:T(8,128)(2,1)S(1)} %slice.121), channel_id=1, source_target_pairs={{0,14},{2,0},{4,2},{6,4},{8,6},{10,8},{12,10},{14,12},{1,15},{3,1}... | collective-permute-start | bytes 393224 | tf_op jit(solution)/shard_map/ppermute | solution.py:141
  56.6 0.0 collective-permute-done.4
  56.6 1.9 %collective-permute-start.6 = (bf16[32,2048]{1,0:T(8,128)(2,1)S(1)}, bf16[32,2048]{1,0:T(8,128)(2,1)S(1)}, u32[]{:S(2)}, u32[]{:S(2)}) collective-permute-start(bf16[32,2048]{1,0:T(8,128)(2,1)S(1)} %slice.120), channel_id=1, source_target_pairs={{0,2},{2,4},{4,6},{6,8},{8,10},{10,12},{12,14},{14,0},{1,3},{3,5},... | collective-permute-start | bytes 393224 | tf_op jit(solution)/shard_map/ppermute | solution.py:140
  58.6 6.1 %collective-permute-done.6 = bf16[32,2048]{1,0:T(8,128)(2,1)S(1)} collective-permute-done((bf16[32,2048]{1,0:T(8,128)(2,1)S(1)}, bf16[32,2048]{1,0:T(8,128)(2,1)S(1)}, u32[]{:S(2)}, u32[]{:S(2)}) %collective-permute-start.6) | collective-permute-done | bytes 131104 | tf_op jit(solution)/shard_map/ppermute | solution.py:140
  64.7 0.0 collective-permute-done.7
  64.7 1.9 %collective-permute-start.8 = (bf16[512,2048]{1,0:T(8,128)(2,1)S(1)}, bf16[512,2048]{1,0:T(8,128)(2,1)}, u32[]{:S(2)}, u32[]{:S(2)}) collective-permute-start(bf16[512,2048]{1,0:T(8,128)(2,1)S(1)} %bitcast.82), channel_id=1, source_target_pairs={{0,1},{1,0},{2,3},{3,2},{4,5},{5,4},{6,7},{7,6},{8,9},{9,8},{10,11... | collective-permute-start | bytes 6291464 | tf_op jit(solution)/shard_map/ppermute | solution.py:168
  66.6 0.1 pad_add_fusion.pos_ref
  66.7 4.2 %collective-permute-done.8.mate_a.mate_b = bf16[512,2048]{1,0:T(8,128)(2,1)} collective-permute-done((bf16[512,2048]{1,0:T(8,128)(2,1)S(1)}, bf16[512,2048]{1,0:T(8,128)(2,1)}, u32[]{:S(2)}, u32[]{:S(2)}) %collective-permute-start.8) | collective-permute-done | bytes 2097184 | tf_op jit(solution)/shard_map/ppermute | solution.py:168
  70.9 5.4 %all-to-all-done = bf16[48,24,512]{2,1,0:T(8,128)(2,1)S(1)} async-done(((bf16[48,24,512]{2,1,0:T(8,128)(2,1)}), bf16[48,24,512]{2,1,0:T(8,128)(2,1)S(1)}, u32[]{:S(2)}, u32[]{:S(2)}) %all-to-all-start) | async-done | bytes 1179680 | tf_op jit(solution)/shard_map/all_to_all | solution.py:159
  76.3 10.0 %main.1 = (bf16[576,1024]{1,0:T(8,128)(2,1)}, bf16[8,2,64,1024]{3,2,1,0:T(8,128)(2,1)S(1)}, bf16[2,64,1024]{2,1,0:T(8,128)(2,1)S(1)}, bf16[7,2,64,1024]{3,2,1,0:T(8,128)(2,1)S(1)}) custom-call(s32[17]{0:T(128)S(1)} %pad_add_fusion.pos_ref, bf16[1152,512]{1,0:T(8,128)(2,1)S(1)} %bitcast.85, bf16[512,2048]{1,0:T(8,128)(2,1)S(1)} %bitcast.83, ...), custom_call_target="tpu_custom_call" | custom-call | tf_op jit(solution)/shard_map/main/pallas_call | solution.py:105
  86.3 1.9 %collective-permute-start.9 = (bf16[7,2,64,1024]{3,2,1,0:T(8,128)(2,1)S(1)}, bf16[7,2,64,1024]{3,2,1,0:T(8,128)(2,1)S(1)}, u32[]{:S(2)}, u32[]{:S(2)}) collective-permute-start(bf16[7,2,64,1024]{3,2,1,0:T(8,128)(2,1)S(1)} %get-tuple-element.13), channel_id=1, source_target_pairs={{0,1},{1,0},{2,3},{3,2},{4,5},{5,4},{6,7},{7,6},{8,9},{9,8},{10,11... | collective-permute-start | bytes 5505032 | tf_op jit(solution)/shard_map/ppermute | solution.py:176
  88.2 2.4 %collective-permute-start.10 = (bf16[2,64,1024]{2,1,0:T(8,128)(2,1)S(1)}, bf16[2,64,1024]{2,1,0:T(8,128)(2,1)S(1)}, u32[]{:S(2)}, u32[]{:S(2)}) collective-permute-start(bf16[2,64,1024]{2,1,0:T(8,128)(2,1)S(1)} %get-tuple-element.14), channel_id=1, source_target_pairs={{0,1},{1,0},{2,3},{3,2},{4,5},{5,4},{6,7},{7,6},{8,9},{9,8},{10,11... | collective-permute-start | bytes 786440 | tf_op jit(solution)/shard_map/ppermute | solution.py:175
  90.6 1.7 %collective-permute-done.10 = bf16[2,64,1024]{2,1,0:T(8,128)(2,1)S(1)} collective-permute-done((bf16[2,64,1024]{2,1,0:T(8,128)(2,1)S(1)}, bf16[2,64,1024]{2,1,0:T(8,128)(2,1)S(1)}, u32[]{:S(2)}, u32[]{:S(2)}) %collective-permute-start.10) | collective-permute-done | bytes 262176 | tf_op jit(solution)/shard_map/ppermute | solution.py:175
  92.3 0.1 fusion
  92.4 1.9 %collective-permute-start.11 = (bf16[64,1024]{1,0:T(8,128)(2,1)S(1)}, bf16[64,1024]{1,0:T(8,128)(2,1)S(1)}, u32[]{:S(2)}, u32[]{:S(2)}) collective-permute-start(bf16[64,1024]{1,0:T(8,128)(2,1)S(1)} %get-tuple-element.24), channel_id=1, source_target_pairs={{0,2},{2,4},{4,6},{6,8},{8,10},{10,12},{12,14},{14,0},{1,3},{3,5},... | collective-permute-start | bytes 393224 | tf_op jit(solution)/shard_map/ppermute | solution.py:140
  94.4 5.1 %collective-permute-start.13 = (bf16[64,1024]{1,0:T(8,128)(2,1)S(1)}, bf16[64,1024]{1,0:T(8,128)(2,1)S(1)}, u32[]{:S(2)}, u32[]{:S(2)}) collective-permute-start(bf16[64,1024]{1,0:T(8,128)(2,1)S(1)} %get-tuple-element.25), channel_id=1, source_target_pairs={{0,14},{2,0},{4,2},{6,4},{8,6},{10,8},{12,10},{14,12},{1,15},{3,1}... | collective-permute-start | bytes 393224 | tf_op jit(solution)/shard_map/ppermute | solution.py:141
  99.5 1.6 %collective-permute-done.11 = bf16[64,1024]{1,0:T(8,128)(2,1)S(1)} collective-permute-done((bf16[64,1024]{1,0:T(8,128)(2,1)S(1)}, bf16[64,1024]{1,0:T(8,128)(2,1)S(1)}, u32[]{:S(2)}, u32[]{:S(2)}) %collective-permute-start.11) | collective-permute-done | bytes 131104 | tf_op jit(solution)/shard_map/ppermute | solution.py:140
  101.1 0.0 collective-permute-done.9
  101.1 0.1 fusion.11
  101.2 0.1 fusion.10
  101.3 1.9 %collective-permute-start.12 = (bf16[2,64,1024]{2,1,0:T(8,128)(2,1)S(1)}, bf16[2,64,1024]{2,1,0:T(8,128)(2,1)S(1)}, u32[]{:S(2)}, u32[]{:S(2)}) collective-permute-start(bf16[2,64,1024]{2,1,0:T(8,128)(2,1)S(1)} %pad_maximum_fusion), channel_id=1, source_target_pairs={{0,2},{2,4},{4,6},{6,8},{8,10},{10,12},{12,14},{14,0},{1,3},{3,5},... | collective-permute-start | bytes 786440 | tf_op jit(solution)/shard_map/ppermute | solution.py:140
  103.2 0.0 collective-permute-done.13
  103.2 0.1 fusion.12
  103.3 5.1 %collective-permute-start.15 = (bf16[2,64,1024]{2,1,0:T(8,128)(2,1)S(1)}, bf16[2,64,1024]{2,1,0:T(8,128)(2,1)S(1)}, u32[]{:S(2)}, u32[]{:S(2)}) collective-permute-start(bf16[2,64,1024]{2,1,0:T(8,128)(2,1)S(1)} %pad_maximum_fusion.1), channel_id=1, source_target_pairs={{0,14},{2,0},{4,2},{6,4},{8,6},{10,8},{12,10},{14,12},{1,15},{3,1}... | collective-permute-start | bytes 786440 | tf_op jit(solution)/shard_map/ppermute | solution.py:141
  108.4 3.4 %collective-permute-done.12 = bf16[2,64,1024]{2,1,0:T(8,128)(2,1)S(1)} collective-permute-done((bf16[2,64,1024]{2,1,0:T(8,128)(2,1)S(1)}, bf16[2,64,1024]{2,1,0:T(8,128)(2,1)S(1)}, u32[]{:S(2)}, u32[]{:S(2)}) %collective-permute-start.12) | collective-permute-done | bytes 262176 | tf_op jit(solution)/shard_map/ppermute | solution.py:140
  111.9 0.1 fusion.3
  112.0 1.9 %collective-permute-start.14 = (bf16[2,64,1024]{2,1,0:T(8,128)(2,1)S(1)}, bf16[2,64,1024]{2,1,0:T(8,128)(2,1)S(1)}, u32[]{:S(2)}, u32[]{:S(2)}) collective-permute-start(bf16[2,64,1024]{2,1,0:T(8,128)(2,1)S(1)} %fusion.3), channel_id=1, source_target_pairs={{0,2},{2,4},{4,6},{6,8},{8,10},{10,12},{12,14},{14,0},{1,3},{3,5},... | collective-permute-start | bytes 786440 | tf_op jit(solution)/shard_map/ppermute | solution.py:140
  113.9 0.0 collective-permute-done.15
  113.9 0.1 fusion.2
  114.1 5.1 %collective-permute-start.17 = (bf16[2,64,1024]{2,1,0:T(8,128)(2,1)S(1)}, bf16[2,64,1024]{2,1,0:T(8,128)(2,1)S(1)}, u32[]{:S(2)}, u32[]{:S(2)}) collective-permute-start(bf16[2,64,1024]{2,1,0:T(8,128)(2,1)S(1)} %fusion.2), channel_id=1, source_target_pairs={{0,14},{2,0},{4,2},{6,4},{8,6},{10,8},{12,10},{14,12},{1,15},{3,1}... | collective-permute-start | bytes 786440 | tf_op jit(solution)/shard_map/ppermute | solution.py:141
  119.2 2.5 %collective-permute-done.14 = bf16[2,64,1024]{2,1,0:T(8,128)(2,1)S(1)} collective-permute-done((bf16[2,64,1024]{2,1,0:T(8,128)(2,1)S(1)}, bf16[2,64,1024]{2,1,0:T(8,128)(2,1)S(1)}, u32[]{:S(2)}, u32[]{:S(2)}) %collective-permute-start.14) | collective-permute-done | bytes 262176 | tf_op jit(solution)/shard_map/ppermute | solution.py:140
  121.7 0.1 fusion.4
  121.9 1.2 collective-permute-done.17
  123.1 0.1 fusion.1
  123.2 5.6 %collective-permute-start.18 = (bf16[2,64,1024]{2,1,0:T(8,128)(2,1)S(1)}, bf16[2,64,1024]{2,1,0:T(8,128)(2,1)S(1)}, u32[]{:S(2)}, u32[]{:S(2)}) collective-permute-start(bf16[2,64,1024]{2,1,0:T(8,128)(2,1)S(1)} %fusion.1), channel_id=1, source_target_pairs={{0,14},{2,0},{4,2},{6,4},{8,6},{10,8},{12,10},{14,12},{1,15},{3,1}... | collective-permute-start | bytes 786440 | tf_op jit(solution)/shard_map/ppermute | solution.py:141
  128.8 1.9 %collective-permute-start.16 = (bf16[2,64,1024]{2,1,0:T(8,128)(2,1)S(1)}, bf16[2,64,1024]{2,1,0:T(8,128)(2,1)S(1)}, u32[]{:S(2)}, u32[]{:S(2)}) collective-permute-start(bf16[2,64,1024]{2,1,0:T(8,128)(2,1)S(1)} %fusion.4), channel_id=1, source_target_pairs={{0,2},{2,4},{4,6},{6,8},{8,10},{10,12},{12,14},{14,0},{1,3},{3,5},... | collective-permute-start | bytes 786440 | tf_op jit(solution)/shard_map/ppermute | solution.py:140
  130.7 1.9 %collective-permute-done.18 = bf16[2,64,1024]{2,1,0:T(8,128)(2,1)S(1)} collective-permute-done((bf16[2,64,1024]{2,1,0:T(8,128)(2,1)S(1)}, bf16[2,64,1024]{2,1,0:T(8,128)(2,1)S(1)}, u32[]{:S(2)}, u32[]{:S(2)}) %collective-permute-start.18) | collective-permute-done | bytes 262176 | tf_op jit(solution)/shard_map/ppermute | solution.py:141
  132.7 5.6 %collective-permute-done.16 = bf16[2,64,1024]{2,1,0:T(8,128)(2,1)S(1)} collective-permute-done((bf16[2,64,1024]{2,1,0:T(8,128)(2,1)S(1)}, bf16[2,64,1024]{2,1,0:T(8,128)(2,1)S(1)}, u32[]{:S(2)}, u32[]{:S(2)}) %collective-permute-start.16) | collective-permute-done | bytes 262176 | tf_op jit(solution)/shard_map/ppermute | solution.py:140
  138.3 0.2 fusion.6
  138.5 0.7 maximum_bitcast_fusion
  (14 shorter events, 0.3 us)
Async XLA Ops:
  0.6 31.1 %collective-permute-start.1 = (bf16[64,2048]{1,0:T(8,128)(2,1)}, bf16[64,2048]{1,0:T(8,128)(2,1)}, u32[]{:S(2)}, u32[]{:S(2)}) collective-permute-start(bf16[64,2048]{1,0:T(8,128)(2,1)} %param.8), channel_id=1, source_target_pairs={{0,14},{2,0},{4,2},{6,4},{8,6},{10,8},{12,10},{14,12},{1,15},{3,1}... | collective-permute-start | bytes 786440 | tf_op jit(solution)/shard_map/ppermute | solution.py:141
  6.0 30.8 %collective-permute-start = (bf16[64,2048]{1,0:T(8,128)(2,1)}, bf16[64,2048]{1,0:T(8,128)(2,1)}, u32[]{:S(2)}, u32[]{:S(2)}) collective-permute-start(bf16[64,2048]{1,0:T(8,128)(2,1)} %param.8), channel_id=1, source_target_pairs={{0,2},{2,4},{4,6},{6,8},{8,10},{10,12},{12,14},{14,0},{1,3},{3,5},... | collective-permute-start | bytes 786440 | tf_op jit(solution)/shard_map/ppermute | solution.py:140
  12.7 18.9 %copy-start = (bf16[64,2048]{1,0:T(8,128)(2,1)S(1)}, bf16[64,2048]{1,0:T(8,128)(2,1)}, u32[]{:S(2)}) copy-start(bf16[64,2048]{1,0:T(8,128)(2,1)} %param.8) | copy-start | bytes 786436
  12.8 63.6 %all-to-all-start = ((bf16[48,24,512]{2,1,0:T(8,128)(2,1)}), bf16[48,24,512]{2,1,0:T(8,128)(2,1)S(1)}, u32[]{:S(2)}, u32[]{:S(2)}) async-start(bf16[48,24,512]{2,1,0:T(8,128)(2,1)} %bitcast.4), calls=%async_computation | async-start | bytes 2359296 | tf_op jit(solution)/shard_map/all_to_all | solution.py:159
  31.7 9.9 %collective-permute-start.3 = (bf16[64,2048]{1,0:T(8,128)(2,1)}, bf16[64,2048]{1,0:T(8,128)(2,1)S(1)}, u32[]{:S(2)}, u32[]{:S(2)}) collective-permute-start(bf16[64,2048]{1,0:T(8,128)(2,1)} %collective-permute-done.1), channel_id=1, source_target_pairs={{0,14},{2,0},{4,2},{6,4},{8,6},{10,8},{12,10},{14,12},{1,15},{3,1}... | collective-permute-start | bytes 786440 | tf_op jit(solution)/shard_map/ppermute | solution.py:141
  36.9 10.2 %collective-permute-start.2 = (bf16[64,2048]{1,0:T(8,128)(2,1)}, bf16[64,2048]{1,0:T(8,128)(2,1)S(1)}, u32[]{:S(2)}, u32[]{:S(2)}) collective-permute-start(bf16[64,2048]{1,0:T(8,128)(2,1)} %collective-permute-done), channel_id=1, source_target_pairs={{0,2},{2,4},{4,6},{6,8},{8,10},{10,12},{12,14},{14,0},{1,3},{3,5},... | collective-permute-start | bytes 786440 | tf_op jit(solution)/shard_map/ppermute | solution.py:140
  41.6 9.4 %collective-permute-start.5 = (bf16[64,2048]{1,0:T(8,128)(2,1)S(1)}, bf16[64,2048]{1,0:T(8,128)(2,1)S(1)}, u32[]{:S(2)}, u32[]{:S(2)}) collective-permute-start(bf16[64,2048]{1,0:T(8,128)(2,1)S(1)} %collective-permute-done.3), channel_id=1, source_target_pairs={{0,14},{2,0},{4,2},{6,4},{8,6},{10,8},{12,10},{14,12},{1,15},{3,1}... | collective-permute-start | bytes 786440 | tf_op jit(solution)/shard_map/ppermute | solution.py:141
  47.1 9.5 %collective-permute-start.4 = (bf16[64,2048]{1,0:T(8,128)(2,1)S(1)}, bf16[64,2048]{1,0:T(8,128)(2,1)S(1)}, u32[]{:S(2)}, u32[]{:S(2)}) collective-permute-start(bf16[64,2048]{1,0:T(8,128)(2,1)S(1)} %collective-permute-done.2), channel_id=1, source_target_pairs={{0,2},{2,4},{4,6},{6,8},{8,10},{10,12},{12,14},{14,0},{1,3},{3,5},... | collective-permute-start | bytes 786440 | tf_op jit(solution)/shard_map/ppermute | solution.py:140
  50.9 13.7 %collective-permute-start.7 = (bf16[32,2048]{1,0:T(8,128)(2,1)S(1)}, bf16[32,2048]{1,0:T(8,128)(2,1)S(1)}, u32[]{:S(2)}, u32[]{:S(2)}) collective-permute-start(bf16[32,2048]{1,0:T(8,128)(2,1)S(1)} %slice.121), channel_id=1, source_target_pairs={{0,14},{2,0},{4,2},{6,4},{8,6},{10,8},{12,10},{14,12},{1,15},{3,1}... | collective-permute-start | bytes 393224 | tf_op jit(solution)/shard_map/ppermute | solution.py:141
  56.6 8.1 %collective-permute-start.6 = (bf16[32,2048]{1,0:T(8,128)(2,1)S(1)}, bf16[32,2048]{1,0:T(8,128)(2,1)S(1)}, u32[]{:S(2)}, u32[]{:S(2)}) collective-permute-start(bf16[32,2048]{1,0:T(8,128)(2,1)S(1)} %slice.120), channel_id=1, source_target_pairs={{0,2},{2,4},{4,6},{6,8},{8,10},{10,12},{12,14},{14,0},{1,3},{3,5},... | collective-permute-start | bytes 393224 | tf_op jit(solution)/shard_map/ppermute | solution.py:140
  64.7 6.2 %collective-permute-start.8 = (bf16[512,2048]{1,0:T(8,128)(2,1)S(1)}, bf16[512,2048]{1,0:T(8,128)(2,1)}, u32[]{:S(2)}, u32[]{:S(2)}) collective-permute-start(bf16[512,2048]{1,0:T(8,128)(2,1)S(1)} %bitcast.82), channel_id=1, source_target_pairs={{0,1},{1,0},{2,3},{3,2},{4,5},{5,4},{6,7},{7,6},{8,9},{9,8},{10,11... | collective-permute-start | bytes 6291464 | tf_op jit(solution)/shard_map/ppermute | solution.py:168
  86.3 14.8 %collective-permute-start.9 = (bf16[7,2,64,1024]{3,2,1,0:T(8,128)(2,1)S(1)}, bf16[7,2,64,1024]{3,2,1,0:T(8,128)(2,1)S(1)}, u32[]{:S(2)}, u32[]{:S(2)}) collective-permute-start(bf16[7,2,64,1024]{3,2,1,0:T(8,128)(2,1)S(1)} %get-tuple-element.13), channel_id=1, source_target_pairs={{0,1},{1,0},{2,3},{3,2},{4,5},{5,4},{6,7},{7,6},{8,9},{9,8},{10,11... | collective-permute-start | bytes 5505032 | tf_op jit(solution)/shard_map/ppermute | solution.py:176
  88.2 4.1 %collective-permute-start.10 = (bf16[2,64,1024]{2,1,0:T(8,128)(2,1)S(1)}, bf16[2,64,1024]{2,1,0:T(8,128)(2,1)S(1)}, u32[]{:S(2)}, u32[]{:S(2)}) collective-permute-start(bf16[2,64,1024]{2,1,0:T(8,128)(2,1)S(1)} %get-tuple-element.14), channel_id=1, source_target_pairs={{0,1},{1,0},{2,3},{3,2},{4,5},{5,4},{6,7},{7,6},{8,9},{9,8},{10,11... | collective-permute-start | bytes 786440 | tf_op jit(solution)/shard_map/ppermute | solution.py:175
  92.4 8.6 %collective-permute-start.11 = (bf16[64,1024]{1,0:T(8,128)(2,1)S(1)}, bf16[64,1024]{1,0:T(8,128)(2,1)S(1)}, u32[]{:S(2)}, u32[]{:S(2)}) collective-permute-start(bf16[64,1024]{1,0:T(8,128)(2,1)S(1)} %get-tuple-element.24), channel_id=1, source_target_pairs={{0,2},{2,4},{4,6},{6,8},{8,10},{10,12},{12,14},{14,0},{1,3},{3,5},... | collective-permute-start | bytes 393224 | tf_op jit(solution)/shard_map/ppermute | solution.py:140
  94.4 8.8 %collective-permute-start.13 = (bf16[64,1024]{1,0:T(8,128)(2,1)S(1)}, bf16[64,1024]{1,0:T(8,128)(2,1)S(1)}, u32[]{:S(2)}, u32[]{:S(2)}) collective-permute-start(bf16[64,1024]{1,0:T(8,128)(2,1)S(1)} %get-tuple-element.25), channel_id=1, source_target_pairs={{0,14},{2,0},{4,2},{6,4},{8,6},{10,8},{12,10},{14,12},{1,15},{3,1}... | collective-permute-start | bytes 393224 | tf_op jit(solution)/shard_map/ppermute | solution.py:141
  101.3 10.6 %collective-permute-start.12 = (bf16[2,64,1024]{2,1,0:T(8,128)(2,1)S(1)}, bf16[2,64,1024]{2,1,0:T(8,128)(2,1)S(1)}, u32[]{:S(2)}, u32[]{:S(2)}) collective-permute-start(bf16[2,64,1024]{2,1,0:T(8,128)(2,1)S(1)} %pad_maximum_fusion), channel_id=1, source_target_pairs={{0,2},{2,4},{4,6},{6,8},{8,10},{10,12},{12,14},{14,0},{1,3},{3,5},... | collective-permute-start | bytes 786440 | tf_op jit(solution)/shard_map/ppermute | solution.py:140
  103.3 10.6 %collective-permute-start.15 = (bf16[2,64,1024]{2,1,0:T(8,128)(2,1)S(1)}, bf16[2,64,1024]{2,1,0:T(8,128)(2,1)S(1)}, u32[]{:S(2)}, u32[]{:S(2)}) collective-permute-start(bf16[2,64,1024]{2,1,0:T(8,128)(2,1)S(1)} %pad_maximum_fusion.1), channel_id=1, source_target_pairs={{0,14},{2,0},{4,2},{6,4},{8,6},{10,8},{12,10},{14,12},{1,15},{3,1}... | collective-permute-start | bytes 786440 | tf_op jit(solution)/shard_map/ppermute | solution.py:141
  112.0 9.7 %collective-permute-start.14 = (bf16[2,64,1024]{2,1,0:T(8,128)(2,1)S(1)}, bf16[2,64,1024]{2,1,0:T(8,128)(2,1)S(1)}, u32[]{:S(2)}, u32[]{:S(2)}) collective-permute-start(bf16[2,64,1024]{2,1,0:T(8,128)(2,1)S(1)} %fusion.3), channel_id=1, source_target_pairs={{0,2},{2,4},{4,6},{6,8},{8,10},{10,12},{12,14},{14,0},{1,3},{3,5},... | collective-permute-start | bytes 786440 | tf_op jit(solution)/shard_map/ppermute | solution.py:140
  114.1 9.0 %collective-permute-start.17 = (bf16[2,64,1024]{2,1,0:T(8,128)(2,1)S(1)}, bf16[2,64,1024]{2,1,0:T(8,128)(2,1)S(1)}, u32[]{:S(2)}, u32[]{:S(2)}) collective-permute-start(bf16[2,64,1024]{2,1,0:T(8,128)(2,1)S(1)} %fusion.2), channel_id=1, source_target_pairs={{0,14},{2,0},{4,2},{6,4},{8,6},{10,8},{12,10},{14,12},{1,15},{3,1}... | collective-permute-start | bytes 786440 | tf_op jit(solution)/shard_map/ppermute | solution.py:141
  123.2 9.5 %collective-permute-start.18 = (bf16[2,64,1024]{2,1,0:T(8,128)(2,1)S(1)}, bf16[2,64,1024]{2,1,0:T(8,128)(2,1)S(1)}, u32[]{:S(2)}, u32[]{:S(2)}) collective-permute-start(bf16[2,64,1024]{2,1,0:T(8,128)(2,1)S(1)} %fusion.1), channel_id=1, source_target_pairs={{0,14},{2,0},{4,2},{6,4},{8,6},{10,8},{12,10},{14,12},{1,15},{3,1}... | collective-permute-start | bytes 786440 | tf_op jit(solution)/shard_map/ppermute | solution.py:141
  128.8 9.5 %collective-permute-start.16 = (bf16[2,64,1024]{2,1,0:T(8,128)(2,1)S(1)}, bf16[2,64,1024]{2,1,0:T(8,128)(2,1)S(1)}, u32[]{:S(2)}, u32[]{:S(2)}) collective-permute-start(bf16[2,64,1024]{2,1,0:T(8,128)(2,1)S(1)} %fusion.4), channel_id=1, source_target_pairs={{0,2},{2,4},{4,6},{6,8},{8,10},{10,12},{12,14},{14,0},{1,3},{3,5},... | collective-permute-start | bytes 786440 | tf_op jit(solution)/shard_map/ppermute | solution.py:140

commit v4 on v3

--- a/solution.py
+++ b/solution.py
@@ -141,7 +141,7 @@
         down = lax.ppermute(down, "y", ring(-1))
         return up, down
 
-    up, down = pass_on(w_pw, w_pw)
+    across = lax.ppermute(w_pw, "y", ring(4))
     anywhere = pl.BlockSpec(memory_space=pltpu.HBM)
     out = pl.pallas_call(
         pick_kernel,
@@ -161,10 +161,12 @@
     own = jnp.zeros((8, 64, 2048), BF)
     place = lambda buf, piece, d, at=0: lax.dynamic_update_slice(buf, piece[None], ((y + d) & 7, at, 0))
     own = place(own, w_pw, 0)
-    for step in range(2, 5):
-        own = place(place(own, up, 1 - step), down, step - 1)
-        up, down = pass_on(up if step < 4 else up[:32], down if step < 4 else down[32:])
-    own = place(place(own, up, 4), down, 4, 32).reshape(512, 2048)
+    own = place(own, across, 4)
+    both = jnp.stack([w_pw, across])
+    up, down = pass_on(both, both)
+    own = place(place(place(place(own, up[0], -1), up[1], 3), down[0], 1), down[1], -3)
+    up, down = pass_on(up[0], down[0])
+    own = place(place(own, up, -2), down, 2).reshape(512, 2048)
     mate = lax.ppermute(own, "c", swap)
 
     f = jnp.arange(16, dtype=jnp.int32)

time: 140 us -> 140 us (level)
  starting transfers between devices: 82.8 us -> 75.2 us
  waiting for transfers between devices: 36.4 us -> 42.5 us
    ppermute x8 -> x6, starting transfers between devices: 42.6 us -> 29.9 us  [pass_on(): down = lax.ppermute(down, 'y', ring(-1))]
    ppermute x0 -> x1, starting transfers between devices: none -> 7.73 us  [body(): across = lax.ppermute(w_pw, 'y', ring(4))]
    ppermute x8 -> x6, waiting for transfers between devices: 19.2 us -> 23.4 us  [pass_on(): up = lax.ppermute(up, 'y', ring(1))]
    all_to_all x1, waiting for transfers between devices: 5.43 us -> 8.53 us  [body(): lax.all_to_all(out.reshape(48, 24, 512), ('z', 'x'), 0, 0, tiled=True)]
    ppermute x8 -> x6, starting transfers between devices: 15.4 us -> 12.8 us  [pass_on(): up = lax.ppermute(up, 'y', ring(1))]
    ppermute x8 -> x6, waiting for transfers between devices: 5.85 us -> 4.68 us  [pass_on(): down = lax.ppermute(down, 'y', ring(-1))]
  transfers between devices with their start and end apart: 20 -> 17, of which waited for: 12 -> 12; matrix products, arithmetic and copies ran while one was open for 2% -> 4% of each run, Pallas kernels for 3% -> 3%
where the time goes in v4:
time: 140 us
  starting transfers between devices  75.2 us (54%)
  waiting for transfers between devices  42.5 us (30%)
  Pallas kernels  14.8 us (11%)
  local copies, waits for them, and re-layouts  3.43 us (2%)
  other arithmetic  2.63 us (2%)
    ppermute x6, starting transfers between devices, pass_on(): down = lax.ppermute(down, 'y', ring(-1))  29.9 us
    ppermute x6, waiting for transfers between devices, pass_on(): up = lax.ppermute(up, 'y', ring(1))  23.4 us
    all_to_all x1, starting transfers between devices, body(): lax.all_to_all(out.reshape(48, 24, 512), ('z', 'x'), 0, 0, tiled=True)  18.5 us
    ppermute x6, starting transfers between devices, pass_on(): up = lax.ppermute(up, 'y', ring(1))  12.8 us
    pallas_call x1, Pallas kernels, main_call(): pl.pallas_call(main_kernel, grid_spec=gs, out_shape=[jax.ShapeDtypeStruct...  9.97 us
    all_to_all x1, waiting for transfers between devices, body(): lax.all_to_all(out.reshape(48, 24, 512), ('z', 'x'), 0, 0, tiled=True)  8.53 us
    ppermute x1, starting transfers between devices, body(): across = lax.ppermute(w_pw, 'y', ring(4))  7.73 us
    pallas_call x1, Pallas kernels, body(): pl.pallas_call(pick_kernel, in_specs=[anywhere] * 3, out_shape=jax.ShapeD...  4.83 us
  transfers between devices with their start and end apart: 17, of which 12 were waited for; matrix products, arithmetic and copies ran while one was open for 4% of the time, Pallas kernels for 3%

profile of v4, /device:TPU:4, one launch (start us, length us, event | category | flops | bytes accessed | tf_op | source)
XLA Modules:
  0.0 139.5 jit_solution(10190567165467607839)
XLA Ops:
  0.6 7.7 %collective-permute-start = (bf16[64,2048]{1,0:T(8,128)(2,1)}, bf16[64,2048]{1,0:T(8,128)(2,1)S(1)}, u32[]{:S(2)}, u32[]{:S(2)}) collective-permute-start(bf16[64,2048]{1,0:T(8,128)(2,1)} %param.8), channel_id=1, source_target_pairs={{0,8},{2,10},{4,12},{6,14},{8,0},{10,2},{12,4},{14,6},{1,9},{3,11}... | collective-permute-start | bytes 786440 | tf_op jit(solution)/shard_map/ppermute | solution.py:144
  8.4 0.0 copy-start
  8.4 4.8 %pick.1 = bf16[1152,512]{1,0:T(8,128)(2,1)} custom-call(s32[1,576]{1,0:T(1,128)} %bitcast.84, s32[1,576]{1,0:T(1,128)} %bitcast.85, bf16[576,1024]{1,0:T(8,128)(2,1)} %bitcast.80), custom_call_target="tpu_custom_call" | custom-call | tf_op jit(solution)/shard_map/pick/pallas_call | solution.py:146
  13.2 18.5 %all-to-all-start = ((bf16[48,24,512]{2,1,0:T(8,128)(2,1)}), bf16[48,24,512]{2,1,0:T(8,128)(2,1)S(1)}, u32[]{:S(2)}, u32[]{:S(2)}) async-start(bf16[48,24,512]{2,1,0:T(8,128)(2,1)} %bitcast.4), calls=%async_computation | async-start | bytes 2359296 | tf_op jit(solution)/shard_map/all_to_all | solution.py:159
  31.7 0.0 collective-permute-done
  31.7 0.0 copy-start.1
  31.7 0.0 copy-done
  31.7 0.9 pad_maximum_fusion
  32.6 0.0 copy-done.1
  32.6 2.6 %collective-permute-start.1 = (bf16[2,64,2048]{2,1,0:T(8,128)(2,1)}, bf16[2,64,2048]{2,1,0:T(8,128)(2,1)}, u32[]{:S(2)}, u32[]{:S(2)}) collective-permute-start(bf16[2,64,2048]{2,1,0:T(8,128)(2,1)} %pad_maximum_fusion), channel_id=1, source_target_pairs={{0,2},{2,4},{4,6},{6,8},{8,10},{10,12},{12,14},{14,0},{1,3},{3,5},... | collective-permute-start | bytes 1572872 | tf_op jit(solution)/shard_map/ppermute | solution.py:140
  35.2 0.2 broadcast_in_dim.25
  35.5 4.5 %collective-permute-start.2 = (bf16[2,64,2048]{2,1,0:T(8,128)(2,1)}, bf16[2,64,2048]{2,1,0:T(8,128)(2,1)S(1)}, u32[]{:S(2)}, u32[]{:S(2)}) collective-permute-start(bf16[2,64,2048]{2,1,0:T(8,128)(2,1)} %pad_maximum_fusion), channel_id=1, source_target_pairs={{0,14},{2,0},{4,2},{6,4},{8,6},{10,8},{12,10},{14,12},{1,15},{3,1}... | collective-permute-start | bytes 1572872 | tf_op jit(solution)/shard_map/ppermute | solution.py:141
  39.9 1.0 constant_dynamic-update-slice_fusion
  40.9 7.9 %collective-permute-done.1 = bf16[2,64,2048]{2,1,0:T(8,128)(2,1)} collective-permute-done((bf16[2,64,2048]{2,1,0:T(8,128)(2,1)}, bf16[2,64,2048]{2,1,0:T(8,128)(2,1)}, u32[]{:S(2)}, u32[]{:S(2)}) %collective-permute-start.1) | collective-permute-done | bytes 524320 | tf_op jit(solution)/shard_map/ppermute | solution.py:140
  48.8 1.0 slice_dynamic-update-slice_fusion.3
  49.8 1.1 slice_bitcast_fusion.1
  50.9 1.9 %collective-permute-start.3 = (bf16[64,2048]{1,0:T(8,128)(2,1)S(1)}, bf16[64,2048]{1,0:T(8,128)(2,1)S(1)}, u32[]{:S(2)}, u32[]{:S(2)}) collective-permute-start(bf16[64,2048]{1,0:T(8,128)(2,1)S(1)} %get-tuple-element.24), channel_id=1, source_target_pairs={{0,2},{2,4},{4,6},{6,8},{8,10},{10,12},{12,14},{14,0},{1,3},{3,5},... | collective-permute-start | bytes 786440 | tf_op jit(solution)/shard_map/ppermute | solution.py:140
  52.8 0.0 collective-permute-done.2
  52.9 5.1 %collective-permute-start.4 = (bf16[64,2048]{1,0:T(8,128)(2,1)S(1)}, bf16[64,2048]{1,0:T(8,128)(2,1)S(1)}, u32[]{:S(2)}, u32[]{:S(2)}) collective-permute-start(bf16[64,2048]{1,0:T(8,128)(2,1)S(1)} %get-tuple-element.22), channel_id=1, source_target_pairs={{0,14},{2,0},{4,2},{6,4},{8,6},{10,8},{12,10},{14,12},{1,15},{3,1}... | collective-permute-start | bytes 786440 | tf_op jit(solution)/shard_map/ppermute | solution.py:141
  58.0 2.3 %collective-permute-done.3 = bf16[64,2048]{1,0:T(8,128)(2,1)S(1)} collective-permute-done((bf16[64,2048]{1,0:T(8,128)(2,1)S(1)}, bf16[64,2048]{1,0:T(8,128)(2,1)S(1)}, u32[]{:S(2)}, u32[]{:S(2)}) %collective-permute-start.3) | collective-permute-done | bytes 262176 | tf_op jit(solution)/shard_map/ppermute | solution.py:140
  60.4 1.5 %collective-permute-done.4 = bf16[64,2048]{1,0:T(8,128)(2,1)S(1)} collective-permute-done((bf16[64,2048]{1,0:T(8,128)(2,1)S(1)}, bf16[64,2048]{1,0:T(8,128)(2,1)S(1)}, u32[]{:S(2)}, u32[]{:S(2)}) %collective-permute-start.4) | collective-permute-done | bytes 262176 | tf_op jit(solution)/shard_map/ppermute | solution.py:141
  61.9 1.9 %collective-permute-start.5 = (bf16[512,2048]{1,0:T(8,128)(2,1)S(1)}, bf16[512,2048]{1,0:T(8,128)(2,1)}, u32[]{:S(2)}, u32[]{:S(2)}) collective-permute-start(bf16[512,2048]{1,0:T(8,128)(2,1)S(1)} %bitcast.76), channel_id=1, source_target_pairs={{0,1},{1,0},{2,3},{3,2},{4,5},{5,4},{6,7},{7,6},{8,9},{9,8},{10,11... | collective-permute-start | bytes 6291464 | tf_op jit(solution)/shard_map/ppermute | solution.py:170
  63.9 0.1 pad_add_fusion.pos_ref
  64.0 4.2 %collective-permute-done.5.mate_a.mate_b = bf16[512,2048]{1,0:T(8,128)(2,1)} collective-permute-done((bf16[512,2048]{1,0:T(8,128)(2,1)S(1)}, bf16[512,2048]{1,0:T(8,128)(2,1)}, u32[]{:S(2)}, u32[]{:S(2)}) %collective-permute-start.5) | collective-permute-done | bytes 2097184 | tf_op jit(solution)/shard_map/ppermute | solution.py:170
  68.1 8.5 %all-to-all-done = bf16[48,24,512]{2,1,0:T(8,128)(2,1)S(1)} async-done(((bf16[48,24,512]{2,1,0:T(8,128)(2,1)}), bf16[48,24,512]{2,1,0:T(8,128)(2,1)S(1)}, u32[]{:S(2)}, u32[]{:S(2)}) %all-to-all-start) | async-done | bytes 1179680 | tf_op jit(solution)/shard_map/all_to_all | solution.py:159
  76.7 10.0 %main.1 = (bf16[576,1024]{1,0:T(8,128)(2,1)}, bf16[8,2,64,1024]{3,2,1,0:T(8,128)(2,1)S(1)}, bf16[2,64,1024]{2,1,0:T(8,128)(2,1)S(1)}, bf16[7,2,64,1024]{3,2,1,0:T(8,128)(2,1)S(1)}) custom-call(s32[17]{0:T(128)S(1)} %pad_add_fusion.pos_ref, bf16[1152,512]{1,0:T(8,128)(2,1)S(1)} %bitcast.79, bf16[512,2048]{1,0:T(8,128)(2,1)S(1)} %bitcast.77, ...), custom_call_target="tpu_custom_call" | custom-call | tf_op jit(solution)/shard_map/main/pallas_call | solution.py:105
  86.6 1.9 %collective-permute-start.6 = (bf16[7,2,64,1024]{3,2,1,0:T(8,128)(2,1)S(1)}, bf16[7,2,64,1024]{3,2,1,0:T(8,128)(2,1)S(1)}, u32[]{:S(2)}, u32[]{:S(2)}) collective-permute-start(bf16[7,2,64,1024]{3,2,1,0:T(8,128)(2,1)S(1)} %get-tuple-element.13), channel_id=1, source_target_pairs={{0,1},{1,0},{2,3},{3,2},{4,5},{5,4},{6,7},{7,6},{8,9},{9,8},{10,11... | collective-permute-start | bytes 5505032 | tf_op jit(solution)/shard_map/ppermute | solution.py:178
  88.6 2.4 %collective-permute-start.7 = (bf16[2,64,1024]{2,1,0:T(8,128)(2,1)S(1)}, bf16[2,64,1024]{2,1,0:T(8,128)(2,1)S(1)}, u32[]{:S(2)}, u32[]{:S(2)}) collective-permute-start(bf16[2,64,1024]{2,1,0:T(8,128)(2,1)S(1)} %get-tuple-element.14), channel_id=1, source_target_pairs={{0,1},{1,0},{2,3},{3,2},{4,5},{5,4},{6,7},{7,6},{8,9},{9,8},{10,11... | collective-permute-start | bytes 786440 | tf_op jit(solution)/shard_map/ppermute | solution.py:177
  91.0 1.7 %collective-permute-done.7 = bf16[2,64,1024]{2,1,0:T(8,128)(2,1)S(1)} collective-permute-done((bf16[2,64,1024]{2,1,0:T(8,128)(2,1)S(1)}, bf16[2,64,1024]{2,1,0:T(8,128)(2,1)S(1)}, u32[]{:S(2)}, u32[]{:S(2)}) %collective-permute-start.7) | collective-permute-done | bytes 262176 | tf_op jit(solution)/shard_map/ppermute | solution.py:177
  92.7 0.1 fusion
  92.8 2.6 %collective-permute-start.8 = (bf16[64,1024]{1,0:T(8,128)(2,1)S(1)}, bf16[64,1024]{1,0:T(8,128)(2,1)S(1)}, u32[]{:S(2)}, u32[]{:S(2)}) collective-permute-start(bf16[64,1024]{1,0:T(8,128)(2,1)S(1)} %get-tuple-element.28), channel_id=1, source_target_pairs={{0,2},{2,4},{4,6},{6,8},{8,10},{10,12},{12,14},{14,0},{1,3},{3,5},... | collective-permute-start | bytes 393224 | tf_op jit(solution)/shard_map/ppermute | solution.py:140
  95.4 4.5 %collective-permute-start.10 = (bf16[64,1024]{1,0:T(8,128)(2,1)S(1)}, bf16[64,1024]{1,0:T(8,128)(2,1)S(1)}, u32[]{:S(2)}, u32[]{:S(2)}) collective-permute-start(bf16[64,1024]{1,0:T(8,128)(2,1)S(1)} %get-tuple-element.29), channel_id=1, source_target_pairs={{0,14},{2,0},{4,2},{6,4},{8,6},{10,8},{12,10},{14,12},{1,15},{3,1}... | collective-permute-start | bytes 393224 | tf_op jit(solution)/shard_map/ppermute | solution.py:141
  99.8 1.6 %collective-permute-done.8 = bf16[64,1024]{1,0:T(8,128)(2,1)S(1)} collective-permute-done((bf16[64,1024]{1,0:T(8,128)(2,1)S(1)}, bf16[64,1024]{1,0:T(8,128)(2,1)S(1)}, u32[]{:S(2)}, u32[]{:S(2)}) %collective-permute-start.8) | collective-permute-done | bytes 131104 | tf_op jit(solution)/shard_map/ppermute | solution.py:140
  101.4 0.0 collective-permute-done.6
  101.4 0.1 fusion.11
  101.5 0.1 fusion.10
  101.6 1.9 %collective-permute-start.9 = (bf16[2,64,1024]{2,1,0:T(8,128)(2,1)S(1)}, bf16[2,64,1024]{2,1,0:T(8,128)(2,1)S(1)}, u32[]{:S(2)}, u32[]{:S(2)}) collective-permute-start(bf16[2,64,1024]{2,1,0:T(8,128)(2,1)S(1)} %pad_maximum_fusion.1), channel_id=1, source_target_pairs={{0,2},{2,4},{4,6},{6,8},{8,10},{10,12},{12,14},{14,0},{1,3},{3,5},... | collective-permute-start | bytes 786440 | tf_op jit(solution)/shard_map/ppermute | solution.py:140
  103.5 0.0 collective-permute-done.10
  103.5 0.1 fusion.12
  103.6 5.1 %collective-permute-start.12 = (bf16[2,64,1024]{2,1,0:T(8,128)(2,1)S(1)}, bf16[2,64,1024]{2,1,0:T(8,128)(2,1)S(1)}, u32[]{:S(2)}, u32[]{:S(2)}) collective-permute-start(bf16[2,64,1024]{2,1,0:T(8,128)(2,1)S(1)} %pad_maximum_fusion.2), channel_id=1, source_target_pairs={{0,14},{2,0},{4,2},{6,4},{8,6},{10,8},{12,10},{14,12},{1,15},{3,1}... | collective-permute-start | bytes 786440 | tf_op jit(solution)/shard_map/ppermute | solution.py:141
  108.8 3.4 %collective-permute-done.9 = bf16[2,64,1024]{2,1,0:T(8,128)(2,1)S(1)} collective-permute-done((bf16[2,64,1024]{2,1,0:T(8,128)(2,1)S(1)}, bf16[2,64,1024]{2,1,0:T(8,128)(2,1)S(1)}, u32[]{:S(2)}, u32[]{:S(2)}) %collective-permute-start.9) | collective-permute-done | bytes 262176 | tf_op jit(solution)/shard_map/ppermute | solution.py:140
  112.2 0.1 fusion.3
  112.3 1.9 %collective-permute-start.11 = (bf16[2,64,1024]{2,1,0:T(8,128)(2,1)S(1)}, bf16[2,64,1024]{2,1,0:T(8,128)(2,1)S(1)}, u32[]{:S(2)}, u32[]{:S(2)}) collective-permute-start(bf16[2,64,1024]{2,1,0:T(8,128)(2,1)S(1)} %fusion.3), channel_id=1, source_target_pairs={{0,2},{2,4},{4,6},{6,8},{8,10},{10,12},{12,14},{14,0},{1,3},{3,5},... | collective-permute-start | bytes 786440 | tf_op jit(solution)/shard_map/ppermute | solution.py:140
  114.2 0.0 collective-permute-done.12
  114.3 0.1 fusion.2
  114.4 5.1 %collective-permute-start.14 = (bf16[2,64,1024]{2,1,0:T(8,128)(2,1)S(1)}, bf16[2,64,1024]{2,1,0:T(8,128)(2,1)S(1)}, u32[]{:S(2)}, u32[]{:S(2)}) collective-permute-start(bf16[2,64,1024]{2,1,0:T(8,128)(2,1)S(1)} %fusion.2), channel_id=1, source_target_pairs={{0,14},{2,0},{4,2},{6,4},{8,6},{10,8},{12,10},{14,12},{1,15},{3,1}... | collective-permute-start | bytes 786440 | tf_op jit(solution)/shard_map/ppermute | solution.py:141
  119.5 2.5 %collective-permute-done.11 = bf16[2,64,1024]{2,1,0:T(8,128)(2,1)S(1)} collective-permute-done((bf16[2,64,1024]{2,1,0:T(8,128)(2,1)S(1)}, bf16[2,64,1024]{2,1,0:T(8,128)(2,1)S(1)}, u32[]{:S(2)}, u32[]{:S(2)}) %collective-permute-start.11) | collective-permute-done | bytes 262176 | tf_op jit(solution)/shard_map/ppermute | solution.py:140
  122.1 0.1 fusion.4
  122.2 1.2 collective-permute-done.14
  123.4 0.1 fusion.1
  123.5 5.6 %collective-permute-start.15 = (bf16[2,64,1024]{2,1,0:T(8,128)(2,1)S(1)}, bf16[2,64,1024]{2,1,0:T(8,128)(2,1)S(1)}, u32[]{:S(2)}, u32[]{:S(2)}) collective-permute-start(bf16[2,64,1024]{2,1,0:T(8,128)(2,1)S(1)} %fusion.1), channel_id=1, source_target_pairs={{0,14},{2,0},{4,2},{6,4},{8,6},{10,8},{12,10},{14,12},{1,15},{3,1}... | collective-permute-start | bytes 786440 | tf_op jit(solution)/shard_map/ppermute | solution.py:141
  129.1 1.9 %collective-permute-start.13 = (bf16[2,64,1024]{2,1,0:T(8,128)(2,1)S(1)}, bf16[2,64,1024]{2,1,0:T(8,128)(2,1)S(1)}, u32[]{:S(2)}, u32[]{:S(2)}) collective-permute-start(bf16[2,64,1024]{2,1,0:T(8,128)(2,1)S(1)} %fusion.4), channel_id=1, source_target_pairs={{0,2},{2,4},{4,6},{6,8},{8,10},{10,12},{12,14},{14,0},{1,3},{3,5},... | collective-permute-start | bytes 786440 | tf_op jit(solution)/shard_map/ppermute | solution.py:140
  131.1 1.9 %collective-permute-done.15 = bf16[2,64,1024]{2,1,0:T(8,128)(2,1)S(1)} collective-permute-done((bf16[2,64,1024]{2,1,0:T(8,128)(2,1)S(1)}, bf16[2,64,1024]{2,1,0:T(8,128)(2,1)S(1)}, u32[]{:S(2)}, u32[]{:S(2)}) %collective-permute-start.15) | collective-permute-done | bytes 262176 | tf_op jit(solution)/shard_map/ppermute | solution.py:141
  133.0 5.6 %collective-permute-done.13 = bf16[2,64,1024]{2,1,0:T(8,128)(2,1)S(1)} collective-permute-done((bf16[2,64,1024]{2,1,0:T(8,128)(2,1)S(1)}, bf16[2,64,1024]{2,1,0:T(8,128)(2,1)S(1)}, u32[]{:S(2)}, u32[]{:S(2)}) %collective-permute-start.13) | collective-permute-done | bytes 262176 | tf_op jit(solution)/shard_map/ppermute | solution.py:140
  138.6 0.2 fusion.6
  138.8 0.7 maximum_bitcast_fusion
  (10 shorter events, 0.2 us)
Async XLA Ops:
  0.6 31.1 %collective-permute-start = (bf16[64,2048]{1,0:T(8,128)(2,1)}, bf16[64,2048]{1,0:T(8,128)(2,1)S(1)}, u32[]{:S(2)}, u32[]{:S(2)}) collective-permute-start(bf16[64,2048]{1,0:T(8,128)(2,1)} %param.8), channel_id=1, source_target_pairs={{0,8},{2,10},{4,12},{6,14},{8,0},{10,2},{12,4},{14,6},{1,9},{3,11}... | collective-permute-start | bytes 786440 | tf_op jit(solution)/shard_map/ppermute | solution.py:144
  8.4 23.3 %copy-start = (bf16[64,2048]{1,0:T(8,128)(2,1)S(1)}, bf16[64,2048]{1,0:T(8,128)(2,1)}, u32[]{:S(2)}) copy-start(bf16[64,2048]{1,0:T(8,128)(2,1)} %param.8) | copy-start | bytes 786436
  13.2 63.4 %all-to-all-start = ((bf16[48,24,512]{2,1,0:T(8,128)(2,1)}), bf16[48,24,512]{2,1,0:T(8,128)(2,1)S(1)}, u32[]{:S(2)}, u32[]{:S(2)}) async-start(bf16[48,24,512]{2,1,0:T(8,128)(2,1)} %bitcast.4), calls=%async_computation | async-start | bytes 2359296 | tf_op jit(solution)/shard_map/all_to_all | solution.py:159
  31.7 0.9 copy-start.1
  32.6 16.2 %collective-permute-start.1 = (bf16[2,64,2048]{2,1,0:T(8,128)(2,1)}, bf16[2,64,2048]{2,1,0:T(8,128)(2,1)}, u32[]{:S(2)}, u32[]{:S(2)}) collective-permute-start(bf16[2,64,2048]{2,1,0:T(8,128)(2,1)} %pad_maximum_fusion), channel_id=1, source_target_pairs={{0,2},{2,4},{4,6},{6,8},{8,10},{10,12},{12,14},{14,0},{1,3},{3,5},... | collective-permute-start | bytes 1572872 | tf_op jit(solution)/shard_map/ppermute | solution.py:140
  35.5 17.3 %collective-permute-start.2 = (bf16[2,64,2048]{2,1,0:T(8,128)(2,1)}, bf16[2,64,2048]{2,1,0:T(8,128)(2,1)S(1)}, u32[]{:S(2)}, u32[]{:S(2)}) collective-permute-start(bf16[2,64,2048]{2,1,0:T(8,128)(2,1)} %pad_maximum_fusion), channel_id=1, source_target_pairs={{0,14},{2,0},{4,2},{6,4},{8,6},{10,8},{12,10},{14,12},{1,15},{3,1}... | collective-permute-start | bytes 1572872 | tf_op jit(solution)/shard_map/ppermute | solution.py:141
  50.9 9.5 %collective-permute-start.3 = (bf16[64,2048]{1,0:T(8,128)(2,1)S(1)}, bf16[64,2048]{1,0:T(8,128)(2,1)S(1)}, u32[]{:S(2)}, u32[]{:S(2)}) collective-permute-start(bf16[64,2048]{1,0:T(8,128)(2,1)S(1)} %get-tuple-element.24), channel_id=1, source_target_pairs={{0,2},{2,4},{4,6},{6,8},{8,10},{10,12},{12,14},{14,0},{1,3},{3,5},... | collective-permute-start | bytes 786440 | tf_op jit(solution)/shard_map/ppermute | solution.py:140
  52.9 9.0 %collective-permute-start.4 = (bf16[64,2048]{1,0:T(8,128)(2,1)S(1)}, bf16[64,2048]{1,0:T(8,128)(2,1)S(1)}, u32[]{:S(2)}, u32[]{:S(2)}) collective-permute-start(bf16[64,2048]{1,0:T(8,128)(2,1)S(1)} %get-tuple-element.22), channel_id=1, source_target_pairs={{0,14},{2,0},{4,2},{6,4},{8,6},{10,8},{12,10},{14,12},{1,15},{3,1}... | collective-permute-start | bytes 786440 | tf_op jit(solution)/shard_map/ppermute | solution.py:141
  61.9 6.2 %collective-permute-start.5 = (bf16[512,2048]{1,0:T(8,128)(2,1)S(1)}, bf16[512,2048]{1,0:T(8,128)(2,1)}, u32[]{:S(2)}, u32[]{:S(2)}) collective-permute-start(bf16[512,2048]{1,0:T(8,128)(2,1)S(1)} %bitcast.76), channel_id=1, source_target_pairs={{0,1},{1,0},{2,3},{3,2},{4,5},{5,4},{6,7},{7,6},{8,9},{9,8},{10,11... | collective-permute-start | bytes 6291464 | tf_op jit(solution)/shard_map/ppermute | solution.py:170
  86.6 14.8 %collective-permute-start.6 = (bf16[7,2,64,1024]{3,2,1,0:T(8,128)(2,1)S(1)}, bf16[7,2,64,1024]{3,2,1,0:T(8,128)(2,1)S(1)}, u32[]{:S(2)}, u32[]{:S(2)}) collective-permute-start(bf16[7,2,64,1024]{3,2,1,0:T(8,128)(2,1)S(1)} %get-tuple-element.13), channel_id=1, source_target_pairs={{0,1},{1,0},{2,3},{3,2},{4,5},{5,4},{6,7},{7,6},{8,9},{9,8},{10,11... | collective-permute-start | bytes 5505032 | tf_op jit(solution)/shard_map/ppermute | solution.py:178
  88.6 4.1 %collective-permute-start.7 = (bf16[2,64,1024]{2,1,0:T(8,128)(2,1)S(1)}, bf16[2,64,1024]{2,1,0:T(8,128)(2,1)S(1)}, u32[]{:S(2)}, u32[]{:S(2)}) collective-permute-start(bf16[2,64,1024]{2,1,0:T(8,128)(2,1)S(1)} %get-tuple-element.14), channel_id=1, source_target_pairs={{0,1},{1,0},{2,3},{3,2},{4,5},{5,4},{6,7},{7,6},{8,9},{9,8},{10,11... | collective-permute-start | bytes 786440 | tf_op jit(solution)/shard_map/ppermute | solution.py:177
  92.8 8.6 %collective-permute-start.8 = (bf16[64,1024]{1,0:T(8,128)(2,1)S(1)}, bf16[64,1024]{1,0:T(8,128)(2,1)S(1)}, u32[]{:S(2)}, u32[]{:S(2)}) collective-permute-start(bf16[64,1024]{1,0:T(8,128)(2,1)S(1)} %get-tuple-element.28), channel_id=1, source_target_pairs={{0,2},{2,4},{4,6},{6,8},{8,10},{10,12},{12,14},{14,0},{1,3},{3,5},... | collective-permute-start | bytes 393224 | tf_op jit(solution)/shard_map/ppermute | solution.py:140
  95.4 8.2 %collective-permute-start.10 = (bf16[64,1024]{1,0:T(8,128)(2,1)S(1)}, bf16[64,1024]{1,0:T(8,128)(2,1)S(1)}, u32[]{:S(2)}, u32[]{:S(2)}) collective-permute-start(bf16[64,1024]{1,0:T(8,128)(2,1)S(1)} %get-tuple-element.29), channel_id=1, source_target_pairs={{0,14},{2,0},{4,2},{6,4},{8,6},{10,8},{12,10},{14,12},{1,15},{3,1}... | collective-permute-start | bytes 393224 | tf_op jit(solution)/shard_map/ppermute | solution.py:141
  101.6 10.6 %collective-permute-start.9 = (bf16[2,64,1024]{2,1,0:T(8,128)(2,1)S(1)}, bf16[2,64,1024]{2,1,0:T(8,128)(2,1)S(1)}, u32[]{:S(2)}, u32[]{:S(2)}) collective-permute-start(bf16[2,64,1024]{2,1,0:T(8,128)(2,1)S(1)} %pad_maximum_fusion.1), channel_id=1, source_target_pairs={{0,2},{2,4},{4,6},{6,8},{8,10},{10,12},{12,14},{14,0},{1,3},{3,5},... | collective-permute-start | bytes 786440 | tf_op jit(solution)/shard_map/ppermute | solution.py:140
  103.6 10.6 %collective-permute-start.12 = (bf16[2,64,1024]{2,1,0:T(8,128)(2,1)S(1)}, bf16[2,64,1024]{2,1,0:T(8,128)(2,1)S(1)}, u32[]{:S(2)}, u32[]{:S(2)}) collective-permute-start(bf16[2,64,1024]{2,1,0:T(8,128)(2,1)S(1)} %pad_maximum_fusion.2), channel_id=1, source_target_pairs={{0,14},{2,0},{4,2},{6,4},{8,6},{10,8},{12,10},{14,12},{1,15},{3,1}... | collective-permute-start | bytes 786440 | tf_op jit(solution)/shard_map/ppermute | solution.py:141
  112.3 9.7 %collective-permute-start.11 = (bf16[2,64,1024]{2,1,0:T(8,128)(2,1)S(1)}, bf16[2,64,1024]{2,1,0:T(8,128)(2,1)S(1)}, u32[]{:S(2)}, u32[]{:S(2)}) collective-permute-start(bf16[2,64,1024]{2,1,0:T(8,128)(2,1)S(1)} %fusion.3), channel_id=1, source_target_pairs={{0,2},{2,4},{4,6},{6,8},{8,10},{10,12},{12,14},{14,0},{1,3},{3,5},... | collective-permute-start | bytes 786440 | tf_op jit(solution)/shard_map/ppermute | solution.py:140
  114.4 9.0 %collective-permute-start.14 = (bf16[2,64,1024]{2,1,0:T(8,128)(2,1)S(1)}, bf16[2,64,1024]{2,1,0:T(8,128)(2,1)S(1)}, u32[]{:S(2)}, u32[]{:S(2)}) collective-permute-start(bf16[2,64,1024]{2,1,0:T(8,128)(2,1)S(1)} %fusion.2), channel_id=1, source_target_pairs={{0,14},{2,0},{4,2},{6,4},{8,6},{10,8},{12,10},{14,12},{1,15},{3,1}... | collective-permute-start | bytes 786440 | tf_op jit(solution)/shard_map/ppermute | solution.py:141
  123.5 9.5 %collective-permute-start.15 = (bf16[2,64,1024]{2,1,0:T(8,128)(2,1)S(1)}, bf16[2,64,1024]{2,1,0:T(8,128)(2,1)S(1)}, u32[]{:S(2)}, u32[]{:S(2)}) collective-permute-start(bf16[2,64,1024]{2,1,0:T(8,128)(2,1)S(1)} %fusion.1), channel_id=1, source_target_pairs={{0,14},{2,0},{4,2},{6,4},{8,6},{10,8},{12,10},{14,12},{1,15},{3,1}... | collective-permute-start | bytes 786440 | tf_op jit(solution)/shard_map/ppermute | solution.py:141
  129.1 9.5 %collective-permute-start.13 = (bf16[2,64,1024]{2,1,0:T(8,128)(2,1)S(1)}, bf16[2,64,1024]{2,1,0:T(8,128)(2,1)S(1)}, u32[]{:S(2)}, u32[]{:S(2)}) collective-permute-start(bf16[2,64,1024]{2,1,0:T(8,128)(2,1)S(1)} %fusion.4), channel_id=1, source_target_pairs={{0,2},{2,4},{4,6},{6,8},{8,10},{10,12},{12,14},{14,0},{1,3},{3,5},... | collective-permute-start | bytes 786440 | tf_op jit(solution)/shard_map/ppermute | solution.py:140

commit v5 on v4

--- a/solution.py
+++ b/solution.py
@@ -77,14 +77,10 @@
     da = (upstream * second).astype(BF)
     db = (upstream * gated * (1.0 - second)).astype(BF)
     for h, slope in enumerate((da, db)):
-        grad = dot(flip, slope).astype(BF)
-        for d in range(8):
-            keep_ref[d, h] = grad[d * 64:d * 64 + 64]
-            block = grad[d * 64 + 512:d * 64 + 576]
-            if d == 4:
-                far_ref[h] = block
-            else:
-                send_ref[d - (d > 4), h] = block
+        grad = dot(flip, slope).astype(BF).reshape(16, 64, COLS)
+        keep_ref[h] = grad[:8]
+        far_ref[h] = grad[8]
+        send_ref[h] = grad[9:]
 
 
 def main_call(pos, got, own, mate, cot):
@@ -96,9 +92,9 @@
         in_specs=[pl.BlockSpec((1152, 512), lambda j, p: (0, 0)), half(0), half(STEPS), half(0), half(STEPS), wide],
         out_specs=[
             wide,
-            pl.BlockSpec((8, 2, 64, COLS), lambda j, p: (0, 0, 0, j)),
+            pl.BlockSpec((2, 8, 64, COLS), lambda j, p: (0, 0, 0, j)),
             pl.BlockSpec((2, 64, COLS), lambda j, p: (0, 0, j)),
-            pl.BlockSpec((7, 2, 64, COLS), lambda j, p: (0, 0, 0, j)),
+            pl.BlockSpec((2, 7, 64, COLS), lambda j, p: (0, 0, 0, j)),
         ],
         scratch_shapes=[pltpu.VMEM((2, 576, 512), BF), pltpu.VMEM((16, 64, 576), BF)],
     )
@@ -107,9 +103,9 @@
         grid_spec=gs,
         out_shape=[
             jax.ShapeDtypeStruct((576, 1024), BF),
-            jax.ShapeDtypeStruct((8, 2, 64, 1024), BF),
+            jax.ShapeDtypeStruct((2, 8, 64, 1024), BF),
             jax.ShapeDtypeStruct((2, 64, 1024), BF),
-            jax.ShapeDtypeStruct((7, 2, 64, 1024), BF),
+            jax.ShapeDtypeStruct((2, 7, 64, 1024), BF),
         ],
         compiler_params=pltpu.CompilerParams(vmem_limit_bytes=40 << 20),
         name="main",
@@ -170,28 +166,36 @@
     mate = lax.ppermute(own, "c", swap)
 
     f = jnp.arange(16, dtype=jnp.int32)
-    pos = ((f & 1) ^ c) * 8 + (((f >> 1) - y) & 7)
+    gap = ((f >> 1) - y) & 7
+    gap = jnp.where(c == 0, gap, (8 - gap) & 7)
+    ends = (gap & 3) == 0
+    turn = (f & 1) ^ c
+    theirs = jnp.where(ends, turn, (gap > 4).astype(jnp.int32))
+    near = jnp.where(gap > 4, 8 - gap, gap)
+    pos = jnp.where(ends, jnp.where(gap == 0, 7, 0), 7 - 2 * near + (turn ^ theirs)) + 8 * theirs
     pos = jnp.concatenate([pos, c[None]]).astype(jnp.int32)
     gated, keep, far, rest = main_call(pos, got, own, mate, stay(cotangent[0, 0]))
 
     far = lax.ppermute(far, "c", swap)
     rest = lax.ppermute(rest, "c", swap)
-    piece = lambda d: (keep[d], rest[d - (d > 4)])
-    mid = total(keep[4], far)
-    up, down = pass_on(mid[0], mid[1])
-    k, g = piece(3)
-    up = jnp.stack([total(k[0], g[0], up), total(k[1], g[1])])
-    k, g = piece(5)
-    down = after(down, up)
-    down = jnp.stack([total(k[0], g[0]), total(k[1], g[1], down)])
-    for d in (2, 1, 0):
-        sent = down
-        up, down = pass_on(up, down)
-        if d:
-            up = total(*piece(d), after(up, sent))
-            down = total(*piece(8 - d), after(down, up))
-    grad = total(*piece(0), up, down)
-    grad = jnp.concatenate([grad[0], grad[1]], axis=1)
+    ways = [(2 * i, 2 * ((i + 1) % 8)) for i in range(8)] + [(2 * i + 1, 2 * ((i - 1) % 8) + 1) for i in range(8)]
+    got = lax.ppermute(total(keep[:, 0], far), ("y", "c"), ways)
+    part = lambda h, i, n=1: (keep[h, i:i + n], rest[h, i - 1:i - 1 + n])
+    chains = [got[0][None], got[1][None]]
+    sent = None
+    for step in range(2, 5):
+        for h in range(2):
+            got = chains[h] if sent is None else after(chains[h], sent)
+            at = 2 * step - 3
+            if step == 2:
+                sent = jnp.concatenate([total(*part(h, at), got), total(*part(h, at + 1))])
+            else:
+                sent = total(*part(h, at, 2), got)
+            chains[h] = lax.ppermute(sent, ("y", "c"), ways)
+    grads = []
+    for h in range(2):
+        grads.append(total(*part(h, 7), chains[h][:1], lax.ppermute(chains[h][1:], "c", swap))[0])
+    grad = jnp.concatenate(grads, axis=1)
     return gated[None, None], grad[None]
 
 

time: 140 us -> 143 us (1.021)
  the two profiles are of different devices: /device:TPU:4 before, /device:TPU:1 now
where the time goes in v5:
time: 143 us; the launch traced here: 142 us
  starting transfers between devices  82.2 us (57%)
  waiting for transfers between devices  37.6 us (26%)
  Pallas kernels  14.8 us (10%)
  local copies, waits for them, and re-layouts  3.42 us (2%)
  other arithmetic  2.64 us (2%)
    all_to_all x1, starting transfers between devices, body(): lax.all_to_all(out.reshape(48, 24, 512), ('z', 'x'), 0, 0, tiled=True)  18 us
    ppermute x6, starting transfers between devices, body(): chains[h] = lax.ppermute(sent, ('y', 'c'), ways)  17.2 us
    ppermute x2, starting transfers between devices, body(): lax.ppermute(chains[h][1:], 'c', swap)  12.4 us
    ppermute x2, waiting for transfers between devices, pass_on(): up = lax.ppermute(up, 'y', ring(1))  10.2 us
    pallas_call x1, Pallas kernels, main_call(): pl.pallas_call(main_kernel, grid_spec=gs, out_shape=[jax.ShapeDtypeStruct...  9.97 us
    ppermute x2, starting transfers between devices, pass_on(): down = lax.ppermute(down, 'y', ring(-1))  8.77 us
    ppermute x6, waiting for transfers between devices, body(): chains[h] = lax.ppermute(sent, ('y', 'c'), ways)  8.35 us
    ppermute x1, starting transfers between devices, body(): across = lax.ppermute(w_pw, 'y', ring(4))  8.27 us
  transfers between devices with their start and end apart: 18, of which 12 were waited for; matrix products, arithmetic and copies ran while one was open for 3% of the time, Pallas kernels for 3%

profile of v5, /device:TPU:1, one launch (start us, length us, event | category | flops | bytes accessed | tf_op | source)
XLA Modules:
  0.0 141.7 jit_solution(10097483138632677907)
XLA Ops:
  0.6 8.3 %collective-permute-start = (bf16[64,2048]{1,0:T(8,128)(2,1)}, bf16[64,2048]{1,0:T(8,128)(2,1)S(1)}, u32[]{:S(2)}, u32[]{:S(2)}) collective-permute-start(bf16[64,2048]{1,0:T(8,128)(2,1)} %param.8), channel_id=1, source_target_pairs={{0,8},{2,10},{4,12},{6,14},{8,0},{10,2},{12,4},{14,6},{1,9},{3,11}... | collective-permute-start | bytes 786440 | tf_op jit(solution)/shard_map/ppermute | solution.py:140
  8.9 0.0 copy-start
  8.9 4.8 %pick.1 = bf16[1152,512]{1,0:T(8,128)(2,1)} custom-call(s32[1,576]{1,0:T(1,128)} %bitcast.84, s32[1,576]{1,0:T(1,128)} %bitcast.85, bf16[576,1024]{1,0:T(8,128)(2,1)} %bitcast.80), custom_call_target="tpu_custom_call" | custom-call | tf_op jit(solution)/shard_map/pick/pallas_call | solution.py:142
  13.8 18.0 %all-to-all-start = ((bf16[48,24,512]{2,1,0:T(8,128)(2,1)}), bf16[48,24,512]{2,1,0:T(8,128)(2,1)S(1)}, u32[]{:S(2)}, u32[]{:S(2)}) async-start(bf16[48,24,512]{2,1,0:T(8,128)(2,1)} %bitcast.4), calls=%async_computation | async-start | bytes 2359296 | tf_op jit(solution)/shard_map/all_to_all | solution.py:155
  31.8 0.0 collective-permute-done
  31.8 0.0 copy-start.1
  31.8 0.0 copy-done
  31.8 0.9 pad_maximum_fusion
  32.7 0.0 copy-done.1
  32.7 2.3 %collective-permute-start.1 = (bf16[2,64,2048]{2,1,0:T(8,128)(2,1)}, bf16[2,64,2048]{2,1,0:T(8,128)(2,1)}, u32[]{:S(2)}, u32[]{:S(2)}) collective-permute-start(bf16[2,64,2048]{2,1,0:T(8,128)(2,1)} %pad_maximum_fusion), channel_id=1, source_target_pairs={{0,2},{2,4},{4,6},{6,8},{8,10},{10,12},{12,14},{14,0},{1,3},{3,5},... | collective-permute-start | bytes 1572872 | tf_op jit(solution)/shard_map/ppermute | solution.py:136
  35.0 0.2 broadcast_in_dim.29
  35.3 4.2 %collective-permute-start.2 = (bf16[2,64,2048]{2,1,0:T(8,128)(2,1)}, bf16[2,64,2048]{2,1,0:T(8,128)(2,1)S(1)}, u32[]{:S(2)}, u32[]{:S(2)}) collective-permute-start(bf16[2,64,2048]{2,1,0:T(8,128)(2,1)} %pad_maximum_fusion), channel_id=1, source_target_pairs={{0,14},{2,0},{4,2},{6,4},{8,6},{10,8},{12,10},{14,12},{1,15},{3,1}... | collective-permute-start | bytes 1572872 | tf_op jit(solution)/shard_map/ppermute | solution.py:137
  39.5 1.0 constant_dynamic-update-slice_fusion
  40.5 7.9 %collective-permute-done.1 = bf16[2,64,2048]{2,1,0:T(8,128)(2,1)} collective-permute-done((bf16[2,64,2048]{2,1,0:T(8,128)(2,1)}, bf16[2,64,2048]{2,1,0:T(8,128)(2,1)}, u32[]{:S(2)}, u32[]{:S(2)}) %collective-permute-start.1) | collective-permute-done | bytes 524320 | tf_op jit(solution)/shard_map/ppermute | solution.py:136
  48.4 1.0 slice_dynamic-update-slice_fusion.3
  49.3 1.1 slice_bitcast_fusion.2
  50.4 1.9 %collective-permute-start.3 = (bf16[64,2048]{1,0:T(8,128)(2,1)S(1)}, bf16[64,2048]{1,0:T(8,128)(2,1)S(1)}, u32[]{:S(2)}, u32[]{:S(2)}) collective-permute-start(bf16[64,2048]{1,0:T(8,128)(2,1)S(1)} %get-tuple-element.26), channel_id=1, source_target_pairs={{0,2},{2,4},{4,6},{6,8},{8,10},{10,12},{12,14},{14,0},{1,3},{3,5},... | collective-permute-start | bytes 786440 | tf_op jit(solution)/shard_map/ppermute | solution.py:136
  52.3 0.0 collective-permute-done.2
  52.4 4.6 %collective-permute-start.4 = (bf16[64,2048]{1,0:T(8,128)(2,1)S(1)}, bf16[64,2048]{1,0:T(8,128)(2,1)S(1)}, u32[]{:S(2)}, u32[]{:S(2)}) collective-permute-start(bf16[64,2048]{1,0:T(8,128)(2,1)S(1)} %get-tuple-element.24), channel_id=1, source_target_pairs={{0,14},{2,0},{4,2},{6,4},{8,6},{10,8},{12,10},{14,12},{1,15},{3,1}... | collective-permute-start | bytes 786440 | tf_op jit(solution)/shard_map/ppermute | solution.py:137
  57.0 2.3 %collective-permute-done.3 = bf16[64,2048]{1,0:T(8,128)(2,1)S(1)} collective-permute-done((bf16[64,2048]{1,0:T(8,128)(2,1)S(1)}, bf16[64,2048]{1,0:T(8,128)(2,1)S(1)}, u32[]{:S(2)}, u32[]{:S(2)}) %collective-permute-start.3) | collective-permute-done | bytes 262176 | tf_op jit(solution)/shard_map/ppermute | solution.py:136
  59.3 1.0 collective-permute-done.4
  60.3 5.1 %collective-permute-start.5 = (bf16[512,2048]{1,0:T(8,128)(2,1)S(1)}, bf16[512,2048]{1,0:T(8,128)(2,1)}, u32[]{:S(2)}, u32[]{:S(2)}) collective-permute-start(bf16[512,2048]{1,0:T(8,128)(2,1)S(1)} %bitcast.76), channel_id=1, source_target_pairs={{0,1},{1,0},{2,3},{3,2},{4,5},{5,4},{6,7},{7,6},{8,9},{9,8},{10,11... | collective-permute-start | bytes 6291464 | tf_op jit(solution)/shard_map/ppermute | solution.py:166
  65.5 0.1 pad_add_fusion.pos_ref
  65.6 3.8 %collective-permute-done.5.mate_a.mate_b = bf16[512,2048]{1,0:T(8,128)(2,1)} collective-permute-done((bf16[512,2048]{1,0:T(8,128)(2,1)S(1)}, bf16[512,2048]{1,0:T(8,128)(2,1)}, u32[]{:S(2)}, u32[]{:S(2)}) %collective-permute-start.5) | collective-permute-done | bytes 2097184 | tf_op jit(solution)/shard_map/ppermute | solution.py:166
  69.4 6.2 %all-to-all-done = bf16[48,24,512]{2,1,0:T(8,128)(2,1)S(1)} async-done(((bf16[48,24,512]{2,1,0:T(8,128)(2,1)}), bf16[48,24,512]{2,1,0:T(8,128)(2,1)S(1)}, u32[]{:S(2)}, u32[]{:S(2)}) %all-to-all-start) | async-done | bytes 1179680 | tf_op jit(solution)/shard_map/all_to_all | solution.py:155
  75.5 10.0 %main.1 = (bf16[576,1024]{1,0:T(8,128)(2,1)}, bf16[2,8,64,1024]{3,2,1,0:T(8,128)(2,1)S(1)}, bf16[2,64,1024]{2,1,0:T(8,128)(2,1)S(1)}, bf16[2,7,64,1024]{3,2,1,0:T(8,128)(2,1)S(1)}) custom-call(s32[17]{0:T(128)S(1)} %pad_add_fusion.pos_ref, bf16[1152,512]{1,0:T(8,128)(2,1)S(1)} %bitcast.79, bf16[512,2048]{1,0:T(8,128)(2,1)S(1)} %bitcast.77, ...), custom_call_target="tpu_custom_call" | custom-call | tf_op jit(solution)/shard_map/main/pallas_call | solution.py:101
  85.5 4.2 %collective-permute-start.6 = (bf16[2,7,64,1024]{3,2,1,0:T(8,128)(2,1)S(1)}, bf16[2,7,64,1024]{3,2,1,0:T(8,128)(2,1)S(1)}, u32[]{:S(2)}, u32[]{:S(2)}) collective-permute-start(bf16[2,7,64,1024]{3,2,1,0:T(8,128)(2,1)S(1)} %get-tuple-element.13), channel_id=1, source_target_pairs={{0,1},{1,0},{2,3},{3,2},{4,5},{5,4},{6,7},{7,6},{8,9},{9,8},{10,11... | collective-permute-start | bytes 5505032 | tf_op jit(solution)/shard_map/ppermute | solution.py:180
  89.8 1.9 %collective-permute-start.7 = (bf16[2,64,1024]{2,1,0:T(8,128)(2,1)S(1)}, bf16[2,64,1024]{2,1,0:T(8,128)(2,1)S(1)}, u32[]{:S(2)}, u32[]{:S(2)}) collective-permute-start(bf16[2,64,1024]{2,1,0:T(8,128)(2,1)S(1)} %get-tuple-element.14), channel_id=1, source_target_pairs={{0,1},{1,0},{2,3},{3,2},{4,5},{5,4},{6,7},{7,6},{8,9},{9,8},{10,11... | collective-permute-start | bytes 786440 | tf_op jit(solution)/shard_map/ppermute | solution.py:179
  91.7 1.8 %collective-permute-done.7 = bf16[2,64,1024]{2,1,0:T(8,128)(2,1)S(1)} collective-permute-done((bf16[2,64,1024]{2,1,0:T(8,128)(2,1)S(1)}, bf16[2,64,1024]{2,1,0:T(8,128)(2,1)S(1)}, u32[]{:S(2)}, u32[]{:S(2)}) %collective-permute-start.7) | collective-permute-done | bytes 262176 | tf_op jit(solution)/shard_map/ppermute | solution.py:179
  93.5 0.1 fusion
  93.6 2.0 %collective-permute-start.8 = (bf16[2,64,1024]{2,1,0:T(8,128)(2,1)S(1)}, bf16[2,64,1024]{2,1,0:T(8,128)(2,1)S(1)}, u32[]{:S(2)}, u32[]{:S(2)}) collective-permute-start(bf16[2,64,1024]{2,1,0:T(8,128)(2,1)S(1)} %fusion), channel_id=1, source_target_pairs={{0,2},{2,4},{4,6},{6,8},{8,10},{10,12},{12,14},{14,0},{1,15},{3,1}... | collective-permute-start | bytes 786440 | tf_op jit(solution)/shard_map/ppermute | solution.py:182
  95.6 5.4 %collective-permute-done.8 = bf16[2,64,1024]{2,1,0:T(8,128)(2,1)S(1)} collective-permute-done((bf16[2,64,1024]{2,1,0:T(8,128)(2,1)S(1)}, bf16[2,64,1024]{2,1,0:T(8,128)(2,1)S(1)}, u32[]{:S(2)}, u32[]{:S(2)}) %collective-permute-start.8) | collective-permute-done | bytes 262176 | tf_op jit(solution)/shard_map/ppermute | solution.py:182
  101.0 0.0 collective-permute-done.6
  101.0 0.1 fusion.8
  101.1 0.1 fusion.11
  101.2 3.0 %collective-permute-start.9 = (bf16[2,64,1024]{2,1,0:T(8,128)(2,1)S(1)}, bf16[2,64,1024]{2,1,0:T(8,128)(2,1)S(1)}, u32[]{:S(2)}, u32[]{:S(2)}) collective-permute-start(bf16[2,64,1024]{2,1,0:T(8,128)(2,1)S(1)} %pad_maximum_fusion.1), channel_id=1, source_target_pairs={{0,2},{2,4},{4,6},{6,8},{8,10},{10,12},{12,14},{14,0},{1,15},{3,1}... | collective-permute-start | bytes 786440 | tf_op jit(solution)/shard_map/ppermute | solution.py:194
  104.2 0.1 fusion.7
  104.3 1.9 %collective-permute-start.11 = (bf16[2,64,1024]{2,1,0:T(8,128)(2,1)S(1)}, bf16[2,64,1024]{2,1,0:T(8,128)(2,1)S(1)}, u32[]{:S(2)}, u32[]{:S(2)}) collective-permute-start(bf16[2,64,1024]{2,1,0:T(8,128)(2,1)S(1)} %pad_maximum_fusion.2), channel_id=1, source_target_pairs={{0,2},{2,4},{4,6},{6,8},{8,10},{10,12},{12,14},{14,0},{1,15},{3,1}... | collective-permute-start | bytes 786440 | tf_op jit(solution)/shard_map/ppermute | solution.py:194
  106.2 2.1 %collective-permute-done.9 = bf16[2,64,1024]{2,1,0:T(8,128)(2,1)S(1)} collective-permute-done((bf16[2,64,1024]{2,1,0:T(8,128)(2,1)S(1)}, bf16[2,64,1024]{2,1,0:T(8,128)(2,1)S(1)}, u32[]{:S(2)}, u32[]{:S(2)}) %collective-permute-start.9) | collective-permute-done | bytes 262176 | tf_op jit(solution)/shard_map/ppermute | solution.py:194
  108.3 0.1 fusion.3
  108.4 4.2 %collective-permute-start.10 = (bf16[2,64,1024]{2,1,0:T(8,128)(2,1)S(1)}, bf16[2,64,1024]{2,1,0:T(8,128)(2,1)S(1)}, u32[]{:S(2)}, u32[]{:S(2)}) collective-permute-start(bf16[2,64,1024]{2,1,0:T(8,128)(2,1)S(1)} %fusion.3), channel_id=1, source_target_pairs={{0,2},{2,4},{4,6},{6,8},{8,10},{10,12},{12,14},{14,0},{1,15},{3,1}... | collective-permute-start | bytes 786440 | tf_op jit(solution)/shard_map/ppermute | solution.py:194
  112.6 0.0 collective-permute-done.11
  112.6 0.1 fusion.2
  112.8 2.7 %collective-permute-start.14 = (bf16[2,64,1024]{2,1,0:T(8,128)(2,1)S(1)}, bf16[2,64,1024]{2,1,0:T(8,128)(2,1)S(1)}, u32[]{:S(2)}, u32[]{:S(2)}) collective-permute-start(bf16[2,64,1024]{2,1,0:T(8,128)(2,1)S(1)} %fusion.2), channel_id=1, source_target_pairs={{0,2},{2,4},{4,6},{6,8},{8,10},{10,12},{12,14},{14,0},{1,15},{3,1}... | collective-permute-start | bytes 786440 | tf_op jit(solution)/shard_map/ppermute | solution.py:194
  115.4 0.5 collective-permute-done.10
  115.9 0.1 fusion.4
  116.0 4.1 %collective-permute-done.14 = bf16[2,64,1024]{2,1,0:T(8,128)(2,1)S(1)} collective-permute-done((bf16[2,64,1024]{2,1,0:T(8,128)(2,1)S(1)}, bf16[2,64,1024]{2,1,0:T(8,128)(2,1)S(1)}, u32[]{:S(2)}, u32[]{:S(2)}) %collective-permute-start.14) | collective-permute-done | bytes 262176 | tf_op jit(solution)/shard_map/ppermute | solution.py:194
  120.2 0.1 fusion.1
  120.3 3.6 %collective-permute-start.15 = (bf16[2,64,1024]{2,1,0:T(8,128)(2,1)S(1)}, bf16[2,64,1024]{2,1,0:T(8,128)(2,1)S(1)}, u32[]{:S(2)}, u32[]{:S(2)}) collective-permute-start(bf16[2,64,1024]{2,1,0:T(8,128)(2,1)S(1)} %fusion.1), channel_id=1, source_target_pairs={{0,2},{2,4},{4,6},{6,8},{8,10},{10,12},{12,14},{14,0},{1,15},{3,1}... | collective-permute-start | bytes 786440 | tf_op jit(solution)/shard_map/ppermute | solution.py:194
  123.9 1.9 %collective-permute-start.12 = (bf16[2,64,1024]{2,1,0:T(8,128)(2,1)S(1)}, bf16[2,64,1024]{2,1,0:T(8,128)(2,1)S(1)}, u32[]{:S(2)}, u32[]{:S(2)}) collective-permute-start(bf16[2,64,1024]{2,1,0:T(8,128)(2,1)S(1)} %fusion.4), channel_id=1, source_target_pairs={{0,2},{2,4},{4,6},{6,8},{8,10},{10,12},{12,14},{14,0},{1,15},{3,1}... | collective-permute-start | bytes 786440 | tf_op jit(solution)/shard_map/ppermute | solution.py:194
  125.8 1.6 %collective-permute-done.15 = bf16[2,64,1024]{2,1,0:T(8,128)(2,1)S(1)} collective-permute-done((bf16[2,64,1024]{2,1,0:T(8,128)(2,1)S(1)}, bf16[2,64,1024]{2,1,0:T(8,128)(2,1)S(1)}, u32[]{:S(2)}, u32[]{:S(2)}) %collective-permute-start.15) | collective-permute-done | bytes 262176 | tf_op jit(solution)/shard_map/ppermute | solution.py:194
  127.4 9.6 %collective-permute-start.16 = (bf16[1,64,1024]{2,1,0:T(8,128)(2,1)S(1)}, bf16[1,64,1024]{2,1,0:T(8,128)(2,1)S(1)}, u32[]{:S(2)}, u32[]{:S(2)}) collective-permute-start(bf16[1,64,1024]{2,1,0:T(8,128)(2,1)S(1)} %slice.146), channel_id=1, source_target_pairs={{0,1},{1,0},{2,3},{3,2},{4,5},{5,4},{6,7},{7,6},{8,9},{9,8},{10,11... | collective-permute-start | bytes 393224 | tf_op jit(solution)/shard_map/ppermute | solution.py:197
  137.1 0.0 collective-permute-done.12
  137.1 2.8 %collective-permute-start.13 = (bf16[1,64,1024]{2,1,0:T(8,128)(2,1)S(1)}, bf16[1,64,1024]{2,1,0:T(8,128)(2,1)S(1)}, u32[]{:S(2)}, u32[]{:S(2)}) collective-permute-start(bf16[1,64,1024]{2,1,0:T(8,128)(2,1)S(1)} %slice.142), channel_id=1, source_target_pairs={{0,1},{1,0},{2,3},{3,2},{4,5},{5,4},{6,7},{7,6},{8,9},{9,8},{10,11... | collective-permute-start | bytes 393224 | tf_op jit(solution)/shard_map/ppermute | solution.py:197
  139.9 0.0 collective-permute-done.16
  139.9 1.0 collective-permute-done.13
  140.8 0.2 fusion.13
  141.0 0.7 maximum_bitcast_fusion
  (11 shorter events, 0.2 us)
Async XLA Ops:
  0.6 31.2 %collective-permute-start = (bf16[64,2048]{1,0:T(8,128)(2,1)}, bf16[64,2048]{1,0:T(8,128)(2,1)S(1)}, u32[]{:S(2)}, u32[]{:S(2)}) collective-permute-start(bf16[64,2048]{1,0:T(8,128)(2,1)} %param.8), channel_id=1, source_target_pairs={{0,8},{2,10},{4,12},{6,14},{8,0},{10,2},{12,4},{14,6},{1,9},{3,11}... | collective-permute-start | bytes 786440 | tf_op jit(solution)/shard_map/ppermute | solution.py:140
  8.9 22.9 %copy-start = (bf16[64,2048]{1,0:T(8,128)(2,1)S(1)}, bf16[64,2048]{1,0:T(8,128)(2,1)}, u32[]{:S(2)}) copy-start(bf16[64,2048]{1,0:T(8,128)(2,1)} %param.8) | copy-start | bytes 786436
  13.8 61.8 %all-to-all-start = ((bf16[48,24,512]{2,1,0:T(8,128)(2,1)}), bf16[48,24,512]{2,1,0:T(8,128)(2,1)S(1)}, u32[]{:S(2)}, u32[]{:S(2)}) async-start(bf16[48,24,512]{2,1,0:T(8,128)(2,1)} %bitcast.4), calls=%async_computation | async-start | bytes 2359296 | tf_op jit(solution)/shard_map/all_to_all | solution.py:155
  31.8 0.9 copy-start.1
  32.7 15.7 %collective-permute-start.1 = (bf16[2,64,2048]{2,1,0:T(8,128)(2,1)}, bf16[2,64,2048]{2,1,0:T(8,128)(2,1)}, u32[]{:S(2)}, u32[]{:S(2)}) collective-permute-start(bf16[2,64,2048]{2,1,0:T(8,128)(2,1)} %pad_maximum_fusion), channel_id=1, source_target_pairs={{0,2},{2,4},{4,6},{6,8},{8,10},{10,12},{12,14},{14,0},{1,3},{3,5},... | collective-permute-start | bytes 1572872 | tf_op jit(solution)/shard_map/ppermute | solution.py:136
  35.3 17.1 %collective-permute-start.2 = (bf16[2,64,2048]{2,1,0:T(8,128)(2,1)}, bf16[2,64,2048]{2,1,0:T(8,128)(2,1)S(1)}, u32[]{:S(2)}, u32[]{:S(2)}) collective-permute-start(bf16[2,64,2048]{2,1,0:T(8,128)(2,1)} %pad_maximum_fusion), channel_id=1, source_target_pairs={{0,14},{2,0},{4,2},{6,4},{8,6},{10,8},{12,10},{14,12},{1,15},{3,1}... | collective-permute-start | bytes 1572872 | tf_op jit(solution)/shard_map/ppermute | solution.py:137
  50.4 8.9 %collective-permute-start.3 = (bf16[64,2048]{1,0:T(8,128)(2,1)S(1)}, bf16[64,2048]{1,0:T(8,128)(2,1)S(1)}, u32[]{:S(2)}, u32[]{:S(2)}) collective-permute-start(bf16[64,2048]{1,0:T(8,128)(2,1)S(1)} %get-tuple-element.26), channel_id=1, source_target_pairs={{0,2},{2,4},{4,6},{6,8},{8,10},{10,12},{12,14},{14,0},{1,3},{3,5},... | collective-permute-start | bytes 786440 | tf_op jit(solution)/shard_map/ppermute | solution.py:136
  52.4 7.9 %collective-permute-start.4 = (bf16[64,2048]{1,0:T(8,128)(2,1)S(1)}, bf16[64,2048]{1,0:T(8,128)(2,1)S(1)}, u32[]{:S(2)}, u32[]{:S(2)}) collective-permute-start(bf16[64,2048]{1,0:T(8,128)(2,1)S(1)} %get-tuple-element.24), channel_id=1, source_target_pairs={{0,14},{2,0},{4,2},{6,4},{8,6},{10,8},{12,10},{14,12},{1,15},{3,1}... | collective-permute-start | bytes 786440 | tf_op jit(solution)/shard_map/ppermute | solution.py:137
  60.3 9.0 %collective-permute-start.5 = (bf16[512,2048]{1,0:T(8,128)(2,1)S(1)}, bf16[512,2048]{1,0:T(8,128)(2,1)}, u32[]{:S(2)}, u32[]{:S(2)}) collective-permute-start(bf16[512,2048]{1,0:T(8,128)(2,1)S(1)} %bitcast.76), channel_id=1, source_target_pairs={{0,1},{1,0},{2,3},{3,2},{4,5},{5,4},{6,7},{7,6},{8,9},{9,8},{10,11... | collective-permute-start | bytes 6291464 | tf_op jit(solution)/shard_map/ppermute | solution.py:166
  85.5 15.5 %collective-permute-start.6 = (bf16[2,7,64,1024]{3,2,1,0:T(8,128)(2,1)S(1)}, bf16[2,7,64,1024]{3,2,1,0:T(8,128)(2,1)S(1)}, u32[]{:S(2)}, u32[]{:S(2)}) collective-permute-start(bf16[2,7,64,1024]{3,2,1,0:T(8,128)(2,1)S(1)} %get-tuple-element.13), channel_id=1, source_target_pairs={{0,1},{1,0},{2,3},{3,2},{4,5},{5,4},{6,7},{7,6},{8,9},{9,8},{10,11... | collective-permute-start | bytes 5505032 | tf_op jit(solution)/shard_map/ppermute | solution.py:180
  89.8 3.8 %collective-permute-start.7 = (bf16[2,64,1024]{2,1,0:T(8,128)(2,1)S(1)}, bf16[2,64,1024]{2,1,0:T(8,128)(2,1)S(1)}, u32[]{:S(2)}, u32[]{:S(2)}) collective-permute-start(bf16[2,64,1024]{2,1,0:T(8,128)(2,1)S(1)} %get-tuple-element.14), channel_id=1, source_target_pairs={{0,1},{1,0},{2,3},{3,2},{4,5},{5,4},{6,7},{7,6},{8,9},{9,8},{10,11... | collective-permute-start | bytes 786440 | tf_op jit(solution)/shard_map/ppermute | solution.py:179
  93.6 7.4 %collective-permute-start.8 = (bf16[2,64,1024]{2,1,0:T(8,128)(2,1)S(1)}, bf16[2,64,1024]{2,1,0:T(8,128)(2,1)S(1)}, u32[]{:S(2)}, u32[]{:S(2)}) collective-permute-start(bf16[2,64,1024]{2,1,0:T(8,128)(2,1)S(1)} %fusion), channel_id=1, source_target_pairs={{0,2},{2,4},{4,6},{6,8},{8,10},{10,12},{12,14},{14,0},{1,15},{3,1}... | collective-permute-start | bytes 786440 | tf_op jit(solution)/shard_map/ppermute | solution.py:182
  101.2 7.1 %collective-permute-start.9 = (bf16[2,64,1024]{2,1,0:T(8,128)(2,1)S(1)}, bf16[2,64,1024]{2,1,0:T(8,128)(2,1)S(1)}, u32[]{:S(2)}, u32[]{:S(2)}) collective-permute-start(bf16[2,64,1024]{2,1,0:T(8,128)(2,1)S(1)} %pad_maximum_fusion.1), channel_id=1, source_target_pairs={{0,2},{2,4},{4,6},{6,8},{8,10},{10,12},{12,14},{14,0},{1,15},{3,1}... | collective-permute-start | bytes 786440 | tf_op jit(solution)/shard_map/ppermute | solution.py:194
  104.3 8.4 %collective-permute-start.11 = (bf16[2,64,1024]{2,1,0:T(8,128)(2,1)S(1)}, bf16[2,64,1024]{2,1,0:T(8,128)(2,1)S(1)}, u32[]{:S(2)}, u32[]{:S(2)}) collective-permute-start(bf16[2,64,1024]{2,1,0:T(8,128)(2,1)S(1)} %pad_maximum_fusion.2), channel_id=1, source_target_pairs={{0,2},{2,4},{4,6},{6,8},{8,10},{10,12},{12,14},{14,0},{1,15},{3,1}... | collective-permute-start | bytes 786440 | tf_op jit(solution)/shard_map/ppermute | solution.py:194
  108.4 7.5 %collective-permute-start.10 = (bf16[2,64,1024]{2,1,0:T(8,128)(2,1)S(1)}, bf16[2,64,1024]{2,1,0:T(8,128)(2,1)S(1)}, u32[]{:S(2)}, u32[]{:S(2)}) collective-permute-start(bf16[2,64,1024]{2,1,0:T(8,128)(2,1)S(1)} %fusion.3), channel_id=1, source_target_pairs={{0,2},{2,4},{4,6},{6,8},{8,10},{10,12},{12,14},{14,0},{1,15},{3,1}... | collective-permute-start | bytes 786440 | tf_op jit(solution)/shard_map/ppermute | solution.py:194
  112.8 7.4 %collective-permute-start.14 = (bf16[2,64,1024]{2,1,0:T(8,128)(2,1)S(1)}, bf16[2,64,1024]{2,1,0:T(8,128)(2,1)S(1)}, u32[]{:S(2)}, u32[]{:S(2)}) collective-permute-start(bf16[2,64,1024]{2,1,0:T(8,128)(2,1)S(1)} %fusion.2), channel_id=1, source_target_pairs={{0,2},{2,4},{4,6},{6,8},{8,10},{10,12},{12,14},{14,0},{1,15},{3,1}... | collective-permute-start | bytes 786440 | tf_op jit(solution)/shard_map/ppermute | solution.py:194
  120.3 7.1 %collective-permute-start.15 = (bf16[2,64,1024]{2,1,0:T(8,128)(2,1)S(1)}, bf16[2,64,1024]{2,1,0:T(8,128)(2,1)S(1)}, u32[]{:S(2)}, u32[]{:S(2)}) collective-permute-start(bf16[2,64,1024]{2,1,0:T(8,128)(2,1)S(1)} %fusion.1), channel_id=1, source_target_pairs={{0,2},{2,4},{4,6},{6,8},{8,10},{10,12},{12,14},{14,0},{1,15},{3,1}... | collective-permute-start | bytes 786440 | tf_op jit(solution)/shard_map/ppermute | solution.py:194
  123.9 13.2 %collective-permute-start.12 = (bf16[2,64,1024]{2,1,0:T(8,128)(2,1)S(1)}, bf16[2,64,1024]{2,1,0:T(8,128)(2,1)S(1)}, u32[]{:S(2)}, u32[]{:S(2)}) collective-permute-start(bf16[2,64,1024]{2,1,0:T(8,128)(2,1)S(1)} %fusion.4), channel_id=1, source_target_pairs={{0,2},{2,4},{4,6},{6,8},{8,10},{10,12},{12,14},{14,0},{1,15},{3,1}... | collective-permute-start | bytes 786440 | tf_op jit(solution)/shard_map/ppermute | solution.py:194
  127.4 12.4 %collective-permute-start.16 = (bf16[1,64,1024]{2,1,0:T(8,128)(2,1)S(1)}, bf16[1,64,1024]{2,1,0:T(8,128)(2,1)S(1)}, u32[]{:S(2)}, u32[]{:S(2)}) collective-permute-start(bf16[1,64,1024]{2,1,0:T(8,128)(2,1)S(1)} %slice.146), channel_id=1, source_target_pairs={{0,1},{1,0},{2,3},{3,2},{4,5},{5,4},{6,7},{7,6},{8,9},{9,8},{10,11... | collective-permute-start | bytes 393224 | tf_op jit(solution)/shard_map/ppermute | solution.py:197
  137.1 3.7 %collective-permute-start.13 = (bf16[1,64,1024]{2,1,0:T(8,128)(2,1)S(1)}, bf16[1,64,1024]{2,1,0:T(8,128)(2,1)S(1)}, u32[]{:S(2)}, u32[]{:S(2)}) collective-permute-start(bf16[1,64,1024]{2,1,0:T(8,128)(2,1)S(1)} %slice.142), channel_id=1, source_target_pairs={{0,1},{1,0},{2,3},{3,2},{4,5},{5,4},{6,7},{7,6},{8,9},{9,8},{10,11... | collective-permute-start | bytes 393224 | tf_op jit(solution)/shard_map/ppermute | solution.py:197

commit v6 on v4

--- a/solution.py
+++ b/solution.py
@@ -7,7 +7,7 @@
 
 
 BF, F32 = jnp.bfloat16, jnp.float32
-COLS = 256
+COLS = 1024
 STEPS = 1024 // COLS
 
 
@@ -178,19 +178,16 @@
     rest = lax.ppermute(rest, "c", swap)
     piece = lambda d: (keep[d], rest[d - (d > 4)])
     mid = total(keep[4], far)
-    up, down = pass_on(mid[0], mid[1])
-    k, g = piece(3)
-    up = jnp.stack([total(k[0], g[0], up), total(k[1], g[1])])
-    k, g = piece(5)
-    down = after(down, up)
-    down = jnp.stack([total(k[0], g[0]), total(k[1], g[1], down)])
+    across = lax.ppermute(mid, "y", ring(4))
+    rest = after(rest, mid)
+    up, down = total(*piece(3)), total(*piece(5))
     for d in (2, 1, 0):
         sent = down
         up, down = pass_on(up, down)
         if d:
             up = total(*piece(d), after(up, sent))
             down = total(*piece(8 - d), after(down, up))
-    grad = total(*piece(0), up, down)
+    grad = total(*piece(0), across, up, down)
     grad = jnp.concatenate([grad[0], grad[1]], axis=1)
     return gated[None, None], grad[None]
 

time: 140 us -> 140 us (level)
  the two profiles are of different devices: /device:TPU:4 before, /device:TPU:60 now
where the time goes in v6:
time: 140 us; the launch traced here: 139 us
  starting transfers between devices  71.7 us (51%)
  waiting for transfers between devices  45.9 us (33%)
  Pallas kernels  14.2 us (10%)
  local copies, waits for them, and re-layouts  3.41 us (2%)
  other arithmetic  2.65 us (2%)
    ppermute x5, starting transfers between devices, pass_on(): up = lax.ppermute(up, 'y', ring(1))  29.7 us
    ppermute x5, waiting for transfers between devices, pass_on(): down = lax.ppermute(down, 'y', ring(-1))  21.5 us
    all_to_all x1, starting transfers between devices, body(): lax.all_to_all(out.reshape(48, 24, 512), ('z', 'x'), 0, 0, tiled=True)  18.5 us
    ppermute x5, waiting for transfers between devices, pass_on(): up = lax.ppermute(up, 'y', ring(1))  13.2 us
    ppermute x5, starting transfers between devices, pass_on(): down = lax.ppermute(down, 'y', ring(-1))  9.6 us
    pallas_call x1, Pallas kernels, main_call(): pl.pallas_call(main_kernel, grid_spec=gs, out_shape=[jax.ShapeDtypeStruct...  9.33 us
    all_to_all x1, waiting for transfers between devices, body(): lax.all_to_all(out.reshape(48, 24, 512), ('z', 'x'), 0, 0, tiled=True)  5.28 us
    pallas_call x1, Pallas kernels, body(): pl.pallas_call(pick_kernel, in_specs=[anywhere] * 3, out_shape=jax.ShapeD...  4.83 us
  transfers between devices with their start and end apart: 16, of which 9 were waited for; matrix products, arithmetic and copies ran while one was open for 4% of the time, Pallas kernels for 3%

profile of v6, /device:TPU:60, one launch (start us, length us, event | category | flops | bytes accessed | tf_op | source)
XLA Modules:
  0.0 138.9 jit_solution(3742774978741333344)
XLA Ops:
  0.6 4.7 %collective-permute-start = (bf16[64,2048]{1,0:T(8,128)(2,1)}, bf16[64,2048]{1,0:T(8,128)(2,1)S(1)}, u32[]{:S(2)}, u32[]{:S(2)}) collective-permute-start(bf16[64,2048]{1,0:T(8,128)(2,1)} %param.8), channel_id=1, source_target_pairs={{0,8},{2,10},{4,12},{6,14},{8,0},{10,2},{12,4},{14,6},{1,9},{3,11}... | collective-permute-start | bytes 786440 | tf_op jit(solution)/shard_map/ppermute | solution.py:144
  5.4 0.0 copy-start
  5.4 4.8 %pick.1 = bf16[1152,512]{1,0:T(8,128)(2,1)} custom-call(s32[1,576]{1,0:T(1,128)} %bitcast.66, s32[1,576]{1,0:T(1,128)} %bitcast.67, bf16[576,1024]{1,0:T(8,128)(2,1)} %bitcast.62), custom_call_target="tpu_custom_call" | custom-call | tf_op jit(solution)/shard_map/pick/pallas_call | solution.py:146
  10.2 18.5 %all-to-all-start = ((bf16[48,24,512]{2,1,0:T(8,128)(2,1)}), bf16[48,24,512]{2,1,0:T(8,128)(2,1)S(1)}, u32[]{:S(2)}, u32[]{:S(2)}) async-start(bf16[48,24,512]{2,1,0:T(8,128)(2,1)} %bitcast.4), calls=%async_computation | async-start | bytes 2359296 | tf_op jit(solution)/shard_map/all_to_all | solution.py:159
  28.7 0.0 collective-permute-done
  28.7 0.0 copy-start.1
  28.7 0.0 copy-done
  28.7 0.9 pad_maximum_fusion
  29.6 0.0 copy-done.1
  29.6 4.7 %collective-permute-start.1 = (bf16[2,64,2048]{2,1,0:T(8,128)(2,1)}, bf16[2,64,2048]{2,1,0:T(8,128)(2,1)}, u32[]{:S(2)}, u32[]{:S(2)}) collective-permute-start(bf16[2,64,2048]{2,1,0:T(8,128)(2,1)} %pad_maximum_fusion), channel_id=1, source_target_pairs={{0,2},{2,4},{4,6},{6,8},{8,10},{10,12},{12,14},{14,0},{1,3},{3,5},... | collective-permute-start | bytes 1572872 | tf_op jit(solution)/shard_map/ppermute | solution.py:140
  34.3 0.2 broadcast_in_dim.25
  34.6 1.9 %collective-permute-start.2 = (bf16[2,64,2048]{2,1,0:T(8,128)(2,1)}, bf16[2,64,2048]{2,1,0:T(8,128)(2,1)S(1)}, u32[]{:S(2)}, u32[]{:S(2)}) collective-permute-start(bf16[2,64,2048]{2,1,0:T(8,128)(2,1)} %pad_maximum_fusion), channel_id=1, source_target_pairs={{0,14},{2,0},{4,2},{6,4},{8,6},{10,8},{12,10},{14,12},{1,15},{3,1}... | collective-permute-start | bytes 1572872 | tf_op jit(solution)/shard_map/ppermute | solution.py:141
  36.5 1.0 constant_dynamic-update-slice_fusion
  37.5 7.4 %collective-permute-done.1 = bf16[2,64,2048]{2,1,0:T(8,128)(2,1)} collective-permute-done((bf16[2,64,2048]{2,1,0:T(8,128)(2,1)}, bf16[2,64,2048]{2,1,0:T(8,128)(2,1)}, u32[]{:S(2)}, u32[]{:S(2)}) %collective-permute-start.1) | collective-permute-done | bytes 524320 | tf_op jit(solution)/shard_map/ppermute | solution.py:140
  44.9 1.0 slice_dynamic-update-slice_fusion.3
  45.9 1.1 slice_bitcast_fusion.1
  47.0 5.6 %collective-permute-start.3 = (bf16[64,2048]{1,0:T(8,128)(2,1)S(1)}, bf16[64,2048]{1,0:T(8,128)(2,1)S(1)}, u32[]{:S(2)}, u32[]{:S(2)}) collective-permute-start(bf16[64,2048]{1,0:T(8,128)(2,1)S(1)} %get-tuple-element.24), channel_id=1, source_target_pairs={{0,2},{2,4},{4,6},{6,8},{8,10},{10,12},{12,14},{14,0},{1,3},{3,5},... | collective-permute-start | bytes 786440 | tf_op jit(solution)/shard_map/ppermute | solution.py:140
  52.6 0.0 collective-permute-done.2
  52.7 1.9 %collective-permute-start.4 = (bf16[64,2048]{1,0:T(8,128)(2,1)S(1)}, bf16[64,2048]{1,0:T(8,128)(2,1)S(1)}, u32[]{:S(2)}, u32[]{:S(2)}) collective-permute-start(bf16[64,2048]{1,0:T(8,128)(2,1)S(1)} %get-tuple-element.22), channel_id=1, source_target_pairs={{0,14},{2,0},{4,2},{6,4},{8,6},{10,8},{12,10},{14,12},{1,15},{3,1}... | collective-permute-start | bytes 786440 | tf_op jit(solution)/shard_map/ppermute | solution.py:141
  54.6 1.9 %collective-permute-done.3 = bf16[64,2048]{1,0:T(8,128)(2,1)S(1)} collective-permute-done((bf16[64,2048]{1,0:T(8,128)(2,1)S(1)}, bf16[64,2048]{1,0:T(8,128)(2,1)S(1)}, u32[]{:S(2)}, u32[]{:S(2)}) %collective-permute-start.3) | collective-permute-done | bytes 262176 | tf_op jit(solution)/shard_map/ppermute | solution.py:140
  56.5 5.7 %collective-permute-done.4 = bf16[64,2048]{1,0:T(8,128)(2,1)S(1)} collective-permute-done((bf16[64,2048]{1,0:T(8,128)(2,1)S(1)}, bf16[64,2048]{1,0:T(8,128)(2,1)S(1)}, u32[]{:S(2)}, u32[]{:S(2)}) %collective-permute-start.4) | collective-permute-done | bytes 262176 | tf_op jit(solution)/shard_map/ppermute | solution.py:141
  62.2 1.9 %collective-permute-start.5 = (bf16[512,2048]{1,0:T(8,128)(2,1)S(1)}, bf16[512,2048]{1,0:T(8,128)(2,1)}, u32[]{:S(2)}, u32[]{:S(2)}) collective-permute-start(bf16[512,2048]{1,0:T(8,128)(2,1)S(1)} %bitcast.58), channel_id=1, source_target_pairs={{0,1},{1,0},{2,3},{3,2},{4,5},{5,4},{6,7},{7,6},{8,9},{9,8},{10,11... | collective-permute-start | bytes 6291464 | tf_op jit(solution)/shard_map/ppermute | solution.py:170
  64.1 0.1 pad_add_fusion.pos_ref
  64.2 4.2 %collective-permute-done.5.mate_a.mate_b = bf16[512,2048]{1,0:T(8,128)(2,1)} collective-permute-done((bf16[512,2048]{1,0:T(8,128)(2,1)S(1)}, bf16[512,2048]{1,0:T(8,128)(2,1)}, u32[]{:S(2)}, u32[]{:S(2)}) %collective-permute-start.5) | collective-permute-done | bytes 2097184 | tf_op jit(solution)/shard_map/ppermute | solution.py:170
  68.3 5.3 %all-to-all-done = bf16[48,24,512]{2,1,0:T(8,128)(2,1)S(1)} async-done(((bf16[48,24,512]{2,1,0:T(8,128)(2,1)}), bf16[48,24,512]{2,1,0:T(8,128)(2,1)S(1)}, u32[]{:S(2)}, u32[]{:S(2)}) %all-to-all-start) | async-done | bytes 1179680 | tf_op jit(solution)/shard_map/all_to_all | solution.py:159
  73.6 9.3 %main.1 = (bf16[576,1024]{1,0:T(8,128)(2,1)}, bf16[8,2,64,1024]{3,2,1,0:T(8,128)(2,1)S(1)}, bf16[2,64,1024]{2,1,0:T(8,128)(2,1)S(1)}, bf16[7,2,64,1024]{3,2,1,0:T(8,128)(2,1)S(1)}) custom-call(s32[17]{0:T(128)S(1)} %pad_add_fusion.pos_ref, bf16[1152,512]{1,0:T(8,128)(2,1)S(1)} %bitcast.61, bf16[512,2048]{1,0:T(8,128)(2,1)S(1)} %bitcast.59, ...), custom_call_target="tpu_custom_call" | custom-call | tf_op jit(solution)/shard_map/main/pallas_call | solution.py:105
  83.0 1.9 %collective-permute-start.6 = (bf16[7,2,64,1024]{3,2,1,0:T(8,128)(2,1)S(1)}, bf16[7,2,64,1024]{3,2,1,0:T(8,128)(2,1)S(1)}, u32[]{:S(2)}, u32[]{:S(2)}) collective-permute-start(bf16[7,2,64,1024]{3,2,1,0:T(8,128)(2,1)S(1)} %get-tuple-element.13), channel_id=1, source_target_pairs={{0,1},{1,0},{2,3},{3,2},{4,5},{5,4},{6,7},{7,6},{8,9},{9,8},{10,11... | collective-permute-start | bytes 5505032 | tf_op jit(solution)/shard_map/ppermute | solution.py:178
  84.9 2.4 %collective-permute-start.7 = (bf16[2,64,1024]{2,1,0:T(8,128)(2,1)S(1)}, bf16[2,64,1024]{2,1,0:T(8,128)(2,1)S(1)}, u32[]{:S(2)}, u32[]{:S(2)}) collective-permute-start(bf16[2,64,1024]{2,1,0:T(8,128)(2,1)S(1)} %get-tuple-element.14), channel_id=1, source_target_pairs={{0,1},{1,0},{2,3},{3,2},{4,5},{5,4},{6,7},{7,6},{8,9},{9,8},{10,11... | collective-permute-start | bytes 786440 | tf_op jit(solution)/shard_map/ppermute | solution.py:177
  87.3 1.7 %collective-permute-done.7 = bf16[2,64,1024]{2,1,0:T(8,128)(2,1)S(1)} collective-permute-done((bf16[2,64,1024]{2,1,0:T(8,128)(2,1)S(1)}, bf16[2,64,1024]{2,1,0:T(8,128)(2,1)S(1)}, u32[]{:S(2)}, u32[]{:S(2)}) %collective-permute-start.7) | collective-permute-done | bytes 262176 | tf_op jit(solution)/shard_map/ppermute | solution.py:177
  89.0 0.1 fusion
  89.1 0.0 collective-permute-done.6
  89.1 0.2 fusion.8
  89.3 4.7 %collective-permute-start.9 = (bf16[2,64,1024]{2,1,0:T(8,128)(2,1)S(1)}, bf16[2,64,1024]{2,1,0:T(8,128)(2,1)S(1)}, u32[]{:S(2)}, u32[]{:S(2)}) collective-permute-start(bf16[2,64,1024]{2,1,0:T(8,128)(2,1)S(1)} %get-tuple-element.20), channel_id=1, source_target_pairs={{0,2},{2,4},{4,6},{6,8},{8,10},{10,12},{12,14},{14,0},{1,3},{3,5},... | collective-permute-start | bytes 786440 | tf_op jit(solution)/shard_map/ppermute | solution.py:140
  94.0 1.9 %collective-permute-start.11 = (bf16[2,64,1024]{2,1,0:T(8,128)(2,1)S(1)}, bf16[2,64,1024]{2,1,0:T(8,128)(2,1)S(1)}, u32[]{:S(2)}, u32[]{:S(2)}) collective-permute-start(bf16[2,64,1024]{2,1,0:T(8,128)(2,1)S(1)} %get-tuple-element.21), channel_id=1, source_target_pairs={{0,14},{2,0},{4,2},{6,4},{8,6},{10,8},{12,10},{14,12},{1,15},{3,1}... | collective-permute-start | bytes 786440 | tf_op jit(solution)/shard_map/ppermute | solution.py:141
  95.9 3.9 %collective-permute-done.9 = bf16[2,64,1024]{2,1,0:T(8,128)(2,1)S(1)} collective-permute-done((bf16[2,64,1024]{2,1,0:T(8,128)(2,1)S(1)}, bf16[2,64,1024]{2,1,0:T(8,128)(2,1)S(1)}, u32[]{:S(2)}, u32[]{:S(2)}) %collective-permute-start.9) | collective-permute-done | bytes 262176 | tf_op jit(solution)/shard_map/ppermute | solution.py:140
  99.8 0.1 fusion.3
  100.0 5.6 %collective-permute-start.10 = (bf16[2,64,1024]{2,1,0:T(8,128)(2,1)S(1)}, bf16[2,64,1024]{2,1,0:T(8,128)(2,1)S(1)}, u32[]{:S(2)}, u32[]{:S(2)}) collective-permute-start(bf16[2,64,1024]{2,1,0:T(8,128)(2,1)S(1)} %fusion.3), channel_id=1, source_target_pairs={{0,2},{2,4},{4,6},{6,8},{8,10},{10,12},{12,14},{14,0},{1,3},{3,5},... | collective-permute-start | bytes 786440 | tf_op jit(solution)/shard_map/ppermute | solution.py:140
  105.6 0.0 collective-permute-done.11
  105.6 0.1 fusion.2
  105.7 1.9 %collective-permute-start.13 = (bf16[2,64,1024]{2,1,0:T(8,128)(2,1)S(1)}, bf16[2,64,1024]{2,1,0:T(8,128)(2,1)S(1)}, u32[]{:S(2)}, u32[]{:S(2)}) collective-permute-start(bf16[2,64,1024]{2,1,0:T(8,128)(2,1)S(1)} %fusion.2), channel_id=1, source_target_pairs={{0,14},{2,0},{4,2},{6,4},{8,6},{10,8},{12,10},{14,12},{1,15},{3,1}... | collective-permute-start | bytes 786440 | tf_op jit(solution)/shard_map/ppermute | solution.py:141
  107.7 3.0 %collective-permute-start.8 = (bf16[2,64,1024]{2,1,0:T(8,128)(2,1)S(1)}, bf16[2,64,1024]{2,1,0:T(8,128)(2,1)S(1)}, u32[]{:S(2)}, u32[]{:S(2)}) collective-permute-start(bf16[2,64,1024]{2,1,0:T(8,128)(2,1)S(1)} %fusion), channel_id=1, source_target_pairs={{0,8},{2,10},{4,12},{6,14},{8,0},{10,2},{12,4},{14,6},{1,9},{3,11}... | collective-permute-start | bytes 786440 | tf_op jit(solution)/shard_map/ppermute | solution.py:181
  110.7 0.0 collective-permute-done.10
  110.7 0.1 fusion.4
  110.9 9.1 %collective-permute-start.12 = (bf16[2,64,1024]{2,1,0:T(8,128)(2,1)S(1)}, bf16[2,64,1024]{2,1,0:T(8,128)(2,1)S(1)}, u32[]{:S(2)}, u32[]{:S(2)}) collective-permute-start(bf16[2,64,1024]{2,1,0:T(8,128)(2,1)S(1)} %fusion.4), channel_id=1, source_target_pairs={{0,2},{2,4},{4,6},{6,8},{8,10},{10,12},{12,14},{14,0},{1,3},{3,5},... | collective-permute-start | bytes 786440 | tf_op jit(solution)/shard_map/ppermute | solution.py:140
  120.0 8.3 %collective-permute-done.13 = bf16[2,64,1024]{2,1,0:T(8,128)(2,1)S(1)} collective-permute-done((bf16[2,64,1024]{2,1,0:T(8,128)(2,1)S(1)}, bf16[2,64,1024]{2,1,0:T(8,128)(2,1)S(1)}, u32[]{:S(2)}, u32[]{:S(2)}) %collective-permute-start.13) | collective-permute-done | bytes 262176 | tf_op jit(solution)/shard_map/ppermute | solution.py:141
  128.3 0.1 fusion.1
  128.4 1.9 %collective-permute-start.14 = (bf16[2,64,1024]{2,1,0:T(8,128)(2,1)S(1)}, bf16[2,64,1024]{2,1,0:T(8,128)(2,1)S(1)}, u32[]{:S(2)}, u32[]{:S(2)}) collective-permute-start(bf16[2,64,1024]{2,1,0:T(8,128)(2,1)S(1)} %fusion.1), channel_id=1, source_target_pairs={{0,14},{2,0},{4,2},{6,4},{8,6},{10,8},{12,10},{14,12},{1,15},{3,1}... | collective-permute-start | bytes 786440 | tf_op jit(solution)/shard_map/ppermute | solution.py:141
  130.4 0.0 collective-permute-done.8
  130.4 0.0 collective-permute-done.12
  130.4 7.5 %collective-permute-done.14 = bf16[2,64,1024]{2,1,0:T(8,128)(2,1)S(1)} collective-permute-done((bf16[2,64,1024]{2,1,0:T(8,128)(2,1)S(1)}, bf16[2,64,1024]{2,1,0:T(8,128)(2,1)S(1)}, u32[]{:S(2)}, u32[]{:S(2)}) %collective-permute-start.14) | collective-permute-done | bytes 262176 | tf_op jit(solution)/shard_map/ppermute | solution.py:141
  137.9 0.2 fusion.7
  138.2 0.7 maximum_bitcast_fusion
  (7 shorter events, 0.2 us)
Async XLA Ops:
  0.6 28.0 %collective-permute-start = (bf16[64,2048]{1,0:T(8,128)(2,1)}, bf16[64,2048]{1,0:T(8,128)(2,1)S(1)}, u32[]{:S(2)}, u32[]{:S(2)}) collective-permute-start(bf16[64,2048]{1,0:T(8,128)(2,1)} %param.8), channel_id=1, source_target_pairs={{0,8},{2,10},{4,12},{6,14},{8,0},{10,2},{12,4},{14,6},{1,9},{3,11}... | collective-permute-start | bytes 786440 | tf_op jit(solution)/shard_map/ppermute | solution.py:144
  5.4 23.3 %copy-start = (bf16[64,2048]{1,0:T(8,128)(2,1)S(1)}, bf16[64,2048]{1,0:T(8,128)(2,1)}, u32[]{:S(2)}) copy-start(bf16[64,2048]{1,0:T(8,128)(2,1)} %param.8) | copy-start | bytes 786436
  10.2 63.4 %all-to-all-start = ((bf16[48,24,512]{2,1,0:T(8,128)(2,1)}), bf16[48,24,512]{2,1,0:T(8,128)(2,1)S(1)}, u32[]{:S(2)}, u32[]{:S(2)}) async-start(bf16[48,24,512]{2,1,0:T(8,128)(2,1)} %bitcast.4), calls=%async_computation | async-start | bytes 2359296 | tf_op jit(solution)/shard_map/all_to_all | solution.py:159
  28.7 0.9 copy-start.1
  29.6 15.3 %collective-permute-start.1 = (bf16[2,64,2048]{2,1,0:T(8,128)(2,1)}, bf16[2,64,2048]{2,1,0:T(8,128)(2,1)}, u32[]{:S(2)}, u32[]{:S(2)}) collective-permute-start(bf16[2,64,2048]{2,1,0:T(8,128)(2,1)} %pad_maximum_fusion), channel_id=1, source_target_pairs={{0,2},{2,4},{4,6},{6,8},{8,10},{10,12},{12,14},{14,0},{1,3},{3,5},... | collective-permute-start | bytes 1572872 | tf_op jit(solution)/shard_map/ppermute | solution.py:140
  34.6 18.0 %collective-permute-start.2 = (bf16[2,64,2048]{2,1,0:T(8,128)(2,1)}, bf16[2,64,2048]{2,1,0:T(8,128)(2,1)S(1)}, u32[]{:S(2)}, u32[]{:S(2)}) collective-permute-start(bf16[2,64,2048]{2,1,0:T(8,128)(2,1)} %pad_maximum_fusion), channel_id=1, source_target_pairs={{0,14},{2,0},{4,2},{6,4},{8,6},{10,8},{12,10},{14,12},{1,15},{3,1}... | collective-permute-start | bytes 1572872 | tf_op jit(solution)/shard_map/ppermute | solution.py:141
  47.0 9.5 %collective-permute-start.3 = (bf16[64,2048]{1,0:T(8,128)(2,1)S(1)}, bf16[64,2048]{1,0:T(8,128)(2,1)S(1)}, u32[]{:S(2)}, u32[]{:S(2)}) collective-permute-start(bf16[64,2048]{1,0:T(8,128)(2,1)S(1)} %get-tuple-element.24), channel_id=1, source_target_pairs={{0,2},{2,4},{4,6},{6,8},{8,10},{10,12},{12,14},{14,0},{1,3},{3,5},... | collective-permute-start | bytes 786440 | tf_op jit(solution)/shard_map/ppermute | solution.py:140
  52.7 9.5 %collective-permute-start.4 = (bf16[64,2048]{1,0:T(8,128)(2,1)S(1)}, bf16[64,2048]{1,0:T(8,128)(2,1)S(1)}, u32[]{:S(2)}, u32[]{:S(2)}) collective-permute-start(bf16[64,2048]{1,0:T(8,128)(2,1)S(1)} %get-tuple-element.22), channel_id=1, source_target_pairs={{0,14},{2,0},{4,2},{6,4},{8,6},{10,8},{12,10},{14,12},{1,15},{3,1}... | collective-permute-start | bytes 786440 | tf_op jit(solution)/shard_map/ppermute | solution.py:141
  62.2 6.2 %collective-permute-start.5 = (bf16[512,2048]{1,0:T(8,128)(2,1)S(1)}, bf16[512,2048]{1,0:T(8,128)(2,1)}, u32[]{:S(2)}, u32[]{:S(2)}) collective-permute-start(bf16[512,2048]{1,0:T(8,128)(2,1)S(1)} %bitcast.58), channel_id=1, source_target_pairs={{0,1},{1,0},{2,3},{3,2},{4,5},{5,4},{6,7},{7,6},{8,9},{9,8},{10,11... | collective-permute-start | bytes 6291464 | tf_op jit(solution)/shard_map/ppermute | solution.py:170
  83.0 6.1 %collective-permute-start.6 = (bf16[7,2,64,1024]{3,2,1,0:T(8,128)(2,1)S(1)}, bf16[7,2,64,1024]{3,2,1,0:T(8,128)(2,1)S(1)}, u32[]{:S(2)}, u32[]{:S(2)}) collective-permute-start(bf16[7,2,64,1024]{3,2,1,0:T(8,128)(2,1)S(1)} %get-tuple-element.13), channel_id=1, source_target_pairs={{0,1},{1,0},{2,3},{3,2},{4,5},{5,4},{6,7},{7,6},{8,9},{9,8},{10,11... | collective-permute-start | bytes 5505032 | tf_op jit(solution)/shard_map/ppermute | solution.py:178
  84.9 4.1 %collective-permute-start.7 = (bf16[2,64,1024]{2,1,0:T(8,128)(2,1)S(1)}, bf16[2,64,1024]{2,1,0:T(8,128)(2,1)S(1)}, u32[]{:S(2)}, u32[]{:S(2)}) collective-permute-start(bf16[2,64,1024]{2,1,0:T(8,128)(2,1)S(1)} %get-tuple-element.14), channel_id=1, source_target_pairs={{0,1},{1,0},{2,3},{3,2},{4,5},{5,4},{6,7},{7,6},{8,9},{9,8},{10,11... | collective-permute-start | bytes 786440 | tf_op jit(solution)/shard_map/ppermute | solution.py:177
  89.3 10.6 %collective-permute-start.9 = (bf16[2,64,1024]{2,1,0:T(8,128)(2,1)S(1)}, bf16[2,64,1024]{2,1,0:T(8,128)(2,1)S(1)}, u32[]{:S(2)}, u32[]{:S(2)}) collective-permute-start(bf16[2,64,1024]{2,1,0:T(8,128)(2,1)S(1)} %get-tuple-element.20), channel_id=1, source_target_pairs={{0,2},{2,4},{4,6},{6,8},{8,10},{10,12},{12,14},{14,0},{1,3},{3,5},... | collective-permute-start | bytes 786440 | tf_op jit(solution)/shard_map/ppermute | solution.py:140
  94.0 11.6 %collective-permute-start.11 = (bf16[2,64,1024]{2,1,0:T(8,128)(2,1)S(1)}, bf16[2,64,1024]{2,1,0:T(8,128)(2,1)S(1)}, u32[]{:S(2)}, u32[]{:S(2)}) collective-permute-start(bf16[2,64,1024]{2,1,0:T(8,128)(2,1)S(1)} %get-tuple-element.21), channel_id=1, source_target_pairs={{0,14},{2,0},{4,2},{6,4},{8,6},{10,8},{12,10},{14,12},{1,15},{3,1}... | collective-permute-start | bytes 786440 | tf_op jit(solution)/shard_map/ppermute | solution.py:141
  100.0 10.7 %collective-permute-start.10 = (bf16[2,64,1024]{2,1,0:T(8,128)(2,1)S(1)}, bf16[2,64,1024]{2,1,0:T(8,128)(2,1)S(1)}, u32[]{:S(2)}, u32[]{:S(2)}) collective-permute-start(bf16[2,64,1024]{2,1,0:T(8,128)(2,1)S(1)} %fusion.3), channel_id=1, source_target_pairs={{0,2},{2,4},{4,6},{6,8},{8,10},{10,12},{12,14},{14,0},{1,3},{3,5},... | collective-permute-start | bytes 786440 | tf_op jit(solution)/shard_map/ppermute | solution.py:140
  105.7 22.6 %collective-permute-start.13 = (bf16[2,64,1024]{2,1,0:T(8,128)(2,1)S(1)}, bf16[2,64,1024]{2,1,0:T(8,128)(2,1)S(1)}, u32[]{:S(2)}, u32[]{:S(2)}) collective-permute-start(bf16[2,64,1024]{2,1,0:T(8,128)(2,1)S(1)} %fusion.2), channel_id=1, source_target_pairs={{0,14},{2,0},{4,2},{6,4},{8,6},{10,8},{12,10},{14,12},{1,15},{3,1}... | collective-permute-start | bytes 786440 | tf_op jit(solution)/shard_map/ppermute | solution.py:141
  107.7 22.7 %collective-permute-start.8 = (bf16[2,64,1024]{2,1,0:T(8,128)(2,1)S(1)}, bf16[2,64,1024]{2,1,0:T(8,128)(2,1)S(1)}, u32[]{:S(2)}, u32[]{:S(2)}) collective-permute-start(bf16[2,64,1024]{2,1,0:T(8,128)(2,1)S(1)} %fusion), channel_id=1, source_target_pairs={{0,8},{2,10},{4,12},{6,14},{8,0},{10,2},{12,4},{14,6},{1,9},{3,11}... | collective-permute-start | bytes 786440 | tf_op jit(solution)/shard_map/ppermute | solution.py:181
  110.9 19.5 %collective-permute-start.12 = (bf16[2,64,1024]{2,1,0:T(8,128)(2,1)S(1)}, bf16[2,64,1024]{2,1,0:T(8,128)(2,1)S(1)}, u32[]{:S(2)}, u32[]{:S(2)}) collective-permute-start(bf16[2,64,1024]{2,1,0:T(8,128)(2,1)S(1)} %fusion.4), channel_id=1, source_target_pairs={{0,2},{2,4},{4,6},{6,8},{8,10},{10,12},{12,14},{14,0},{1,3},{3,5},... | collective-permute-start | bytes 786440 | tf_op jit(solution)/shard_map/ppermute | solution.py:140
  128.4 9.5 %collective-permute-start.14 = (bf16[2,64,1024]{2,1,0:T(8,128)(2,1)S(1)}, bf16[2,64,1024]{2,1,0:T(8,128)(2,1)S(1)}, u32[]{:S(2)}, u32[]{:S(2)}) collective-permute-start(bf16[2,64,1024]{2,1,0:T(8,128)(2,1)S(1)} %fusion.1), channel_id=1, source_target_pairs={{0,14},{2,0},{4,2},{6,4},{8,6},{10,8},{12,10},{14,12},{1,15},{3,1}... | collective-permute-start | bytes 786440 | tf_op jit(solution)/shard_map/ppermute | solution.py:141
